TPU v7x, 32 devices: a whole 2x2x4 slice. The times are simulated.
32 devices in a mesh: sample: 8 (over y, x, core), chan: 4 (over z).
Axes of the slice: x: 2, y: 2, z: 4, core: 2. Of those that a mesh axis runs over, the one named last changes fastest.
Arguments:
- snapshots: bfloat16 [8, 256, 512], P('sample', None, 'chan'), may hold values from -6 to 6
- first_weight: bfloat16 [256, 27, 256], P('chan'), may hold values from -0.078125 to 0.078125
- second_weight: bfloat16 [256, 27, 256], P('chan'), may hold values from -0.078125 to 0.078125
- cotangent: bfloat16 [8, 256, 512], P('sample', 'chan'), may hold values from -0.09375 to 0.09375
Outputs:
- second_out: bfloat16 [8, 256, 512], P('sample', 'chan')
- first_grad: float32 [256, 27, 256], P('chan', None, 'sample')
- second_grad: float32 [256, 27, 256], P('chan', None, 'sample')
All inputs are finite; a program needn't handle non-finite values.
Results may differ from a plain program's by a relative error of at most 0.0061.
Values may be sent and summed in bfloat16 or wider, within the bound.
No kernel may reach another device: no remote copies, remote signals or barrier semaphores. Data moves between devices by JAX's collectives and lax.ppermute only.
A program may use at most 128 MiB of HBM per device.

v0:
```python
import jax
import jax.numpy as jnp
from jax import lax
from jax.sharding import PartitionSpec as P

SIDE = 8


def shifted(fields):
    batch_size, channels = (fields.shape[0], fields.shape[1])
    cube_form = fields.reshape(batch_size, channels, SIDE, SIDE, SIDE)
    padded = jnp.pad(cube_form, ((0, 0), (0, 0), (1, 1), (1, 1), (1, 1)))
    shifted_views = []
    for tap_index in range(27):
        shift_depth, shift_rows, shift_cols = (tap_index // 9, tap_index // 3 % 3, tap_index % 3)
        shifted_views.append(
            padded[
                :,
                :,
                shift_depth : shift_depth + SIDE,
                shift_rows : shift_rows + SIDE,
                shift_cols : shift_cols + SIDE,
            ]
        )
    return jnp.stack(shifted_views, axis=2).reshape(batch_size, channels * 27, SIDE * SIDE * SIDE)


def spread(terms):
    batch_size, channels = (terms.shape[0], terms.shape[1] // 27)
    cube_form = terms.reshape(batch_size, channels, 27, SIDE, SIDE, SIDE)
    padded = jnp.pad(cube_form, ((0, 0), (0, 0), (0, 0), (1, 1), (1, 1), (1, 1)))
    total = jnp.zeros((batch_size, channels, SIDE, SIDE, SIDE), jnp.float32)
    for tap_index in range(27):
        shift_depth, shift_rows, shift_cols = (tap_index // 9, tap_index // 3 % 3, tap_index % 3)
        total = (
            total
            + padded[
                :,
                :,
                tap_index,
                2 - shift_depth : 2 - shift_depth + SIDE,
                2 - shift_rows : 2 - shift_rows + SIDE,
                2 - shift_cols : 2 - shift_cols + SIDE,
            ]
        )
    return total.reshape(batch_size, channels, SIDE * SIDE * SIDE)


def layer_sums(kernel_rows, patches):
    partial_value = jnp.einsum(
        "kc,bkp->bcp", kernel_rows, patches, preferred_element_type=jnp.float32
    )
    return lax.psum_scatter(partial_value, "chan", scatter_dimension=1, tiled=True)


def all_channels(grad_maps):
    return lax.all_gather(grad_maps, "chan", axis=1, tiled=True)


def body(snapshots, first_weight, second_weight, cotangent):
    channel_maps = lax.all_to_all(snapshots, "chan", split_axis=1, concat_axis=2, tiled=True)
    input_patches = shifted(channel_maps)
    first_rows = first_weight.reshape(-1, first_weight.shape[2])
    second_rows = second_weight.reshape(-1, second_weight.shape[2])
    first_sum = layer_sums(first_rows, input_patches)
    first_map = first_sum.astype(jnp.bfloat16)
    first_values = first_map.astype(jnp.float32)
    hidden = jax.nn.silu(first_values).astype(jnp.bfloat16)
    hidden_patches = shifted(hidden)
    second_out = layer_sums(second_rows, hidden_patches).astype(jnp.bfloat16)
    full_cotangent = all_channels(cotangent)
    second_term = jnp.einsum(
        "bkp,bcp->kc", hidden_patches, full_cotangent, preferred_element_type=jnp.float32
    )
    terms = jnp.einsum(
        "kc,bcp->bkp", second_rows, full_cotangent, preferred_element_type=jnp.float32
    )
    hidden_grad = spread(terms)
    sigmoid_values = jax.nn.sigmoid(first_values)
    first_map_grad = (
        hidden_grad * sigmoid_values * (1.0 + first_values * (1.0 - sigmoid_values))
    ).astype(jnp.bfloat16)
    full_map_grad = all_channels(first_map_grad)
    first_term = jnp.einsum(
        "bkp,bcp->kc", input_patches, full_map_grad, preferred_element_type=jnp.float32
    )
    first_grad, second_grad = (
        lax.psum_scatter(first_term, "sample", scatter_dimension=1, tiled=True),
        lax.psum_scatter(second_term, "sample", scatter_dimension=1, tiled=True),
    )
    return (
        second_out,
        first_grad.reshape(first_weight.shape[0], 27, -1),
        second_grad.reshape(second_weight.shape[0], 27, -1),
    )


def solution(mesh):
    placed = (
        P("sample", None, "chan"),
        P("chan", None, None),
        P("chan", None, None),
        P("sample", "chan", None),
    )
    return jax.shard_map(
        body,
        mesh=mesh,
        in_specs=placed,
        out_specs=(P("sample", "chan", None), P("chan", None, "sample"), P("chan", None, "sample")),
        check_vma=False,
    )
```

profile of v0, /device:TPU:0, one launch (start us, length us, event | category | flops | bytes accessed | tf_op | source)
XLA Modules:
  0.0 640.3 jit_solution(11114681304338015524)
XLA Ops:
  7.2 1.0 copy.72
  8.7 1.0 reduce.22
  10.3 6.3 all-to-all-start
  16.7 1.7 copy.63
  18.3 1.2 reshape.411
  19.5 14.5 %all_gather.6 = bf16[1,256,512]{2,1,0:T(8,128)(2,1)S(1)} all-gather(bf16[1,64,512]{2,1,0:T(8,128)(2,1)S(1)} %copy-done.4), channel_id=1, replica_groups=mesh['sample'=8,'chan'=4] {'chan'}, dimensions={1}, use_global_device_ids=true | all-gather | bytes 327680 | tf_op jit(solution)/shard_map/all_gather | solution.py:57
  34.0 0.7 copy-done.1
  34.7 1.8 convolution_bitcast_fusion
  36.5 3.1 copy.65
  39.6 22.4 %reshape.413 = f32[1,64,27,8,8,8]{2,1,5,4,3,0:T(8,128)} reshape(f32[1,1728,512]{1,2,0:T(8,128)} %copy.65) | data formatting | bytes 7077888 | tf_op jit(solution)/shard_map/reshape | solution.py:30
  62.0 178.1 %fusion.16 = (f32[64,8,8,8]{0,3,2,1:T(8,128)S(1)}, f32[64,8,8,8]{0,3,2,1:T(8,128)S(1)}, f32[64,8,8,8]{0,3,2,1:T(8,128)S(1)}, f32[64,8,8,8]{0,3,2,1:T(8,128)S(1)}...) fusion(f32[1,64,27,8,8,8]{2,1,5,4,3,0:T(8,128)} %reshape.413), kind=kLoop, calls=%fused_computation.42 | loop fusion | flops 524288 | bytes 34996224 | tf_op jit(solution)/shard_map/slice | solution.py:37
  240.6 1.2 reshape.408
  243.1 0.9 reshape.443
  253.7 0.7 fusion.66
  257.8 0.7 fusion.78
  262.6 9.5 %copy.58 = bf16[1,64,27,8,8,8]{2,1,5,4,3,0:T(8,128)(2,1)} copy(bf16[1,64,27,8,8,8]{1,5,4,3,2,0:T(8,128)(2,1)} %fusion.90) | data formatting | bytes 3538944 | tf_op jit(solution)/shard_map/stack | solution.py:25
  272.1 11.3 %reshape.407 = bf16[1728,512]{0,1:T(8,128)(2,1)S(1)} reshape(bf16[1,64,27,8,8,8]{2,1,5,4,3,0:T(8,128)(2,1)} %copy.58) | data formatting | bytes 3538944 | tf_op jit(solution)/shard_map/reshape.2
  283.4 2.6 convolution_bitcast_fusion.2
  286.0 1.3 copy.60
  287.3 140.8 %all-reduce.7 = bf16[1,256,512]{2,0,1:T(2,128)(2,1)} all-reduce(f32[1,256,512]{2,0,1:T(1,128)S(1)} %copy.60), channel_id=2, replica_groups=mesh['sample'=8,'chan'=4] {'chan'}, use_global_device_ids=true, to_apply=%region_0.1.clone | all-reduce | flops 131072 | bytes 786432
  428.1 1.0 constant_dynamic-slice_fusion
  429.3 1.6 fusion.33
  435.1 14.1 %all_gather.7 = bf16[1,256,512]{2,1,0:T(8,128)(2,1)S(1)} all-gather(bf16[1,64,512]{2,1,0:T(8,128)(2,1)S(1)} %copy.66), channel_id=1, replica_groups=mesh['sample'=8,'chan'=4] {'chan'}, dimensions={1}, use_global_device_ids=true | all-gather | bytes 327680 | tf_op jit(solution)/shard_map/all_gather | solution.py:57
  449.2 2.0 fusion.34
  465.7 9.6 %copy.62 = bf16[1,64,27,8,8,8]{2,1,5,4,3,0:T(8,128)(2,1)} copy(bf16[1,64,27,8,8,8]{1,5,4,3,2,0:T(8,128)(2,1)} %fusion.142) | data formatting | bytes 3538944 | tf_op jit(solution)/shard_map/stack | solution.py:25
  475.2 11.3 %reshape.410 = bf16[1728,512]{0,1:T(8,128)(2,1)S(1)} reshape(bf16[1,64,27,8,8,8]{2,1,5,4,3,0:T(8,128)(2,1)} %copy.62) | data formatting | bytes 3538944 | tf_op jit(solution)/shard_map/reshape.5
  486.6 1.9 fusion.37
  489.6 136.3 %all-reduce.8 = bf16[1,256,512]{2,0,1:T(2,128)(2,1)S(1)} all-reduce(f32[1,256,512]{2,0,1:T(1,128)S(1)} %copy.64), channel_id=3, replica_groups=mesh['sample'=8,'chan'=4] {'chan'}, use_global_device_ids=true, to_apply=%region_1.2.clone | all-reduce | flops 131072 | bytes 786432
  626.7 2.2 reshape.415
  628.9 1.2 copy.68
  630.1 2.2 reshape.416
  632.3 1.2 copy.69
  (82 shorter events, 40.0 us)
Async XLA Ops:
  7.2 12.4 %copy-start.4 = (bf16[1,64,512]{2,1,0:T(8,128)(2,1)S(1)}, bf16[1,64,512]{2,1,0:T(8,128)(2,1)}, u32[]{:S(2)}) copy-start(bf16[1,64,512]{2,1,0:T(8,128)(2,1)} %param.7) | copy-start | bytes 196612
  10.3 232.7 %all-to-all-start = ((bf16[4,2,4096]{2,1,0:T(2,128)(2,1)}), bf16[4,2,4096]{2,1,0:T(2,128)(2,1)}, u32[]{:S(2)}, u32[]{:S(2)}) async-start(bf16[4,2,4096]{2,1,0:T(2,128)(2,1)} %reshape.442), calls=%async_computation | async-start | bytes 131072 | tf_op jit(solution)/shard_map/all_to_all | solution.py:61
  16.6 610.1 %reduce-scatter.3.cloned.1.call-start = ((), (), s32[]{:S(2)}) async-start(), calls=%async_computation.3 | async-start | bytes 2064384 | tf_op jit(solution)/shard_map/reduce_scatter | solution.py:88
  34.0 0.7 copy-start.1
  62.0 178.1 %copy-start.3 = (bf16[64,27,256]{2,0,1:T(8,128)(2,1)S(1)}, bf16[64,27,256]{2,0,1:T(8,128)(2,1)}, u32[]{:S(2)}) copy-start(bf16[64,27,256]{2,0,1:T(8,128)(2,1)} %param.5) | copy-start | bytes 2654212
  240.1 1.7 copy-start.5
  451.2 178.8 %reduce-scatter.5.cloned.1.call-start = ((), (), s32[]{:S(2)}) async-start(), calls=%async_computation.4 | async-start | bytes 2064384 | tf_op jit(solution)/shard_map/reduce_scatter | solution.py:89
  475.2 11.4 %copy-start.2 = (bf16[1,256,512]{2,1,0:T(8,128)(2,1)S(1)}, bf16[1,256,512]{2,1,0:T(8,128)(2,1)}, u32[]{:S(2)}) copy-start(bf16[1,256,512]{2,1,0:T(8,128)(2,1)} %copy-done.1) | copy-start | bytes 786436
  486.6 1.9 copy-start
Sparse Core Ops, SparseCore 0:
  451.4 40.2 reduce-scatter.2
  495.0 39.6 reduce-scatter.4
where the time goes:
time: 642 us; the launch traced here: 640 us
  blocking collectives  306 us (48%)
  other arithmetic  181 us (28%)
  local copies, waits for them, and re-layouts  124 us (19%)
  between operations  14.9 us (2%)
  matrix products  8.92 us (1%)
    unnamed x2, blocking collectives  277 us
    slice x1, other arithmetic, spread(): padded[:, :, tap_index, 2 - shift_depth:2 - shift_depth + SIDE, 2 - shift...  178 us
    unnamed x76, local copies, waits for them, and re-layouts  46.2 us
    all_gather x2, blocking collectives, all_channels(): return lax.all_gather(grad_maps, 'chan', axis=1, tiled=True)  28.6 us
    another operation x2, local copies, waits for them, and re-layouts  22.6 us
    reshape x1, local copies, waits for them, and re-layouts, spread(): cube_form = terms.reshape(batch_size, channels, 27, SIDE, SIDE, SIDE)  22.4 us
    another operation x4, local copies, waits for them, and re-layouts, shifted(): jnp.stack(shifted_views, axis=2)  20.4 us
  transfers between devices with their start and end apart: 3, of which 0 were waited for; matrix products, arithmetic and copies ran while one was open for 39% of the time, Pallas kernels for 0%

commit v1 on v0

v1 whole, which is shorter than its diff:
```python
import functools

import jax
import jax.numpy as jnp
from jax import lax
from jax.experimental import pallas as pl
from jax.experimental.pallas import tpu as pltpu
from jax.sharding import PartitionSpec as P

SIDE = 8
CELLS = SIDE**3
F32 = jnp.float32
BF16 = jnp.bfloat16
VMEM = pl.BlockSpec(memory_space=pltpu.VMEM)
TAPS = [(a, b, e) for a in (-1, 0, 1) for b in (-1, 0, 1) for e in (-1, 0, 1)]


def coords():
    cell = lax.broadcasted_iota(jnp.int32, (1, CELLS), 1)
    return cell >> 6, (cell >> 3) & 7, cell & 7


def moved(v, step):
    delta = 64 * step[0] + 8 * step[1] + step[2]
    if delta == 0:
        return v
    out = pltpu.roll(v, (-delta) % CELLS, 1)
    ok = None
    for at, by in zip(coords(), step):
        if by:
            good = at < SIDE - by if by > 0 else at >= -by
            ok = good if ok is None else ok & good
    return jnp.where(ok, out, 0)


def conv_part(w_ref, v, patches):
    rows = v.shape[0]
    v = v.astype(F32)
    for t, step in enumerate(TAPS):
        patches[t * rows : (t + 1) * rows, :] = moved(v, step).astype(BF16)
    return lax.dot_general(
        w_ref[...].reshape(-1, w_ref.shape[2]),
        patches[...],
        (((0,), (0,)), ((), ())),
        preferred_element_type=F32,
    )


def conv_kernel(w_ref, v_ref, o_ref, patches):
    o_ref[...] = conv_part(w_ref, v_ref[...], patches).astype(BF16)


def conv(w, v):
    taps, rows, outs = w.shape
    return pl.pallas_call(
        conv_kernel,
        out_shape=jax.ShapeDtypeStruct((outs, CELLS), BF16),
        in_specs=[VMEM] * 2,
        out_specs=VMEM,
        scratch_shapes=[pltpu.VMEM((taps * rows, CELLS), BF16)],
        name="conv",
    )(w, v)


def spread_kernel(w_ref, g_ref, o_ref):
    taps, rows, outs = w_ref.shape
    total = jnp.zeros((rows, CELLS), F32)
    for t, step in enumerate(TAPS):
        term = jnp.dot(w_ref[t], g_ref[...], preferred_element_type=F32)
        total = total + moved(term, tuple(-s for s in step))
    o_ref[...] = total


def spread(w, g):
    taps, rows, outs = w.shape
    return pl.pallas_call(
        spread_kernel,
        out_shape=jax.ShapeDtypeStruct((rows, CELLS), F32),
        in_specs=[VMEM] * 2,
        out_specs=VMEM,
        name="spread",
    )(w, g)


def grad_kernel(x_ref, g_ref, o_ref, left, right, acc):
    n = pl.program_id(0)
    ins, outs = x_ref.shape[1], g_ref.shape[1]

    @pl.when(n == 0)
    def _():
        acc[...] = jnp.zeros_like(acc)

    x = x_ref[0].astype(F32)
    g = g_ref[0].astype(F32)
    for e in range(3):
        right[e * ins : (e + 1) * ins, :] = moved(x, (0, 0, e - 1)).astype(BF16)
    for a in range(3):
        for b in range(3):
            at = (a * 3 + b) * outs
            left[at : at + outs, :] = moved(g, (1 - a, 1 - b, 0)).astype(BF16)
    acc[...] += lax.dot_general(
        left[...], right[...], (((1,), (1,)), ((), ())), preferred_element_type=F32
    )

    @pl.when(n == pl.num_programs(0) - 1)
    def _():
        for ab in range(9):
            for e in range(3):
                o_ref[ab * 3 + e] = acc[ab * outs : (ab + 1) * outs, e * ins : (e + 1) * ins]


def grad(x, g):
    count, ins, _ = x.shape
    outs = g.shape[1]
    return pl.pallas_call(
        grad_kernel,
        grid=(count,),
        out_shape=jax.ShapeDtypeStruct((27, outs, ins), F32),
        in_specs=[
            pl.BlockSpec((1, ins, CELLS), lambda n: (n, 0, 0)),
            pl.BlockSpec((1, outs, CELLS), lambda n: (n, 0, 0)),
        ],
        out_specs=pl.BlockSpec((27, outs, ins), lambda n: (0, 0, 0)),
        scratch_shapes=[
            pltpu.VMEM((9 * outs, CELLS), BF16),
            pltpu.VMEM((3 * ins, CELLS), BF16),
            pltpu.VMEM((9 * outs, 3 * ins), F32),
        ],
        name="grad",
    )(x, g)


def swap(v, axis):
    return lax.all_to_all(v, axis, 0, 0, tiled=True)


def body(samples, chans, snapshots, first_weight, second_weight, cotangent):
    ins = first_weight.shape[0]
    full = snapshots.shape[1]
    outs = full // samples
    first_w = first_weight.transpose(1, 0, 2)
    second_w = second_weight.transpose(1, 0, 2)

    part = snapshots[0].reshape(chans, ins, -1)
    packed = jnp.concatenate(
        [part, jnp.broadcast_to(cotangent, (chans,) + cotangent.shape[1:])], axis=2
    )
    packed = swap(packed, "chan")
    x = packed[:, :, : part.shape[2]].transpose(1, 0, 2).reshape(ins, CELLS)
    full_cot = packed[:, :, part.shape[2] :].reshape(full, CELLS)

    packed = jnp.concatenate(
        [jnp.broadcast_to(x, (samples,) + x.shape), full_cot.reshape(samples, outs, CELLS)], axis=1
    )
    packed = swap(packed, "sample")
    all_x, all_cot = packed[:, :ins], packed[:, ins:]

    first_parts = swap(conv(first_w, x).reshape(chans, ins, CELLS), "chan")
    hidden_grad = spread(second_w, full_cot)
    first_map = jnp.sum(first_parts.astype(F32), axis=0).astype(BF16).astype(F32)
    gate = jax.nn.sigmoid(first_map)
    hidden = (first_map * gate).astype(BF16)
    map_grad = (hidden_grad * gate * (1.0 + first_map * (1.0 - gate))).astype(BF16)

    second_parts = conv(second_w, hidden).reshape(chans, ins, CELLS)
    packed = jnp.concatenate(
        [second_parts, jnp.broadcast_to(map_grad, (chans,) + map_grad.shape)], axis=1
    )
    packed = swap(packed, "chan")
    second_out = jnp.sum(packed[:, :ins].astype(F32), axis=0).astype(BF16)
    full_map_grad = packed[:, ins:].reshape(samples, outs, CELLS)

    packed = jnp.concatenate(
        [jnp.broadcast_to(hidden, (samples,) + hidden.shape), full_map_grad], axis=1
    )
    packed = swap(packed, "sample")
    all_hidden, all_map_grad = packed[:, :ins], packed[:, ins:]

    second_grad = grad(all_hidden, all_cot)
    first_grad = grad(all_x, all_map_grad)
    return (
        second_out[None],
        first_grad.transpose(2, 0, 1),
        second_grad.transpose(2, 0, 1),
    )


def solution(mesh):
    placed = (
        P("sample", None, "chan"),
        P("chan", None, None),
        P("chan", None, None),
        P("sample", "chan", None),
    )
    return jax.shard_map(
        functools.partial(body, mesh.shape["sample"], mesh.shape["chan"]),
        mesh=mesh,
        in_specs=placed,
        out_specs=(P("sample", "chan", None), P("chan", None, "sample"), P("chan", None, "sample")),
        check_vma=False,
    )
```

time: 642 us -> 101 us (0.16)
  blocking collectives: 306 us -> 16.4 us
  other arithmetic: 181 us -> 6.94 us
  local copies, waits for them, and re-layouts: 124 us -> 5.46 us
  waiting for transfers between devices: 0.04 us -> 35.6 us
  Pallas kernels: 0 us -> 20.9 us
  between operations: 14.9 us -> 0.72 us
  matrix products: 8.92 us -> 0 us
  starting transfers between devices: 6.36 us -> 14.3 us
    unnamed x2 -> x0, blocking collectives: 277 us -> none
    slice x1, other arithmetic: 178 us -> 0.67 us  [body(): full_map_grad = packed[:, ins:].reshape(samples, outs, CELLS)]
    unnamed x76 -> x6, local copies, waits for them, and re-layouts: 46.2 us -> 0.01 us
    another operation x6 -> x0, local copies, waits for them, and re-layouts: 43.1 us -> none
    all_to_all x1 -> x4, waiting for transfers between devices: 0.01 us -> 35.6 us  [swap(): return lax.all_to_all(v, axis, 0, 0, tiled=True)]
    all_gather x2 -> x0, blocking collectives: 28.6 us -> none  [all_channels(): return lax.all_gather(grad_maps, 'chan', axis=1, tiled=True)]
    reshape x5 -> x1, local copies, waits for them, and re-layouts: 29.1 us -> 0.64 us  [body(): x = packed[:, :, :part.shape[2]].transpose(1, 0, 2).reshape(ins, CELLS)]
    pallas_call x0 -> x5, Pallas kernels: none -> 20.9 us  [the longest x2 12 us: grad(): pl.pallas_call(grad_kernel, grid=(count,), out_shape=jax.ShapeDtypeStruct...]
  transfers between devices with their start and end apart: 3 -> 4, of which waited for: 0 -> 4; matrix products, arithmetic and copies ran while one was open for 39% -> 5% of each run, Pallas kernels for 0% -> 3%
where the time goes in v1:
time: 101 us; the launch traced here: 100 us
  waiting for transfers between devices  35.6 us (35%)
  Pallas kernels  20.9 us (21%)
  blocking collectives  16.4 us (16%)
  starting transfers between devices  14.3 us (14%)
  other arithmetic  6.94 us (7%)
  local copies, waits for them, and re-layouts  5.46 us (5%)
    all_to_all x4, waiting for transfers between devices, swap(): return lax.all_to_all(v, axis, 0, 0, tiled=True)  35.6 us
    all_to_all x1, blocking collectives, swap(): return lax.all_to_all(v, axis, 0, 0, tiled=True)  16.4 us
    all_to_all x4, starting transfers between devices, swap(): return lax.all_to_all(v, axis, 0, 0, tiled=True)  14.3 us
    pallas_call x2, Pallas kernels, grad(): pl.pallas_call(grad_kernel, grid=(count,), out_shape=jax.ShapeDtypeStruct...  12 us
    pallas_call x2, Pallas kernels, conv(): pl.pallas_call(conv_kernel, out_shape=jax.ShapeDtypeStruct((outs, CELLS),...  5.54 us
    pallas_call x1, Pallas kernels, spread(): pl.pallas_call(spread_kernel, out_shape=jax.ShapeDtypeStruct((rows, CELLS...  3.39 us
  transfers between devices with their start and end apart: 4, of which 4 were waited for; matrix products, arithmetic and copies ran while one was open for 5% of the time, Pallas kernels for 3%

profile of v1, /device:TPU:0, one launch (start us, length us, event | category | flops | bytes accessed | tf_op | source)
XLA Modules:
  0.0 100.3 jit_solution(17176725278231760745)
XLA Ops:
  0.6 0.9 broadcast_in_dim.20
  1.5 0.9 pad_maximum_fusion.3
  2.4 16.4 %all_to_all.25 = bf16[4,64,640]{2,1,0:T(8,128)(2,1)S(1)} all-to-all(bf16[4,64,640]{2,1,0:T(8,128)(2,1)S(1)} %pad_maximum_fusion.3), channel_id=1, replica_groups=mesh['sample'=8,'chan'=4] {'chan'}, dimensions={0} | all-to-all | bytes 655360 | tf_op jit(solution)/shard_map/all_to_all | solution.py:134
  18.8 0.6 copy_bitcast_fusion.v_ref
  19.4 2.8 %conv.2 = bf16[256,512]{1,0:T(8,128)(2,1)} custom-call(bf16[27,64,256]{2,1,0:T(8,128)(2,1)} %bitcast.25, bf16[64,512]{1,0:T(8,128)(2,1)} %copy_bitcast_fusion.v_ref), custom_call_target="tpu_custom_call" | custom-call | tf_op jit(solution)/shard_map/conv/pallas_call | solution.py:55
  22.2 3.4 %all-to-all-start.1 = ((bf16[4,64,512]{2,1,0:T(8,128)(2,1)}), bf16[4,64,512]{2,1,0:T(8,128)(2,1)S(1)}, u32[]{:S(2)}, u32[]{:S(2)}) async-start(bf16[4,64,512]{2,1,0:T(8,128)(2,1)} %bitcast.22), calls=%async_computation.1 | async-start | bytes 524288 | tf_op jit(solution)/shard_map/all_to_all | solution.py:134
  25.6 0.7 slice.33
  26.3 3.4 %spread.1 = f32[64,512]{1,0:T(8,128)} custom-call(bf16[27,64,256]{2,1,0:T(8,128)(2,1)} %bitcast.18, bf16[256,512]{1,0:T(8,128)(2,1)} %bitcast.20), custom_call_target="tpu_custom_call" | custom-call | tf_op jit(solution)/shard_map/spread/pallas_call | solution.py:76
  29.7 3.7 %all-to-all-done.1 = bf16[4,64,512]{2,1,0:T(8,128)(2,1)S(1)} async-done(((bf16[4,64,512]{2,1,0:T(8,128)(2,1)}), bf16[4,64,512]{2,1,0:T(8,128)(2,1)S(1)}, u32[]{:S(2)}, u32[]{:S(2)}) %all-to-all-start.1) | async-done | bytes 262176 | tf_op jit(solution)/shard_map/all_to_all | solution.py:134
  33.4 1.6 %fusion.3 = (bf16[64,512]{1,0:T(8,128)(2,1)}, bf16[64,512]{1,0:T(8,128)(2,1)S(1)}) fusion(bf16[64,512]{1,0:T(8,128)(2,1)S(1)} %reduce_sum.24, f32[64,512]{1,0:T(8,128)} %spread.1), kind=kLoop, calls=%fused_computation.11 | loop fusion | flops 393216 | bytes 327680 | tf_op jit(solution)/shard_map/convert_element_type | solution.py:162
  35.0 2.8 %conv.3 = bf16[256,512]{1,0:T(8,128)(2,1)} custom-call(bf16[27,64,256]{2,1,0:T(8,128)(2,1)} %bitcast.19, bf16[64,512]{1,0:T(8,128)(2,1)} %get-tuple-element.5.v_ref), custom_call_target="tpu_custom_call" | custom-call | tf_op jit(solution)/shard_map/conv/pallas_call | solution.py:55
  37.8 0.0 copy-start.2
  37.8 1.8 %pad_maximum_fusion.2 = bf16[4,128,512]{2,1,0:T(8,128)(2,1)} fusion(bf16[4,64,512]{2,1,0:T(8,128)(2,1)S(1)} %broadcast_in_dim.21, bf16[4,64,512]{2,1,0:T(8,128)(2,1)} %bitcast.23), kind=kLoop, calls=%fused_computation.2 | loop fusion | flops 1048576 | bytes 1048576 | tf_op jit(solution)/shard_map/concatenate | solution.py:166
  39.6 0.0 copy-start
  39.6 3.6 %all-to-all-start.2 = ((bf16[4,128,512]{2,1,0:T(8,128)(2,1)}), bf16[4,128,512]{2,1,0:T(8,128)(2,1)S(1)}, u32[]{:S(2)}, u32[]{:S(2)}) async-start(bf16[4,128,512]{2,1,0:T(8,128)(2,1)} %pad_maximum_fusion.2), calls=%async_computation.2 | async-start | bytes 1048576 | tf_op jit(solution)/shard_map/all_to_all | solution.py:134
  43.2 0.0 copy-done.2
  43.3 0.0 copy-done
  43.3 1.0 pad_maximum_fusion
  44.3 10.1 %all-to-all-done.2 = bf16[4,128,512]{2,1,0:T(8,128)(2,1)S(1)} async-done(((bf16[4,128,512]{2,1,0:T(8,128)(2,1)}), bf16[4,128,512]{2,1,0:T(8,128)(2,1)S(1)}, u32[]{:S(2)}, u32[]{:S(2)}) %all-to-all-start.2) | async-done | bytes 524320 | tf_op jit(solution)/shard_map/all_to_all | solution.py:134
  54.3 3.7 %all-to-all-start.3 = ((bf16[8,96,512]{2,1,0:T(8,128)(2,1)}), bf16[8,96,512]{2,1,0:T(8,128)(2,1)S(1)}, u32[]{:S(2)}, u32[]{:S(2)}) async-start(bf16[8,96,512]{2,1,0:T(8,128)(2,1)} %pad_maximum_fusion), calls=%async_computation.3 | async-start | bytes 1572864 | tf_op jit(solution)/shard_map/all_to_all | solution.py:134
  58.0 0.7 fusion.7
  58.7 0.0 copy-done.1
  58.8 1.0 pad_maximum_fusion.1
  59.7 10.9 %all-to-all-done.3 = bf16[8,96,512]{2,1,0:T(8,128)(2,1)S(1)} async-done(((bf16[8,96,512]{2,1,0:T(8,128)(2,1)}), bf16[8,96,512]{2,1,0:T(8,128)(2,1)S(1)}, u32[]{:S(2)}, u32[]{:S(2)}) %all-to-all-start.3) | async-done | bytes 786464 | tf_op jit(solution)/shard_map/all_to_all | solution.py:134
  70.6 3.5 %all-to-all-start.4 = ((bf16[8,96,512]{2,1,0:T(8,128)(2,1)}), bf16[8,96,512]{2,1,0:T(8,128)(2,1)S(1)}, u32[]{:S(2)}, u32[]{:S(2)}) async-start(bf16[8,96,512]{2,1,0:T(8,128)(2,1)} %pad_maximum_fusion.1), calls=%async_computation.4 | async-start | bytes 1572864 | tf_op jit(solution)/shard_map/all_to_all | solution.py:134
  74.2 0.7 slice.39.g_ref
  74.9 0.8 slice.35.x_ref
  75.8 11.0 %all-to-all-done.4 = bf16[8,96,512]{2,1,0:T(8,128)(2,1)S(1)} async-done(((bf16[8,96,512]{2,1,0:T(8,128)(2,1)}), bf16[8,96,512]{2,1,0:T(8,128)(2,1)S(1)}, u32[]{:S(2)}, u32[]{:S(2)}) %all-to-all-start.4) | async-done | bytes 786464 | tf_op jit(solution)/shard_map/all_to_all | solution.py:134
  86.7 0.8 slice.38.x_ref
  87.6 6.0 %grad.3 = f32[27,32,64]{2,1,0:T(8,128)} custom-call(bf16[8,64,512]{2,1,0:T(8,128)(2,1)} %slice.38.x_ref, bf16[8,32,512]{2,1,0:T(8,128)(2,1)} %slice.39.g_ref), custom_call_target="tpu_custom_call" | custom-call | tf_op jit(solution)/shard_map/grad/pallas_call | solution.py:115
  93.6 0.7 slice.37.g_ref
  94.3 6.0 %grad.2 = f32[27,32,64]{2,1,0:T(8,128)} custom-call(bf16[8,64,512]{2,1,0:T(8,128)(2,1)} %slice.35.x_ref, bf16[8,32,512]{2,1,0:T(8,128)(2,1)} %slice.37.g_ref), custom_call_target="tpu_custom_call" | custom-call | tf_op jit(solution)/shard_map/grad/pallas_call | solution.py:115
  (5 shorter events, 0.1 us)
Async XLA Ops:
  22.2 11.2 %all-to-all-start.1 = ((bf16[4,64,512]{2,1,0:T(8,128)(2,1)}), bf16[4,64,512]{2,1,0:T(8,128)(2,1)S(1)}, u32[]{:S(2)}, u32[]{:S(2)}) async-start(bf16[4,64,512]{2,1,0:T(8,128)(2,1)} %bitcast.22), calls=%async_computation.1 | async-start | bytes 524288 | tf_op jit(solution)/shard_map/all_to_all | solution.py:134
  37.8 5.4 %copy-start.2 = (bf16[64,512]{1,0:T(8,128)(2,1)S(1)}, bf16[64,512]{1,0:T(8,128)(2,1)}, u32[]{:S(2)}) copy-start(bf16[64,512]{1,0:T(8,128)(2,1)} %copy_bitcast_fusion.v_ref) | copy-start | bytes 196612
  39.6 3.7 %copy-start = (bf16[4,64,512]{2,1,0:T(8,128)(2,1)S(1)}, bf16[4,64,512]{2,1,0:T(8,128)(2,1)}, u32[]{:S(2)}) copy-start(bf16[4,64,512]{2,1,0:T(8,128)(2,1)} %slice.33) | copy-start | bytes 786436
  39.6 14.7 %all-to-all-start.2 = ((bf16[4,128,512]{2,1,0:T(8,128)(2,1)}), bf16[4,128,512]{2,1,0:T(8,128)(2,1)S(1)}, u32[]{:S(2)}, u32[]{:S(2)}) async-start(bf16[4,128,512]{2,1,0:T(8,128)(2,1)} %pad_maximum_fusion.2), calls=%async_computation.2 | async-start | bytes 1048576 | tf_op jit(solution)/shard_map/all_to_all | solution.py:134
  44.3 14.5 %copy-start.1 = (bf16[64,512]{1,0:T(8,128)(2,1)S(1)}, bf16[64,512]{1,0:T(8,128)(2,1)}, u32[]{:S(2)}) copy-start(bf16[64,512]{1,0:T(8,128)(2,1)} %get-tuple-element.5.v_ref) | copy-start | bytes 196612
  54.3 16.3 %all-to-all-start.3 = ((bf16[8,96,512]{2,1,0:T(8,128)(2,1)}), bf16[8,96,512]{2,1,0:T(8,128)(2,1)S(1)}, u32[]{:S(2)}, u32[]{:S(2)}) async-start(bf16[8,96,512]{2,1,0:T(8,128)(2,1)} %pad_maximum_fusion), calls=%async_computation.3 | async-start | bytes 1572864 | tf_op jit(solution)/shard_map/all_to_all | solution.py:134
  70.6 16.1 %all-to-all-start.4 = ((bf16[8,96,512]{2,1,0:T(8,128)(2,1)}), bf16[8,96,512]{2,1,0:T(8,128)(2,1)S(1)}, u32[]{:S(2)}, u32[]{:S(2)}) async-start(bf16[8,96,512]{2,1,0:T(8,128)(2,1)} %pad_maximum_fusion.1), calls=%async_computation.4 | async-start | bytes 1572864 | tf_op jit(solution)/shard_map/all_to_all | solution.py:134

commit v2 on v1

v2 whole, which is shorter than its diff:
```python
import functools

import jax
import jax.numpy as jnp
from jax import lax
from jax.experimental import pallas as pl
from jax.experimental.pallas import tpu as pltpu
from jax.sharding import PartitionSpec as P

SIDE = 8
CELLS = SIDE**3
F32 = jnp.float32
BF16 = jnp.bfloat16
VMEM = pl.BlockSpec(memory_space=pltpu.VMEM)
TAPS = [(a, b, e) for a in (-1, 0, 1) for b in (-1, 0, 1) for e in (-1, 0, 1)]


def coords():
    cell = lax.broadcasted_iota(jnp.int32, (1, CELLS), 1)
    return cell >> 6, (cell >> 3) & 7, cell & 7


def moved(v, step):
    delta = 64 * step[0] + 8 * step[1] + step[2]
    if delta == 0:
        return v
    out = pltpu.roll(v, (-delta) % CELLS, 1)
    ok = None
    for at, by in zip(coords(), step):
        if by:
            good = at < SIDE - by if by > 0 else at >= -by
            ok = good if ok is None else ok & good
    return jnp.where(ok, out, jnp.zeros_like(out))


def call(kernel, outs, args, scratch=(), name=None):
    return pl.pallas_call(
        kernel,
        out_shape=[jax.ShapeDtypeStruct(shape, dtype) for shape, dtype in outs],
        in_specs=[VMEM] * len(args),
        out_specs=[VMEM] * len(outs),
        scratch_shapes=list(scratch),
        name=name,
    )(*args)


def block(j, chans, width):
    start = lax.rem(lax.axis_index("chan") + j, chans) * width
    return pl.ds(pl.multiple_of(start, width), width)


def split_kernel(chans, v_ref, *outs):
    rows = outs[0].shape[0]
    for j in range(chans):
        outs[j][...] = v_ref[block(j, chans, rows), :]


def conv_part(chans, w_ref, v, outs, patches, sums):
    rows = v.shape[0]
    for t, step in enumerate(TAPS):
        patches[t * rows : (t + 1) * rows, :] = moved(v, step)
    sums[...] = lax.dot_general(
        w_ref[...].reshape(-1, w_ref.shape[2]),
        patches[...],
        (((0,), (0,)), ((), ())),
        preferred_element_type=F32,
    ).astype(BF16)
    for j in range(chans):
        outs[j][...] = sums[block(j, chans, outs[j].shape[0]), :]


def first_kernel(chans, w_ref, *refs):
    parts, (x_ref, *outs), (patches, sums) = refs[:chans], refs[chans:-2], refs[-2:]
    width = CELLS // chans
    for j in range(chans):
        x_ref[:, block(chans - j, chans, width)] = parts[j][...]
    conv_part(chans, w_ref, x_ref[...], outs, patches, sums)


def second_kernel(chans, w_ref, v_ref, *refs):
    conv_part(chans, w_ref, v_ref[...], refs[:chans], *refs[chans:])


def join_kernel(chans, *refs):
    parts, out = refs[:chans], refs[chans]
    rows = parts[0].shape[0]
    for j in range(chans):
        out[block(chans - j, chans, rows), :] = parts[j][...]


def pack_kernel(chans, x_ref, *refs):
    parts, (full, out) = refs[:chans], refs[chans:]
    join_kernel(chans, *parts, full)
    rows = x_ref.shape[0]
    outs = out.shape[1] - rows
    for s in range(out.shape[0]):
        out[s, :rows, :] = x_ref[...]
        out[s, rows:, :] = full[s * outs : (s + 1) * outs, :]


def spread_kernel(w_ref, g_ref, o_ref):
    taps, rows, outs = w_ref.shape
    total = jnp.zeros((rows, CELLS), F32)
    for t, step in enumerate(TAPS):
        term = jnp.dot(w_ref[t], g_ref[...], preferred_element_type=F32)
        total = total + moved(term, tuple(-s for s in step))
    o_ref[...] = total


def middle_kernel(chans, hidden_grad, *refs):
    parts, (hidden_ref, copies_ref, map_grad_ref) = refs[:chans], refs[chans:]
    total = parts[0][...].astype(F32)
    for j in range(1, chans):
        total = total + parts[j][...].astype(F32)
    first_map = total.astype(BF16).astype(F32)
    gate = 1.0 / (1.0 + jnp.exp(-first_map))
    hidden = (first_map * gate).astype(BF16)
    hidden_ref[...] = hidden
    for s in range(copies_ref.shape[0]):
        copies_ref[s] = hidden
    map_grad_ref[...] = (hidden_grad[...] * gate * (1.0 + first_map * (1.0 - gate))).astype(BF16)


def grad_kernel(at, x_ref, g_ref, o_ref, left, right):
    count, outs, _ = g_ref.shape
    ins = o_ref.shape[2]
    for n in range(count):
        cells = pl.ds(n * CELLS, CELLS)
        x = x_ref[n, :ins, :]
        for e in range(3):
            right[e * ins : (e + 1) * ins, cells] = moved(x, (0, 0, e - 1))
        g = g_ref[n, at:, :]
        rows = g.shape[0]
        for a in range(3):
            for b in range(3):
                row = (a * 3 + b) * rows
                left[row : row + rows, cells] = moved(g, (1 - a, 1 - b, 0))
    acc = lax.dot_general(
        left[...], right[...], (((1,), (1,)), ((), ())), preferred_element_type=F32
    )
    rows = o_ref.shape[1]
    for ab in range(9):
        for e in range(3):
            o_ref[ab * 3 + e] = acc[ab * rows : (ab + 1) * rows, e * ins : (e + 1) * ins]


def grad(x, g, ins, at):
    count = x.shape[0]
    outs = g.shape[1] - at
    return call(
        functools.partial(grad_kernel, at),
        [((27, outs, ins), F32)],
        [x, g],
        [
            pltpu.VMEM((9 * outs, count * CELLS), BF16),
            pltpu.VMEM((3 * ins, count * CELLS), BF16),
        ],
        name="grad",
    )[0]


def swap(v, axis):
    return lax.all_to_all(v, axis, 0, 0, tiled=True)


def send(v, step, size):
    return lax.ppermute(v, "chan", [(k, (k + step) % size) for k in range(size)])


def exchange(parts, size):
    return [parts[0]] + [send(parts[j], j, size) for j in range(1, size)]


def body(samples, chans, snapshots, first_weight, second_weight, cotangent):
    ins = first_weight.shape[0]
    full = snapshots.shape[1]
    outs = full // samples
    width = CELLS // chans
    run = lambda kernel: functools.partial(kernel, chans)
    first_w = first_weight.transpose(1, 0, 2)
    second_w = second_weight.transpose(1, 0, 2)
    patches = [pltpu.VMEM((27 * ins, CELLS), BF16), pltpu.VMEM((full, CELLS), BF16)]
    piece = ((ins, CELLS), BF16)

    cots = exchange([cotangent[0]] * chans, chans)
    if width % 128 == 0:
        cells = [((ins, width), BF16)] * chans
        cells = exchange(call(run(split_kernel), cells, [snapshots[0]], name="split"), chans)
        x, *parts = call(
            run(first_kernel), [piece] * (chans + 1), [first_w] + cells, patches, "first"
        )
    else:
        x = swap(snapshots[0].reshape(chans, ins, width), "chan")
        x = x.transpose(1, 0, 2).reshape(ins, CELLS)
        parts = call(run(second_kernel), [piece] * chans, [first_w, x], patches, "first")
    parts = exchange(parts, chans)
    full_cot, packed = call(
        run(pack_kernel),
        [((full, CELLS), BF16), ((samples, ins + outs, CELLS), BF16)],
        [x] + cots,
        name="pack",
    )
    packed = swap(packed, "sample")
    hidden_grad = call(spread_kernel, [((ins, CELLS), F32)], [second_w, full_cot], name="spread")[0]
    hidden, copies, map_grad = call(
        run(middle_kernel),
        [piece, ((samples, ins, CELLS), BF16), piece],
        [hidden_grad] + parts,
        name="middle",
    )
    all_hidden = swap(copies, "sample")
    map_grads = exchange([map_grad] * chans, chans)
    parts = exchange(
        call(run(second_kernel), [piece] * chans, [second_w, hidden], patches, "second"), chans
    )
    full_map_grad = call(run(join_kernel), [((full, CELLS), BF16)], map_grads, name="join")[0]
    all_map_grad = swap(full_map_grad.reshape(samples, outs, CELLS), "sample")
    second_out = sum(p.astype(F32) for p in parts).astype(BF16)
    second_grad = grad(all_hidden, packed, ins, ins)
    first_grad = grad(packed, all_map_grad, ins, 0)
    return (
        second_out[None],
        first_grad.transpose(2, 0, 1),
        second_grad.transpose(2, 0, 1),
    )


def solution(mesh):
    placed = (
        P("sample", None, "chan"),
        P("chan", None, None),
        P("chan", None, None),
        P("sample", "chan", None),
    )
    return jax.shard_map(
        functools.partial(body, mesh.shape["sample"], mesh.shape["chan"]),
        mesh=mesh,
        in_specs=placed,
        out_specs=(P("sample", "chan", None), P("chan", None, "sample"), P("chan", None, "sample")),
        check_vma=False,
    )
```

time: 101 us -> 76.8 us (0.76)
  waiting for transfers between devices: 35.6 us -> 3.68 us
  starting transfers between devices: 14.3 us -> 31.3 us
  other arithmetic: 6.94 us -> 0.67 us
  blocking collectives: 16.4 us -> 13.9 us
  local copies, waits for them, and re-layouts: 5.46 us -> 3.85 us
    all_to_all x4 -> x2, waiting for transfers between devices: 35.6 us -> 3.22 us  [swap(): return lax.all_to_all(v, axis, 0, 0, tiled=True)]
    ppermute x0 -> x15, starting transfers between devices: none -> 23.4 us  [send(): lax.ppermute(v, 'chan', [(k, (k + step) % size) for k in range(size)])]
    all_to_all x4 -> x2, starting transfers between devices: 14.3 us -> 7.89 us  [swap(): return lax.all_to_all(v, axis, 0, 0, tiled=True)]
    concatenate x4 -> x0, other arithmetic: 4.64 us -> none  [the longest x1 1.81 us: body(): jnp.concatenate([second_parts, jnp.broadcast_to(map_grad, (chans,) + map_...]
    slice x5 -> x0, local copies, waits for them, and re-layouts: 3.86 us -> none  [the longest x2 1.57 us: body(): all_x, all_cot = (packed[:, :ins], packed[:, ins:])]
    unnamed x6 -> x34, local copies, waits for them, and re-layouts: 0.01 us -> 3.85 us
    all_to_all x1, blocking collectives: 16.4 us -> 13.9 us  [swap(): return lax.all_to_all(v, axis, 0, 0, tiled=True)]
    convert_element_type x1 -> x0, other arithmetic: 1.59 us -> none  [body(): hidden = (first_map * gate).astype(BF16)]
  transfers between devices with their start and end apart: 4 -> 17, of which waited for: 4 -> 2; matrix products, arithmetic and copies ran while one was open for 5% -> 1% of each run, Pallas kernels for 3% -> 22%
where the time goes in v2:
time: 76.8 us; the launch traced here: 76.1 us
  starting transfers between devices  31.3 us (41%)
  Pallas kernels  21.9 us (29%)
  blocking collectives  13.9 us (18%)
  local copies, waits for them, and re-layouts  3.85 us (5%)
  waiting for transfers between devices  3.68 us (5%)
  between operations  0.77 us (1%)
    ppermute x15, starting transfers between devices, send(): lax.ppermute(v, 'chan', [(k, (k + step) % size) for k in range(size)])  23.4 us
    pallas_call x9, Pallas kernels, call(): pl.pallas_call(kernel, out_shape=[jax.ShapeDtypeStruct(shape, dtype) for...  21.9 us
    all_to_all x1, blocking collectives, swap(): return lax.all_to_all(v, axis, 0, 0, tiled=True)  13.9 us
    all_to_all x2, starting transfers between devices, swap(): return lax.all_to_all(v, axis, 0, 0, tiled=True)  7.89 us
    unnamed x34, local copies, waits for them, and re-layouts  3.85 us
    all_to_all x2, waiting for transfers between devices, swap(): return lax.all_to_all(v, axis, 0, 0, tiled=True)  3.22 us
  transfers between devices with their start and end apart: 17, of which 2 were waited for; matrix products, arithmetic and copies ran while one was open for 1% of the time, Pallas kernels for 22%

profile of v2, /device:TPU:0, one launch (start us, length us, event | category | flops | bytes accessed | tf_op | source)
XLA Modules:
  0.0 76.1 jit_solution(14203378504597140093)
XLA Ops:
  0.6 5.1 %collective-permute-start.5 = (bf16[64,512]{1,0:T(8,128)(2,1)}, bf16[64,512]{1,0:T(8,128)(2,1)S(1)}, u32[]{:S(2)}, u32[]{:S(2)}) collective-permute-start(bf16[64,512]{1,0:T(8,128)(2,1)} %bitcast.15), channel_id=1, source_target_pairs={{0,3},{1,0},{2,1},{3,2},{4,7},{5,4},{6,5},{7,6},{8,11},{9,8},{10,9... | collective-permute-start | bytes 196616 | tf_op jit(solution)/shard_map/ppermute | solution.py:167
  5.7 1.5 %split.1 = (bf16[64,128]{1,0:T(8,128)(2,1)}, bf16[64,128]{1,0:T(8,128)(2,1)}, bf16[64,128]{1,0:T(8,128)(2,1)}, bf16[64,128]{1,0:T(8,128)(2,1)}) custom-call(bf16[256,128]{1,0:T(8,128)(2,1)} %bitcast.19), custom_call_target="tpu_custom_call" | custom-call | tf_op jit(solution)/shard_map/split/pallas_call | solution.py:37
  7.2 1.0 %collective-permute-start.1 = (bf16[64,128]{1,0:T(8,128)(2,1)}, bf16[64,128]{1,0:T(8,128)(2,1)S(1)}, u32[]{:S(2)}, u32[]{:S(2)}) collective-permute-start(bf16[64,128]{1,0:T(8,128)(2,1)} %get-tuple-element.23), channel_id=1, source_target_pairs={{0,2},{1,3},{2,0},{3,1},{4,6},{5,7},{6,4},{7,5},{8,10},{9,11},{10,... | collective-permute-start | bytes 49160 | tf_op jit(solution)/shard_map/ppermute | solution.py:167
  8.2 2.8 %collective-permute-start.2 = (bf16[64,128]{1,0:T(8,128)(2,1)}, bf16[64,128]{1,0:T(8,128)(2,1)S(1)}, u32[]{:S(2)}, u32[]{:S(2)}) collective-permute-start(bf16[64,128]{1,0:T(8,128)(2,1)} %get-tuple-element.24), channel_id=1, source_target_pairs={{0,3},{1,0},{2,1},{3,2},{4,7},{5,4},{6,5},{7,6},{8,11},{9,8},{10,9... | collective-permute-start | bytes 49160 | tf_op jit(solution)/shard_map/ppermute | solution.py:167
  11.0 2.0 %collective-permute-start.4 = (bf16[64,512]{1,0:T(8,128)(2,1)S(1)}, bf16[64,512]{1,0:T(8,128)(2,1)S(1)}, u32[]{:S(2)}, u32[]{:S(2)}) collective-permute-start(bf16[64,512]{1,0:T(8,128)(2,1)S(1)} %bitcast.17), channel_id=1, source_target_pairs={{0,2},{1,3},{2,0},{3,1},{4,6},{5,7},{6,4},{7,5},{8,10},{9,11},{10,... | collective-permute-start | bytes 196616 | tf_op jit(solution)/shard_map/ppermute | solution.py:167
  13.7 0.4 copy-done.16
  14.1 2.8 %first.1 = (bf16[64,512]{1,0:T(8,128)(2,1)}, bf16[64,512]{1,0:T(8,128)(2,1)}, bf16[64,512]{1,0:T(8,128)(2,1)}, bf16[64,512]{1,0:T(8,128)(2,1)}, bf16[64,512]{1,0:T(8,128)(2,1)}) custom-call(bf16[27,64,256]{2,1,0:T(8,128)(2,1)} %bitcast.12, bf16[64,128]{1,0:T(8,128)(2,1)} %get-tuple-element.21.refs_0_, bf16[64,128]{1,0:T(8,128)(2,1)} %copy-done.14, ...), custom_call_target="tpu_custom_call" | custom-call | tf_op jit(solution)/shard_map/first/pallas_call | solution.py:37
  16.9 2.1 %collective-permute-start.6 = (bf16[64,512]{1,0:T(8,128)(2,1)}, bf16[64,512]{1,0:T(8,128)(2,1)S(1)}, u32[]{:S(2)}, u32[]{:S(2)}) collective-permute-start(bf16[64,512]{1,0:T(8,128)(2,1)} %get-tuple-element.28), channel_id=1, source_target_pairs={{0,1},{1,2},{2,3},{3,0},{4,5},{5,6},{6,7},{7,4},{8,9},{9,10},{10,1... | collective-permute-start | bytes 196616 | tf_op jit(solution)/shard_map/ppermute | solution.py:167
  19.1 1.9 %collective-permute-start.7 = (bf16[64,512]{1,0:T(8,128)(2,1)}, bf16[64,512]{1,0:T(8,128)(2,1)S(1)}, u32[]{:S(2)}, u32[]{:S(2)}) collective-permute-start(bf16[64,512]{1,0:T(8,128)(2,1)} %get-tuple-element.29), channel_id=1, source_target_pairs={{0,2},{1,3},{2,0},{3,1},{4,6},{5,7},{6,4},{7,5},{8,10},{9,11},{10,... | collective-permute-start | bytes 196616 | tf_op jit(solution)/shard_map/ppermute | solution.py:167
  20.9 0.5 collective-permute-start.8
  21.6 0.5 copy-done.4
  22.1 2.0 %pack.1 = (bf16[256,512]{1,0:T(8,128)(2,1)}, bf16[8,96,512]{2,1,0:T(8,128)(2,1)}) custom-call(bf16[64,512]{1,0:T(8,128)(2,1)} %get-tuple-element.25.x_ref, bf16[64,512]{1,0:T(8,128)(2,1)} %bitcast.16, bf16[64,512]{1,0:T(8,128)(2,1)} %copy-done.6, bf16[64,512]{1,0:T(8,128)(2,1)} %copy-done.4, bf16[64,512]{1,0:T(8,128)(2,1)} %copy-done.3), custom_call_target="tpu_custom_call" | custom-call | tf_op jit(solution)/shard_map/pack/pallas_call | solution.py:37
  24.1 3.4 %spread.1.hidden_grad = f32[64,512]{1,0:T(8,128)} custom-call(bf16[27,64,256]{2,1,0:T(8,128)(2,1)} %bitcast.9, bf16[256,512]{1,0:T(8,128)(2,1)} %get-tuple-element.26.g_ref), custom_call_target="tpu_custom_call" | custom-call | tf_op jit(solution)/shard_map/spread/pallas_call | solution.py:37
  27.5 0.6 copy-done.7
  28.2 1.9 %middle.1 = (bf16[64,512]{1,0:T(8,128)(2,1)}, bf16[8,64,512]{2,1,0:T(8,128)(2,1)}, bf16[64,512]{1,0:T(8,128)(2,1)}) custom-call(f32[64,512]{1,0:T(8,128)} %spread.1.hidden_grad, bf16[64,512]{1,0:T(8,128)(2,1)} %get-tuple-element.27.refs_0_, bf16[64,512]{1,0:T(8,128)(2,1)} %copy-done.7, bf16[64,512]{1,0:T(8,128)(2,1)} %copy-done.8, bf16[64,512]{1,0:T(8,128)(2,1)} %copy-done.9), custom_call_target="tpu_custom_call" | custom-call | tf_op jit(solution)/shard_map/middle/pallas_call | solution.py:37
  30.1 13.9 %all_to_all.15.x_ref = bf16[8,64,512]{2,1,0:T(8,128)(2,1)} all-to-all(bf16[8,64,512]{2,1,0:T(8,128)(2,1)} %get-tuple-element.38), channel_id=1, replica_groups=mesh['sample'=8,'chan'=4] {'sample'}, dimensions={0} | all-to-all | bytes 1048576 | tf_op jit(solution)/shard_map/all_to_all | solution.py:163
  44.0 3.7 %all-to-all-start = ((bf16[8,96,512]{2,1,0:T(8,128)(2,1)}), bf16[8,96,512]{2,1,0:T(8,128)(2,1)S(1)}, u32[]{:S(2)}, u32[]{:S(2)}) async-start(bf16[8,96,512]{2,1,0:T(8,128)(2,1)} %get-tuple-element.36), calls=%async_computation | async-start | bytes 1572864 | tf_op jit(solution)/shard_map/all_to_all | solution.py:163
  47.7 2.1 %collective-permute-start.14 = (bf16[64,512]{1,0:T(8,128)(2,1)S(1)}, bf16[64,512]{1,0:T(8,128)(2,1)S(1)}, u32[]{:S(2)}, u32[]{:S(2)}) collective-permute-start(bf16[64,512]{1,0:T(8,128)(2,1)S(1)} %copy-done.10), channel_id=1, source_target_pairs={{0,3},{1,0},{2,1},{3,2},{4,7},{5,4},{6,5},{7,6},{8,11},{9,8},{10,9... | collective-permute-start | bytes 196616 | tf_op jit(solution)/shard_map/ppermute | solution.py:167
  49.7 1.0 %collective-permute-start.13 = (bf16[64,512]{1,0:T(8,128)(2,1)S(1)}, bf16[64,512]{1,0:T(8,128)(2,1)S(1)}, u32[]{:S(2)}, u32[]{:S(2)}) collective-permute-start(bf16[64,512]{1,0:T(8,128)(2,1)S(1)} %copy-done.10), channel_id=1, source_target_pairs={{0,2},{1,3},{2,0},{3,1},{4,6},{5,7},{6,4},{7,5},{8,10},{9,11},{10,... | collective-permute-start | bytes 196616 | tf_op jit(solution)/shard_map/ppermute | solution.py:167
  51.1 2.7 %second.1 = (bf16[64,512]{1,0:T(8,128)(2,1)}, bf16[64,512]{1,0:T(8,128)(2,1)}, bf16[64,512]{1,0:T(8,128)(2,1)}, bf16[64,512]{1,0:T(8,128)(2,1)}) custom-call(bf16[27,64,256]{2,1,0:T(8,128)(2,1)} %bitcast.10, bf16[64,512]{1,0:T(8,128)(2,1)} %get-tuple-element.31.v_ref), custom_call_target="tpu_custom_call" | custom-call | tf_op jit(solution)/shard_map/second/pallas_call | solution.py:37
  53.8 2.1 %collective-permute-start.9 = (bf16[64,512]{1,0:T(8,128)(2,1)}, bf16[64,512]{1,0:T(8,128)(2,1)S(1)}, u32[]{:S(2)}, u32[]{:S(2)}) collective-permute-start(bf16[64,512]{1,0:T(8,128)(2,1)} %get-tuple-element.33), channel_id=1, source_target_pairs={{0,1},{1,2},{2,3},{3,0},{4,5},{5,6},{6,7},{7,4},{8,9},{9,10},{10,1... | collective-permute-start | bytes 196616 | tf_op jit(solution)/shard_map/ppermute | solution.py:167
  56.0 1.9 %collective-permute-start.10 = (bf16[64,512]{1,0:T(8,128)(2,1)}, bf16[64,512]{1,0:T(8,128)(2,1)S(1)}, u32[]{:S(2)}, u32[]{:S(2)}) collective-permute-start(bf16[64,512]{1,0:T(8,128)(2,1)} %get-tuple-element.34), channel_id=1, source_target_pairs={{0,2},{1,3},{2,0},{3,1},{4,6},{5,7},{6,4},{7,5},{8,10},{9,11},{10,... | collective-permute-start | bytes 196616 | tf_op jit(solution)/shard_map/ppermute | solution.py:167
  57.9 0.5 collective-permute-start.11
  58.5 0.5 copy-done.12
  59.0 0.6 copy-done.13
  59.6 1.7 %join.1 = bf16[256,512]{1,0:T(8,128)(2,1)} custom-call(bf16[64,512]{1,0:T(8,128)(2,1)} %get-tuple-element.37.refs_0_, bf16[64,512]{1,0:T(8,128)(2,1)} %copy-done.13, bf16[64,512]{1,0:T(8,128)(2,1)} %copy-done.12, bf16[64,512]{1,0:T(8,128)(2,1)} %copy-done.11), custom_call_target="tpu_custom_call" | custom-call | tf_op jit(solution)/shard_map/join/pallas_call | solution.py:37
  61.3 4.2 %all-to-all-start.1 = ((bf16[8,32,512]{2,1,0:T(8,128)(2,1)}), bf16[8,32,512]{2,1,0:T(8,128)(2,1)S(1)}, u32[]{:S(2)}, u32[]{:S(2)}) async-start(bf16[8,32,512]{2,1,0:T(8,128)(2,1)} %bitcast.11), calls=%async_computation.1 | async-start | bytes 524288 | tf_op jit(solution)/shard_map/all_to_all | solution.py:163
  65.5 0.7 fusion
  66.2 3.0 %grad.3 = f32[27,32,64]{2,1,0:T(8,128)} custom-call(bf16[8,64,512]{2,1,0:T(8,128)(2,1)} %all_to_all.15.x_ref, bf16[8,96,512]{2,1,0:T(8,128)(2,1)} %copy-done), custom_call_target="tpu_custom_call" | custom-call | tf_op jit(solution)/shard_map/grad/pallas_call | solution.py:37
  69.2 3.2 %all-to-all-done.1.g_ref = bf16[8,32,512]{2,1,0:T(8,128)(2,1)S(1)} async-done(((bf16[8,32,512]{2,1,0:T(8,128)(2,1)}), bf16[8,32,512]{2,1,0:T(8,128)(2,1)S(1)}, u32[]{:S(2)}, u32[]{:S(2)}) %all-to-all-start.1) | async-done | bytes 262176 | tf_op jit(solution)/shard_map/all_to_all | solution.py:163
  72.4 0.7 copy-done.1
  73.1 2.9 %grad.2 = f32[27,32,64]{2,1,0:T(8,128)} custom-call(bf16[8,96,512]{2,1,0:T(8,128)(2,1)} %copy-done, bf16[8,32,512]{2,1,0:T(8,128)(2,1)} %copy-done.1), custom_call_target="tpu_custom_call" | custom-call | tf_op jit(solution)/shard_map/grad/pallas_call | solution.py:37
  (47 shorter events, 1.3 us)
Async XLA Ops:
  0.6 10.4 %copy-start.2 = (bf16[1,64,512]{2,1,0:T(8,128)(2,1)S(1)}, bf16[1,64,512]{2,1,0:T(8,128)(2,1)}, u32[]{:S(2)}) copy-start(bf16[1,64,512]{2,1,0:T(8,128)(2,1)} %param.7) | copy-start | bytes 196612
  0.6 20.3 %collective-permute-start.5 = (bf16[64,512]{1,0:T(8,128)(2,1)}, bf16[64,512]{1,0:T(8,128)(2,1)S(1)}, u32[]{:S(2)}, u32[]{:S(2)}) collective-permute-start(bf16[64,512]{1,0:T(8,128)(2,1)} %bitcast.15), channel_id=1, source_target_pairs={{0,3},{1,0},{2,1},{3,2},{4,7},{5,4},{6,5},{7,6},{8,11},{9,8},{10,9... | collective-permute-start | bytes 196616 | tf_op jit(solution)/shard_map/ppermute | solution.py:167
  7.2 5.9 %collective-permute-start = (bf16[64,128]{1,0:T(8,128)(2,1)}, bf16[64,128]{1,0:T(8,128)(2,1)S(1)}, u32[]{:S(2)}, u32[]{:S(2)}) collective-permute-start(bf16[64,128]{1,0:T(8,128)(2,1)} %get-tuple-element.22), channel_id=1, source_target_pairs={{0,1},{1,2},{2,3},{3,0},{4,5},{5,6},{6,7},{7,4},{8,9},{9,10},{10,1... | collective-permute-start | bytes 49160 | tf_op jit(solution)/shard_map/ppermute | solution.py:167
  7.2 5.9 %collective-permute-start.1 = (bf16[64,128]{1,0:T(8,128)(2,1)}, bf16[64,128]{1,0:T(8,128)(2,1)S(1)}, u32[]{:S(2)}, u32[]{:S(2)}) collective-permute-start(bf16[64,128]{1,0:T(8,128)(2,1)} %get-tuple-element.23), channel_id=1, source_target_pairs={{0,2},{1,3},{2,0},{3,1},{4,6},{5,7},{6,4},{7,5},{8,10},{9,11},{10,... | collective-permute-start | bytes 49160 | tf_op jit(solution)/shard_map/ppermute | solution.py:167
  8.2 5.3 %collective-permute-start.2 = (bf16[64,128]{1,0:T(8,128)(2,1)}, bf16[64,128]{1,0:T(8,128)(2,1)S(1)}, u32[]{:S(2)}, u32[]{:S(2)}) collective-permute-start(bf16[64,128]{1,0:T(8,128)(2,1)} %get-tuple-element.24), channel_id=1, source_target_pairs={{0,3},{1,0},{2,1},{3,2},{4,7},{5,4},{6,5},{7,6},{8,11},{9,8},{10,9... | collective-permute-start | bytes 49160 | tf_op jit(solution)/shard_map/ppermute | solution.py:167
  11.0 10.4 %collective-permute-start.4 = (bf16[64,512]{1,0:T(8,128)(2,1)S(1)}, bf16[64,512]{1,0:T(8,128)(2,1)S(1)}, u32[]{:S(2)}, u32[]{:S(2)}) collective-permute-start(bf16[64,512]{1,0:T(8,128)(2,1)S(1)} %bitcast.17), channel_id=1, source_target_pairs={{0,2},{1,3},{2,0},{3,1},{4,6},{5,7},{6,4},{7,5},{8,10},{9,11},{10,... | collective-permute-start | bytes 196616 | tf_op jit(solution)/shard_map/ppermute | solution.py:167
  13.1 8.4 %collective-permute-start.3 = (bf16[64,512]{1,0:T(8,128)(2,1)S(1)}, bf16[64,512]{1,0:T(8,128)(2,1)S(1)}, u32[]{:S(2)}, u32[]{:S(2)}) collective-permute-start(bf16[64,512]{1,0:T(8,128)(2,1)S(1)} %bitcast.18), channel_id=1, source_target_pairs={{0,1},{1,2},{2,3},{3,0},{4,5},{5,6},{6,7},{7,4},{8,9},{9,10},{10,1... | collective-permute-start | bytes 196616 | tf_op jit(solution)/shard_map/ppermute | solution.py:167
  13.1 0.6 copy-start.15
  16.9 10.6 %collective-permute-start.6 = (bf16[64,512]{1,0:T(8,128)(2,1)}, bf16[64,512]{1,0:T(8,128)(2,1)S(1)}, u32[]{:S(2)}, u32[]{:S(2)}) collective-permute-start(bf16[64,512]{1,0:T(8,128)(2,1)} %get-tuple-element.28), channel_id=1, source_target_pairs={{0,1},{1,2},{2,3},{3,0},{4,5},{5,6},{6,7},{7,4},{8,9},{9,10},{10,1... | collective-permute-start | bytes 196616 | tf_op jit(solution)/shard_map/ppermute | solution.py:167
  19.1 8.4 %collective-permute-start.7 = (bf16[64,512]{1,0:T(8,128)(2,1)}, bf16[64,512]{1,0:T(8,128)(2,1)S(1)}, u32[]{:S(2)}, u32[]{:S(2)}) collective-permute-start(bf16[64,512]{1,0:T(8,128)(2,1)} %get-tuple-element.29), channel_id=1, source_target_pairs={{0,2},{1,3},{2,0},{3,1},{4,6},{5,7},{6,4},{7,5},{8,10},{9,11},{10,... | collective-permute-start | bytes 196616 | tf_op jit(solution)/shard_map/ppermute | solution.py:167
  20.9 0.6 copy-start.3
  20.9 6.6 %collective-permute-start.8 = (bf16[64,512]{1,0:T(8,128)(2,1)}, bf16[64,512]{1,0:T(8,128)(2,1)S(1)}, u32[]{:S(2)}, u32[]{:S(2)}) collective-permute-start(bf16[64,512]{1,0:T(8,128)(2,1)} %get-tuple-element.30), channel_id=1, source_target_pairs={{0,3},{1,0},{2,1},{3,2},{4,7},{5,4},{6,5},{7,6},{8,11},{9,8},{10,9... | collective-permute-start | bytes 196616 | tf_op jit(solution)/shard_map/ppermute | solution.py:167
  21.4 0.6 copy-start.4
  21.5 0.6 copy-start.6
  27.5 0.6 copy-start.7
  27.5 0.6 copy-start.8
  27.5 0.6 copy-start.9
  44.0 3.7 %copy-start.10 = (bf16[64,512]{1,0:T(8,128)(2,1)S(1)}, bf16[64,512]{1,0:T(8,128)(2,1)}, u32[]{:S(2)}) copy-start(bf16[64,512]{1,0:T(8,128)(2,1)} %get-tuple-element.37.refs_0_) | copy-start | bytes 196612
  44.0 17.3 %all-to-all-start = ((bf16[8,96,512]{2,1,0:T(8,128)(2,1)}), bf16[8,96,512]{2,1,0:T(8,128)(2,1)S(1)}, u32[]{:S(2)}, u32[]{:S(2)}) async-start(bf16[8,96,512]{2,1,0:T(8,128)(2,1)} %get-tuple-element.36), calls=%async_computation | async-start | bytes 1572864 | tf_op jit(solution)/shard_map/all_to_all | solution.py:163
  47.7 10.2 %collective-permute-start.14 = (bf16[64,512]{1,0:T(8,128)(2,1)S(1)}, bf16[64,512]{1,0:T(8,128)(2,1)S(1)}, u32[]{:S(2)}, u32[]{:S(2)}) collective-permute-start(bf16[64,512]{1,0:T(8,128)(2,1)S(1)} %copy-done.10), channel_id=1, source_target_pairs={{0,3},{1,0},{2,1},{3,2},{4,7},{5,4},{6,5},{7,6},{8,11},{9,8},{10,9... | collective-permute-start | bytes 196616 | tf_op jit(solution)/shard_map/ppermute | solution.py:167
  49.7 8.6 %collective-permute-start.13 = (bf16[64,512]{1,0:T(8,128)(2,1)S(1)}, bf16[64,512]{1,0:T(8,128)(2,1)S(1)}, u32[]{:S(2)}, u32[]{:S(2)}) collective-permute-start(bf16[64,512]{1,0:T(8,128)(2,1)S(1)} %copy-done.10), channel_id=1, source_target_pairs={{0,2},{1,3},{2,0},{3,1},{4,6},{5,7},{6,4},{7,5},{8,10},{9,11},{10,... | collective-permute-start | bytes 196616 | tf_op jit(solution)/shard_map/ppermute | solution.py:167
  50.7 7.6 %collective-permute-start.12 = (bf16[64,512]{1,0:T(8,128)(2,1)S(1)}, bf16[64,512]{1,0:T(8,128)(2,1)S(1)}, u32[]{:S(2)}, u32[]{:S(2)}) collective-permute-start(bf16[64,512]{1,0:T(8,128)(2,1)S(1)} %copy-done.10), channel_id=1, source_target_pairs={{0,1},{1,2},{2,3},{3,0},{4,5},{5,6},{6,7},{7,4},{8,9},{9,10},{10,1... | collective-permute-start | bytes 196616 | tf_op jit(solution)/shard_map/ppermute | solution.py:167
  53.8 11.7 %collective-permute-start.9 = (bf16[64,512]{1,0:T(8,128)(2,1)}, bf16[64,512]{1,0:T(8,128)(2,1)S(1)}, u32[]{:S(2)}, u32[]{:S(2)}) collective-permute-start(bf16[64,512]{1,0:T(8,128)(2,1)} %get-tuple-element.33), channel_id=1, source_target_pairs={{0,1},{1,2},{2,3},{3,0},{4,5},{5,6},{6,7},{7,4},{8,9},{9,10},{10,1... | collective-permute-start | bytes 196616 | tf_op jit(solution)/shard_map/ppermute | solution.py:167
  56.0 9.5 %collective-permute-start.10 = (bf16[64,512]{1,0:T(8,128)(2,1)}, bf16[64,512]{1,0:T(8,128)(2,1)S(1)}, u32[]{:S(2)}, u32[]{:S(2)}) collective-permute-start(bf16[64,512]{1,0:T(8,128)(2,1)} %get-tuple-element.34), channel_id=1, source_target_pairs={{0,2},{1,3},{2,0},{3,1},{4,6},{5,7},{6,4},{7,5},{8,10},{9,11},{10,... | collective-permute-start | bytes 196616 | tf_op jit(solution)/shard_map/ppermute | solution.py:167
  57.9 0.6 copy-start.11
  57.9 7.7 %collective-permute-start.11 = (bf16[64,512]{1,0:T(8,128)(2,1)}, bf16[64,512]{1,0:T(8,128)(2,1)S(1)}, u32[]{:S(2)}, u32[]{:S(2)}) collective-permute-start(bf16[64,512]{1,0:T(8,128)(2,1)} %get-tuple-element.35), channel_id=1, source_target_pairs={{0,3},{1,0},{2,1},{3,2},{4,7},{5,4},{6,5},{7,6},{8,11},{9,8},{10,9... | collective-permute-start | bytes 196616 | tf_op jit(solution)/shard_map/ppermute | solution.py:167
  58.4 0.6 copy-start.12
  59.0 0.6 copy-start.13
  61.3 4.9 %copy-start = (bf16[8,96,512]{2,1,0:T(8,128)(2,1)}, bf16[8,96,512]{2,1,0:T(8,128)(2,1)S(1)}, u32[]{:S(2)}) copy-start(bf16[8,96,512]{2,1,0:T(8,128)(2,1)S(1)} %all-to-all-done.x_ref.g_ref) | copy-start | bytes 2359300
  61.3 4.2 %copy-start.5 = (bf16[64,512]{1,0:T(8,128)(2,1)S(1)}, bf16[64,512]{1,0:T(8,128)(2,1)}, u32[]{:S(2)}) copy-start(bf16[64,512]{1,0:T(8,128)(2,1)} %get-tuple-element.32) | copy-start | bytes 196612
  61.3 11.2 %all-to-all-start.1 = ((bf16[8,32,512]{2,1,0:T(8,128)(2,1)}), bf16[8,32,512]{2,1,0:T(8,128)(2,1)S(1)}, u32[]{:S(2)}, u32[]{:S(2)}) async-start(bf16[8,32,512]{2,1,0:T(8,128)(2,1)} %bitcast.11), calls=%async_computation.1 | async-start | bytes 524288 | tf_op jit(solution)/shard_map/all_to_all | solution.py:163
  72.4 0.7 copy-start.1
  (2 other events, 1.2 us)

commit v3 on v2

--- a/solution.py
+++ b/solution.py
@@ -33,13 +33,16 @@
     return jnp.where(ok, out, jnp.zeros_like(out))
 
 
-def call(kernel, outs, args, scratch=(), name=None):
+def call(kernel, outs, args, scratch=(), name=None, us=1.0):
     return pl.pallas_call(
         kernel,
         out_shape=[jax.ShapeDtypeStruct(shape, dtype) for shape, dtype in outs],
         in_specs=[VMEM] * len(args),
         out_specs=[VMEM] * len(outs),
         scratch_shapes=list(scratch),
+        cost_estimate=pl.CostEstimate(
+            flops=int(us * 1.1e9), bytes_accessed=int(us * 3.0e6), transcendentals=0
+        ),
         name=name,
     )(*args)
 
@@ -49,10 +52,12 @@
     return pl.ds(pl.multiple_of(start, width), width)
 
 
-def split_kernel(chans, v_ref, *outs):
-    rows = outs[0].shape[0]
-    for j in range(chans):
-        outs[j][...] = v_ref[block(j, chans, rows), :]
+def split_kernel(chans, v_ref, g_ref, own, *outs):
+    rows, width = own.shape
+    own[...] = v_ref[block(0, chans, rows), :]
+    for j, out in enumerate(outs):
+        out[:, :width] = v_ref[block(j + 1, chans, rows), :]
+        out[:, width:] = g_ref[...]
 
 
 def conv_part(chans, w_ref, v, outs, patches, sums):
@@ -69,12 +74,25 @@
         outs[j][...] = sums[block(j, chans, outs[j].shape[0]), :]
 
 
-def first_kernel(chans, w_ref, *refs):
-    parts, (x_ref, *outs), (patches, sums) = refs[:chans], refs[chans:-2], refs[-2:]
-    width = CELLS // chans
-    for j in range(chans):
-        x_ref[:, block(chans - j, chans, width)] = parts[j][...]
-    conv_part(chans, w_ref, x_ref[...], outs, patches, sums)
+def first_kernel(chans, w_ref, own, g_ref, *refs):
+    parts, (packed, full, *outs), scratch = refs[: chans - 1], refs[chans - 1 : -3], refs[-3:]
+    x, *scratch = scratch
+    rows, width = own.shape
+    x[:, block(0, chans, width)] = own[...]
+    full[block(0, chans, rows), :] = g_ref[...]
+    for j, part in enumerate(parts):
+        x[:, block(chans - j - 1, chans, width)] = part[:, :width]
+        full[block(chans - j - 1, chans, rows), :] = part[:, width:]
+    conv_part(chans, w_ref, x[...], outs, *scratch)
+    fill(packed, x, full)
+
+
+def fill(packed, x, full):
+    rows = x.shape[0]
+    outs = packed.shape[1] - rows
+    for s in range(packed.shape[0]):
+        packed[s, :rows, :] = x[...]
+        packed[s, rows:, :] = full[s * outs : (s + 1) * outs, :]
 
 
 def second_kernel(chans, w_ref, v_ref, *refs):
@@ -89,13 +107,9 @@
 
 
 def pack_kernel(chans, x_ref, *refs):
-    parts, (full, out) = refs[:chans], refs[chans:]
+    parts, (packed, full) = refs[:chans], refs[chans:]
     join_kernel(chans, *parts, full)
-    rows = x_ref.shape[0]
-    outs = out.shape[1] - rows
-    for s in range(out.shape[0]):
-        out[s, :rows, :] = x_ref[...]
-        out[s, rows:, :] = full[s * outs : (s + 1) * outs, :]
+    fill(packed, x_ref, full)
 
 
 def spread_kernel(w_ref, g_ref, o_ref):
@@ -156,6 +170,7 @@
             pltpu.VMEM((3 * ins, count * CELLS), BF16),
         ],
         name="grad",
+        us=3.0,
     )[0]
 
 
@@ -182,38 +197,43 @@
     patches = [pltpu.VMEM((27 * ins, CELLS), BF16), pltpu.VMEM((full, CELLS), BF16)]
     piece = ((ins, CELLS), BF16)
 
-    cots = exchange([cotangent[0]] * chans, chans)
+    gathered = [((samples, ins + outs, CELLS), BF16), ((full, CELLS), BF16)]
     if width % 128 == 0:
-        cells = [((ins, width), BF16)] * chans
-        cells = exchange(call(run(split_kernel), cells, [snapshots[0]], name="split"), chans)
-        x, *parts = call(
-            run(first_kernel), [piece] * (chans + 1), [first_w] + cells, patches, "first"
+        cells = [((ins, width), BF16)] + [((ins, width + CELLS), BF16)] * (chans - 1)
+        cells = call(run(split_kernel), cells, [snapshots[0], cotangent[0]], name="split")
+        own, *cells = exchange(cells, chans)
+        packed, full_cot, *parts = call(
+            run(first_kernel),
+            gathered + [piece] * chans,
+            [first_w, own, cotangent[0]] + cells,
+            [pltpu.VMEM((ins, CELLS), BF16)] + patches,
+            "first",
+            3.0,
         )
     else:
         x = swap(snapshots[0].reshape(chans, ins, width), "chan")
         x = x.transpose(1, 0, 2).reshape(ins, CELLS)
-        parts = call(run(second_kernel), [piece] * chans, [first_w, x], patches, "first")
+        parts = call(run(second_kernel), [piece] * chans, [first_w, x], patches, "first", 2.8)
+        cots = exchange([cotangent[0]] * chans, chans)
+        packed, full_cot = call(run(pack_kernel), gathered, [x] + cots, name="pack")
     parts = exchange(parts, chans)
-    full_cot, packed = call(
-        run(pack_kernel),
-        [((full, CELLS), BF16), ((samples, ins + outs, CELLS), BF16)],
-        [x] + cots,
-        name="pack",
-    )
     packed = swap(packed, "sample")
-    hidden_grad = call(spread_kernel, [((ins, CELLS), F32)], [second_w, full_cot], name="spread")[0]
+    hidden_grad = call(spread_kernel, [((ins, CELLS), F32)], [second_w, full_cot], (), "spread", 3.4)[0]
     hidden, copies, map_grad = call(
         run(middle_kernel),
         [piece, ((samples, ins, CELLS), BF16), piece],
         [hidden_grad] + parts,
         name="middle",
-    )
+        us=2.0,
+    )
+    copies, packed = lax.optimization_barrier((copies, packed))
     all_hidden = swap(copies, "sample")
     map_grads = exchange([map_grad] * chans, chans)
     parts = exchange(
-        call(run(second_kernel), [piece] * chans, [second_w, hidden], patches, "second"), chans
+        call(run(second_kernel), [piece] * chans, [second_w, hidden], patches, "second", 2.8), chans
     )
     full_map_grad = call(run(join_kernel), [((full, CELLS), BF16)], map_grads, name="join")[0]
+    full_map_grad, all_hidden = lax.optimization_barrier((full_map_grad, all_hidden))
     all_map_grad = swap(full_map_grad.reshape(samples, outs, CELLS), "sample")
     second_out = sum(p.astype(F32) for p in parts).astype(BF16)
     second_grad = grad(all_hidden, packed, ins, ins)

time: 76.8 us -> 69.1 us (0.90)
  blocking collectives: 13.9 us -> 0 us
  waiting for transfers between devices: 3.68 us -> 11.9 us
  Pallas kernels: 21.9 us -> 20.3 us
    all_to_all x1 -> x0, blocking collectives: 13.9 us -> none  [swap(): return lax.all_to_all(v, axis, 0, 0, tiled=True)]
    ppermute x15 -> x12, waiting for transfers between devices: 0.46 us -> 8 us  [send(): lax.ppermute(v, 'chan', [(k, (k + step) % size) for k in range(size)])]
    all_to_all x2 -> x3, starting transfers between devices: 7.89 us -> 11.7 us  [swap(): return lax.all_to_all(v, axis, 0, 0, tiled=True)]
    ppermute x15 -> x12, starting transfers between devices: 23.4 us -> 19.9 us  [send(): lax.ppermute(v, 'chan', [(k, (k + step) % size) for k in range(size)])]
    pallas_call x9 -> x8, Pallas kernels: 21.9 us -> 20.3 us  [call(): pl.pallas_call(kernel, out_shape=[jax.ShapeDtypeStruct(shape, dtype) for...]
    all_to_all x2 -> x3, waiting for transfers between devices: 3.22 us -> 3.92 us  [swap(): return lax.all_to_all(v, axis, 0, 0, tiled=True)]
    unnamed x34 -> x32, local copies, waits for them, and re-layouts: 3.85 us -> 3.2 us
  transfers between devices with their start and end apart: 17 -> 15, of which waited for: 2 -> 8; matrix products, arithmetic and copies ran while one was open for 1% -> 1% of each run, Pallas kernels for 22% -> 19%
where the time goes in v3:
time: 69.1 us; the launch traced here: 68.4 us
  starting transfers between devices  31.6 us (46%)
  Pallas kernels  20.3 us (29%)
  waiting for transfers between devices  11.9 us (17%)
  local copies, waits for them, and re-layouts  3.2 us (5%)
    pallas_call x8, Pallas kernels, call(): pl.pallas_call(kernel, out_shape=[jax.ShapeDtypeStruct(shape, dtype) for...  20.3 us
    ppermute x12, starting transfers between devices, send(): lax.ppermute(v, 'chan', [(k, (k + step) % size) for k in range(size)])  19.9 us
    all_to_all x3, starting transfers between devices, swap(): return lax.all_to_all(v, axis, 0, 0, tiled=True)  11.7 us
    ppermute x12, waiting for transfers between devices, send(): lax.ppermute(v, 'chan', [(k, (k + step) % size) for k in range(size)])  8 us
    all_to_all x3, waiting for transfers between devices, swap(): return lax.all_to_all(v, axis, 0, 0, tiled=True)  3.92 us
    unnamed x32, local copies, waits for them, and re-layouts  3.2 us
  transfers between devices with their start and end apart: 15, of which 8 were waited for; matrix products, arithmetic and copies ran while one was open for 1% of the time, Pallas kernels for 19%

profile of v3, /device:TPU:0, one launch (start us, length us, event | category | flops | bytes accessed | tf_op | source)
XLA Modules:
  0.0 68.4 jit_solution(1044558883658077106)
XLA Ops:
  0.6 1.6 %split.1 = (bf16[64,128]{1,0:T(8,128)(2,1)}, bf16[64,640]{1,0:T(8,128)(2,1)}, bf16[64,640]{1,0:T(8,128)(2,1)}, bf16[64,640]{1,0:T(8,128)(2,1)}) custom-call(bf16[256,128]{1,0:T(8,128)(2,1)} %bitcast.12, bf16[64,512]{1,0:T(8,128)(2,1)} %bitcast.13), custom_call_target="tpu_custom_call" | custom-call | flops 1100000000 | bytes 3000000 | tf_op jit(solution)/shard_map/split/pallas_call | solution.py:37
  2.2 3.0 %collective-permute-start = (bf16[64,640]{1,0:T(8,128)(2,1)}, bf16[64,640]{1,0:T(8,128)(2,1)S(1)}, u32[]{:S(2)}, u32[]{:S(2)}) collective-permute-start(bf16[64,640]{1,0:T(8,128)(2,1)} %get-tuple-element.25), channel_id=1, source_target_pairs={{0,1},{1,2},{2,3},{3,0},{4,5},{5,6},{6,7},{7,4},{8,9},{9,10},{10,1... | collective-permute-start | bytes 245768 | tf_op jit(solution)/shard_map/ppermute | solution.py:182
  5.2 2.6 %collective-permute-start.1 = (bf16[64,640]{1,0:T(8,128)(2,1)}, bf16[64,640]{1,0:T(8,128)(2,1)S(1)}, u32[]{:S(2)}, u32[]{:S(2)}) collective-permute-start(bf16[64,640]{1,0:T(8,128)(2,1)} %get-tuple-element.26), channel_id=1, source_target_pairs={{0,2},{1,3},{2,0},{3,1},{4,6},{5,7},{6,4},{7,5},{8,10},{9,11},{10,... | collective-permute-start | bytes 245768 | tf_op jit(solution)/shard_map/ppermute | solution.py:182
  7.8 1.3 %collective-permute-start.2 = (bf16[64,640]{1,0:T(8,128)(2,1)}, bf16[64,640]{1,0:T(8,128)(2,1)S(1)}, u32[]{:S(2)}, u32[]{:S(2)}) collective-permute-start(bf16[64,640]{1,0:T(8,128)(2,1)} %get-tuple-element.27), channel_id=1, source_target_pairs={{0,3},{1,0},{2,1},{3,2},{4,7},{5,4},{6,5},{7,6},{8,11},{9,8},{10,9... | collective-permute-start | bytes 245768 | tf_op jit(solution)/shard_map/ppermute | solution.py:182
  9.2 1.3 %collective-permute-done.refs_0_ = bf16[64,640]{1,0:T(8,128)(2,1)S(1)} collective-permute-done((bf16[64,640]{1,0:T(8,128)(2,1)}, bf16[64,640]{1,0:T(8,128)(2,1)S(1)}, u32[]{:S(2)}, u32[]{:S(2)}) %collective-permute-start) | collective-permute-done | bytes 81952 | tf_op jit(solution)/shard_map/ppermute | solution.py:182
  10.5 3.0 %collective-permute-done.1.refs_1_ = bf16[64,640]{1,0:T(8,128)(2,1)S(1)} collective-permute-done((bf16[64,640]{1,0:T(8,128)(2,1)}, bf16[64,640]{1,0:T(8,128)(2,1)S(1)}, u32[]{:S(2)}, u32[]{:S(2)}) %collective-permute-start.1) | collective-permute-done | bytes 81952 | tf_op jit(solution)/shard_map/ppermute | solution.py:182
  14.4 3.1 %first.1 = (bf16[8,96,512]{2,1,0:T(8,128)(2,1)}, bf16[256,512]{1,0:T(8,128)(2,1)}, bf16[64,512]{1,0:T(8,128)(2,1)}, bf16[64,512]{1,0:T(8,128)(2,1)}, bf16[64,512]{1,0:T(8,128)(2,1)}, /*index=5*/bf16[64,512]{1,0:T(8,128)(2,1)}) custom-call(bf16[27,64,256]{2,1,0:T(8,128)(2,1)} %bitcast.9, bf16[64,128]{1,0:T(8,128)(2,1)} %get-tuple-element.24.own, ...), custom_call_target="tpu_custom_call" | custom-call | flops 3300000000 | bytes 9000000 | tf_op jit(solution)/shard_map/first/pallas_call | solution.py:37
  17.5 3.9 %all-to-all-start = ((bf16[8,96,512]{2,1,0:T(8,128)(2,1)}), bf16[8,96,512]{2,1,0:T(8,128)(2,1)S(1)}, u32[]{:S(2)}, u32[]{:S(2)}) async-start(bf16[8,96,512]{2,1,0:T(8,128)(2,1)} %get-tuple-element.39), calls=%async_computation | async-start | bytes 1572864 | tf_op jit(solution)/shard_map/all_to_all | solution.py:178
  21.3 2.1 %collective-permute-start.3 = (bf16[64,512]{1,0:T(8,128)(2,1)S(1)}, bf16[64,512]{1,0:T(8,128)(2,1)S(1)}, u32[]{:S(2)}, u32[]{:S(2)}) collective-permute-start(bf16[64,512]{1,0:T(8,128)(2,1)S(1)} %copy-done.12), channel_id=1, source_target_pairs={{0,1},{1,2},{2,3},{3,0},{4,5},{5,6},{6,7},{7,4},{8,9},{9,10},{10,1... | collective-permute-start | bytes 196616 | tf_op jit(solution)/shard_map/ppermute | solution.py:182
  23.4 1.8 %collective-permute-start.4 = (bf16[64,512]{1,0:T(8,128)(2,1)S(1)}, bf16[64,512]{1,0:T(8,128)(2,1)S(1)}, u32[]{:S(2)}, u32[]{:S(2)}) collective-permute-start(bf16[64,512]{1,0:T(8,128)(2,1)S(1)} %copy-done.11), channel_id=1, source_target_pairs={{0,2},{1,3},{2,0},{3,1},{4,6},{5,7},{6,4},{7,5},{8,10},{9,11},{10,... | collective-permute-start | bytes 196616 | tf_op jit(solution)/shard_map/ppermute | solution.py:182
  25.2 0.7 collective-permute-start.5
  25.9 3.4 %spread.1.hidden_grad = f32[64,512]{1,0:T(8,128)} custom-call(bf16[27,64,256]{2,1,0:T(8,128)(2,1)} %bitcast.10, bf16[256,512]{1,0:T(8,128)(2,1)} %get-tuple-element.28.g_ref), custom_call_target="tpu_custom_call" | custom-call | flops 3740000000 | bytes 10200000 | tf_op jit(solution)/shard_map/spread/pallas_call | solution.py:37
  29.3 1.3 %collective-permute-done.4.refs_2_ = bf16[64,512]{1,0:T(8,128)(2,1)S(1)} collective-permute-done((bf16[64,512]{1,0:T(8,128)(2,1)S(1)}, bf16[64,512]{1,0:T(8,128)(2,1)S(1)}, u32[]{:S(2)}, u32[]{:S(2)}) %collective-permute-start.4) | collective-permute-done | bytes 65568 | tf_op jit(solution)/shard_map/ppermute | solution.py:182
  31.4 2.0 %middle.1 = (bf16[64,512]{1,0:T(8,128)(2,1)}, bf16[8,64,512]{2,1,0:T(8,128)(2,1)}, bf16[64,512]{1,0:T(8,128)(2,1)}) custom-call(f32[64,512]{1,0:T(8,128)} %spread.1.hidden_grad, bf16[64,512]{1,0:T(8,128)(2,1)} %get-tuple-element.29.refs_0_, bf16[64,512]{1,0:T(8,128)(2,1)} %copy-done.13, bf16[64,512]{1,0:T(8,128)(2,1)} %copy-done.14, bf16[64,512]{1,0:T(8,128)(2,1)} %copy-done.15), custom_call_target="tpu_custom_call" | custom-call | flops 2200000000 | bytes 6000000 | tf_op jit(solution)/shard_map/middle/pallas_call | solution.py:37
  33.3 2.4 %collective-permute-start.11 = (bf16[64,512]{1,0:T(8,128)(2,1)}, bf16[64,512]{1,0:T(8,128)(2,1)S(1)}, u32[]{:S(2)}, u32[]{:S(2)}) collective-permute-start(bf16[64,512]{1,0:T(8,128)(2,1)} %get-tuple-element.41.refs_0_), channel_id=1, source_target_pairs={{0,3},{1,0},{2,1},{3,2},{4,7},{5,4},{6,5},{7,6},{8,11},{9,8},{10,9... | collective-permute-start | bytes 196616 | tf_op jit(solution)/shard_map/ppermute | solution.py:182
  35.8 0.7 collective-permute-start.10
  36.5 3.9 %all-to-all-start.1 = ((bf16[8,64,512]{2,1,0:T(8,128)(2,1)}), bf16[8,64,512]{2,1,0:T(8,128)(2,1)S(1)}, u32[]{:S(2)}, u32[]{:S(2)}) async-start(bf16[8,64,512]{2,1,0:T(8,128)(2,1)} %get-tuple-element.42), calls=%async_computation.1 | async-start | bytes 1048576 | tf_op jit(solution)/shard_map/all_to_all | solution.py:178
  40.3 2.7 %second.1 = (bf16[64,512]{1,0:T(8,128)(2,1)}, bf16[64,512]{1,0:T(8,128)(2,1)}, bf16[64,512]{1,0:T(8,128)(2,1)}, bf16[64,512]{1,0:T(8,128)(2,1)}) custom-call(bf16[27,64,256]{2,1,0:T(8,128)(2,1)} %bitcast.11, bf16[64,512]{1,0:T(8,128)(2,1)} %get-tuple-element.33.v_ref), custom_call_target="tpu_custom_call" | custom-call | flops 3080000000 | bytes 8400000 | tf_op jit(solution)/shard_map/second/pallas_call | solution.py:37
  43.1 2.9 %collective-permute-start.6 = (bf16[64,512]{1,0:T(8,128)(2,1)}, bf16[64,512]{1,0:T(8,128)(2,1)S(1)}, u32[]{:S(2)}, u32[]{:S(2)}) collective-permute-start(bf16[64,512]{1,0:T(8,128)(2,1)} %get-tuple-element.35), channel_id=1, source_target_pairs={{0,1},{1,2},{2,3},{3,0},{4,5},{5,6},{6,7},{7,4},{8,9},{9,10},{10,1... | collective-permute-start | bytes 196616 | tf_op jit(solution)/shard_map/ppermute | solution.py:182
  46.0 1.5 %collective-permute-start.7 = (bf16[64,512]{1,0:T(8,128)(2,1)}, bf16[64,512]{1,0:T(8,128)(2,1)S(1)}, u32[]{:S(2)}, u32[]{:S(2)}) collective-permute-start(bf16[64,512]{1,0:T(8,128)(2,1)} %get-tuple-element.36), channel_id=1, source_target_pairs={{0,2},{1,3},{2,0},{3,1},{4,6},{5,7},{6,4},{7,5},{8,10},{9,11},{10,... | collective-permute-start | bytes 196616 | tf_op jit(solution)/shard_map/ppermute | solution.py:182
  47.4 0.9 %collective-permute-start.8 = (bf16[64,512]{1,0:T(8,128)(2,1)}, bf16[64,512]{1,0:T(8,128)(2,1)S(1)}, u32[]{:S(2)}, u32[]{:S(2)}) collective-permute-start(bf16[64,512]{1,0:T(8,128)(2,1)} %get-tuple-element.37), channel_id=1, source_target_pairs={{0,3},{1,0},{2,1},{3,2},{4,7},{5,4},{6,5},{7,6},{8,11},{9,8},{10,9... | collective-permute-start | bytes 196616 | tf_op jit(solution)/shard_map/ppermute | solution.py:182
  48.4 0.6 copy-done.8
  49.0 0.6 copy-done.9
  49.6 1.7 %join.1 = bf16[256,512]{1,0:T(8,128)(2,1)} custom-call(bf16[64,512]{1,0:T(8,128)(2,1)} %get-tuple-element.41.refs_0_, bf16[64,512]{1,0:T(8,128)(2,1)} %copy-done.9, bf16[64,512]{1,0:T(8,128)(2,1)} %copy-done.8, bf16[64,512]{1,0:T(8,128)(2,1)} %copy-done.7), custom_call_target="tpu_custom_call" | custom-call | flops 1100000000 | bytes 3000000 | tf_op jit(solution)/shard_map/join/pallas_call | solution.py:37
  51.3 1.5 %collective-permute-done.7 = bf16[64,512]{1,0:T(8,128)(2,1)S(1)} collective-permute-done((bf16[64,512]{1,0:T(8,128)(2,1)}, bf16[64,512]{1,0:T(8,128)(2,1)S(1)}, u32[]{:S(2)}, u32[]{:S(2)}) %collective-permute-start.7) | collective-permute-done | bytes 65568 | tf_op jit(solution)/shard_map/ppermute | solution.py:182
  52.8 0.5 collective-permute-done.8
  53.2 0.7 fusion
  53.9 4.0 %all-to-all-start.2 = ((bf16[8,32,512]{2,1,0:T(8,128)(2,1)}), bf16[8,32,512]{2,1,0:T(8,128)(2,1)S(1)}, u32[]{:S(2)}, u32[]{:S(2)}) async-start(bf16[8,32,512]{2,1,0:T(8,128)(2,1)} %bitcast.5), calls=%async_computation.2 | async-start | bytes 524288 | tf_op jit(solution)/shard_map/all_to_all | solution.py:178
  57.9 3.0 %grad.3 = f32[27,32,64]{2,1,0:T(8,128)} custom-call(bf16[8,64,512]{2,1,0:T(8,128)(2,1)} %copy-done.1, bf16[8,96,512]{2,1,0:T(8,128)(2,1)} %copy-done), custom_call_target="tpu_custom_call" | custom-call | flops 3300000000 | bytes 9000000 | tf_op jit(solution)/shard_map/grad/pallas_call | solution.py:37
  60.9 3.9 %all-to-all-done.2.g_ref = bf16[8,32,512]{2,1,0:T(8,128)(2,1)S(1)} async-done(((bf16[8,32,512]{2,1,0:T(8,128)(2,1)}), bf16[8,32,512]{2,1,0:T(8,128)(2,1)S(1)}, u32[]{:S(2)}, u32[]{:S(2)}) %all-to-all-start.2) | async-done | bytes 262176 | tf_op jit(solution)/shard_map/all_to_all | solution.py:178
  64.8 0.7 %copy-done.2 = bf16[8,32,512]{2,1,0:T(8,128)(2,1)} copy-done((bf16[8,32,512]{2,1,0:T(8,128)(2,1)}, bf16[8,32,512]{2,1,0:T(8,128)(2,1)S(1)}, u32[]{:S(2)}) %copy-start.2) | copy-done | bytes 262168
  65.5 2.9 %grad.2 = f32[27,32,64]{2,1,0:T(8,128)} custom-call(bf16[8,96,512]{2,1,0:T(8,128)(2,1)} %copy-done, bf16[8,32,512]{2,1,0:T(8,128)(2,1)} %copy-done.2), custom_call_target="tpu_custom_call" | custom-call | flops 3300000000 | bytes 9000000 | tf_op jit(solution)/shard_map/grad/pallas_call | solution.py:37
  (39 shorter events, 1.7 us)
Async XLA Ops:
  2.2 8.3 %collective-permute-start = (bf16[64,640]{1,0:T(8,128)(2,1)}, bf16[64,640]{1,0:T(8,128)(2,1)S(1)}, u32[]{:S(2)}, u32[]{:S(2)}) collective-permute-start(bf16[64,640]{1,0:T(8,128)(2,1)} %get-tuple-element.25), channel_id=1, source_target_pairs={{0,1},{1,2},{2,3},{3,0},{4,5},{5,6},{6,7},{7,4},{8,9},{9,10},{10,1... | collective-permute-start | bytes 245768 | tf_op jit(solution)/shard_map/ppermute | solution.py:182
  5.2 8.3 %collective-permute-start.1 = (bf16[64,640]{1,0:T(8,128)(2,1)}, bf16[64,640]{1,0:T(8,128)(2,1)S(1)}, u32[]{:S(2)}, u32[]{:S(2)}) collective-permute-start(bf16[64,640]{1,0:T(8,128)(2,1)} %get-tuple-element.26), channel_id=1, source_target_pairs={{0,2},{1,3},{2,0},{3,1},{4,6},{5,7},{6,4},{7,5},{8,10},{9,11},{10,... | collective-permute-start | bytes 245768 | tf_op jit(solution)/shard_map/ppermute | solution.py:182
  7.8 5.9 %collective-permute-start.2 = (bf16[64,640]{1,0:T(8,128)(2,1)}, bf16[64,640]{1,0:T(8,128)(2,1)S(1)}, u32[]{:S(2)}, u32[]{:S(2)}) collective-permute-start(bf16[64,640]{1,0:T(8,128)(2,1)} %get-tuple-element.27), channel_id=1, source_target_pairs={{0,3},{1,0},{2,1},{3,2},{4,7},{5,4},{6,5},{7,6},{8,11},{9,8},{10,9... | collective-permute-start | bytes 245768 | tf_op jit(solution)/shard_map/ppermute | solution.py:182
  10.5 3.3 %copy-start.4 = (bf16[64,640]{1,0:T(8,128)(2,1)}, bf16[64,640]{1,0:T(8,128)(2,1)S(1)}, u32[]{:S(2)}) copy-start(bf16[64,640]{1,0:T(8,128)(2,1)S(1)} %collective-permute-done.refs_0_) | copy-start | bytes 245764
  13.5 0.6 copy-start.5
  13.7 0.6 copy-start.6
  17.5 3.9 %copy-start.12 = (bf16[64,512]{1,0:T(8,128)(2,1)S(1)}, bf16[64,512]{1,0:T(8,128)(2,1)}, u32[]{:S(2)}) copy-start(bf16[64,512]{1,0:T(8,128)(2,1)} %get-tuple-element.30) | copy-start | bytes 196612
  17.5 5.9 %copy-start.11 = (bf16[64,512]{1,0:T(8,128)(2,1)S(1)}, bf16[64,512]{1,0:T(8,128)(2,1)}, u32[]{:S(2)}) copy-start(bf16[64,512]{1,0:T(8,128)(2,1)} %get-tuple-element.31) | copy-start | bytes 196612
  17.5 7.7 %copy-start.10 = (bf16[64,512]{1,0:T(8,128)(2,1)S(1)}, bf16[64,512]{1,0:T(8,128)(2,1)}, u32[]{:S(2)}) copy-start(bf16[64,512]{1,0:T(8,128)(2,1)} %get-tuple-element.32) | copy-start | bytes 196612
  17.5 19.0 %all-to-all-start = ((bf16[8,96,512]{2,1,0:T(8,128)(2,1)}), bf16[8,96,512]{2,1,0:T(8,128)(2,1)S(1)}, u32[]{:S(2)}, u32[]{:S(2)}) async-start(bf16[8,96,512]{2,1,0:T(8,128)(2,1)} %get-tuple-element.39), calls=%async_computation | async-start | bytes 1572864 | tf_op jit(solution)/shard_map/all_to_all | solution.py:178
  21.3 7.9 %collective-permute-start.3 = (bf16[64,512]{1,0:T(8,128)(2,1)S(1)}, bf16[64,512]{1,0:T(8,128)(2,1)S(1)}, u32[]{:S(2)}, u32[]{:S(2)}) collective-permute-start(bf16[64,512]{1,0:T(8,128)(2,1)S(1)} %copy-done.12), channel_id=1, source_target_pairs={{0,1},{1,2},{2,3},{3,0},{4,5},{5,6},{6,7},{7,4},{8,9},{9,10},{10,1... | collective-permute-start | bytes 196616 | tf_op jit(solution)/shard_map/ppermute | solution.py:182
  23.4 7.1 %collective-permute-start.4 = (bf16[64,512]{1,0:T(8,128)(2,1)S(1)}, bf16[64,512]{1,0:T(8,128)(2,1)S(1)}, u32[]{:S(2)}, u32[]{:S(2)}) collective-permute-start(bf16[64,512]{1,0:T(8,128)(2,1)S(1)} %copy-done.11), channel_id=1, source_target_pairs={{0,2},{1,3},{2,0},{3,1},{4,6},{5,7},{6,4},{7,5},{8,10},{9,11},{10,... | collective-permute-start | bytes 196616 | tf_op jit(solution)/shard_map/ppermute | solution.py:182
  25.2 5.6 %collective-permute-start.5 = (bf16[64,512]{1,0:T(8,128)(2,1)S(1)}, bf16[64,512]{1,0:T(8,128)(2,1)S(1)}, u32[]{:S(2)}, u32[]{:S(2)}) collective-permute-start(bf16[64,512]{1,0:T(8,128)(2,1)S(1)} %copy-done.10), channel_id=1, source_target_pairs={{0,3},{1,0},{2,1},{3,2},{4,7},{5,4},{6,5},{7,6},{8,11},{9,8},{10,9... | collective-permute-start | bytes 196616 | tf_op jit(solution)/shard_map/ppermute | solution.py:182
  29.3 1.5 %copy-start.13 = (bf16[64,512]{1,0:T(8,128)(2,1)}, bf16[64,512]{1,0:T(8,128)(2,1)S(1)}, u32[]{:S(2)}) copy-start(bf16[64,512]{1,0:T(8,128)(2,1)S(1)} %collective-permute-done.3.refs_1_) | copy-start | bytes 196612
  30.6 0.6 copy-start.14
  30.8 0.6 copy-start.15
  33.3 14.1 %collective-permute-start.11 = (bf16[64,512]{1,0:T(8,128)(2,1)}, bf16[64,512]{1,0:T(8,128)(2,1)S(1)}, u32[]{:S(2)}, u32[]{:S(2)}) collective-permute-start(bf16[64,512]{1,0:T(8,128)(2,1)} %get-tuple-element.41.refs_0_), channel_id=1, source_target_pairs={{0,3},{1,0},{2,1},{3,2},{4,7},{5,4},{6,5},{7,6},{8,11},{9,8},{10,9... | collective-permute-start | bytes 196616 | tf_op jit(solution)/shard_map/ppermute | solution.py:182
  35.8 12.6 %collective-permute-start.10 = (bf16[64,512]{1,0:T(8,128)(2,1)}, bf16[64,512]{1,0:T(8,128)(2,1)S(1)}, u32[]{:S(2)}, u32[]{:S(2)}) collective-permute-start(bf16[64,512]{1,0:T(8,128)(2,1)} %get-tuple-element.41.refs_0_), channel_id=1, source_target_pairs={{0,2},{1,3},{2,0},{3,1},{4,6},{5,7},{6,4},{7,5},{8,10},{9,11},{10,... | collective-permute-start | bytes 196616 | tf_op jit(solution)/shard_map/ppermute | solution.py:182
  36.5 11.9 %collective-permute-start.9 = (bf16[64,512]{1,0:T(8,128)(2,1)}, bf16[64,512]{1,0:T(8,128)(2,1)S(1)}, u32[]{:S(2)}, u32[]{:S(2)}) collective-permute-start(bf16[64,512]{1,0:T(8,128)(2,1)} %get-tuple-element.41.refs_0_), channel_id=1, source_target_pairs={{0,1},{1,2},{2,3},{3,0},{4,5},{5,6},{6,7},{7,4},{8,9},{9,10},{10,1... | collective-permute-start | bytes 196616 | tf_op jit(solution)/shard_map/ppermute | solution.py:182
  36.5 6.6 %copy-start = (bf16[8,96,512]{2,1,0:T(8,128)(2,1)}, bf16[8,96,512]{2,1,0:T(8,128)(2,1)S(1)}, u32[]{:S(2)}) copy-start(bf16[8,96,512]{2,1,0:T(8,128)(2,1)S(1)} %all-to-all-done.x_ref.g_ref) | copy-start | bytes 2359300
  36.5 17.4 %all-to-all-start.1 = ((bf16[8,64,512]{2,1,0:T(8,128)(2,1)}), bf16[8,64,512]{2,1,0:T(8,128)(2,1)S(1)}, u32[]{:S(2)}, u32[]{:S(2)}) async-start(bf16[8,64,512]{2,1,0:T(8,128)(2,1)} %get-tuple-element.42), calls=%async_computation.1 | async-start | bytes 1048576 | tf_op jit(solution)/shard_map/all_to_all | solution.py:178
  43.1 8.2 %collective-permute-start.6 = (bf16[64,512]{1,0:T(8,128)(2,1)}, bf16[64,512]{1,0:T(8,128)(2,1)S(1)}, u32[]{:S(2)}, u32[]{:S(2)}) collective-permute-start(bf16[64,512]{1,0:T(8,128)(2,1)} %get-tuple-element.35), channel_id=1, source_target_pairs={{0,1},{1,2},{2,3},{3,0},{4,5},{5,6},{6,7},{7,4},{8,9},{9,10},{10,1... | collective-permute-start | bytes 196616 | tf_op jit(solution)/shard_map/ppermute | solution.py:182
  46.0 6.8 %collective-permute-start.7 = (bf16[64,512]{1,0:T(8,128)(2,1)}, bf16[64,512]{1,0:T(8,128)(2,1)S(1)}, u32[]{:S(2)}, u32[]{:S(2)}) collective-permute-start(bf16[64,512]{1,0:T(8,128)(2,1)} %get-tuple-element.36), channel_id=1, source_target_pairs={{0,2},{1,3},{2,0},{3,1},{4,6},{5,7},{6,4},{7,5},{8,10},{9,11},{10,... | collective-permute-start | bytes 196616 | tf_op jit(solution)/shard_map/ppermute | solution.py:182
  47.4 1.0 %copy-start.7 = (bf16[64,512]{1,0:T(8,128)(2,1)}, bf16[64,512]{1,0:T(8,128)(2,1)S(1)}, u32[]{:S(2)}) copy-start(bf16[64,512]{1,0:T(8,128)(2,1)S(1)} %collective-permute-done.11.refs_3_) | copy-start | bytes 196612
  47.4 5.8 %copy-start.3 = (bf16[64,512]{1,0:T(8,128)(2,1)S(1)}, bf16[64,512]{1,0:T(8,128)(2,1)}, u32[]{:S(2)}) copy-start(bf16[64,512]{1,0:T(8,128)(2,1)} %get-tuple-element.34) | copy-start | bytes 196612
  47.4 5.8 %collective-permute-start.8 = (bf16[64,512]{1,0:T(8,128)(2,1)}, bf16[64,512]{1,0:T(8,128)(2,1)S(1)}, u32[]{:S(2)}, u32[]{:S(2)}) collective-permute-start(bf16[64,512]{1,0:T(8,128)(2,1)} %get-tuple-element.37), channel_id=1, source_target_pairs={{0,3},{1,0},{2,1},{3,2},{4,7},{5,4},{6,5},{7,6},{8,11},{9,8},{10,9... | collective-permute-start | bytes 196616 | tf_op jit(solution)/shard_map/ppermute | solution.py:182
  48.4 0.6 copy-start.8
  49.0 0.6 copy-start.9
  53.9 4.0 %copy-start.1 = (bf16[8,64,512]{2,1,0:T(8,128)(2,1)}, bf16[8,64,512]{2,1,0:T(8,128)(2,1)S(1)}, u32[]{:S(2)}) copy-start(bf16[8,64,512]{2,1,0:T(8,128)(2,1)S(1)} %all-to-all-done.1.x_ref) | copy-start | bytes 1572868
  53.9 10.9 %all-to-all-start.2 = ((bf16[8,32,512]{2,1,0:T(8,128)(2,1)}), bf16[8,32,512]{2,1,0:T(8,128)(2,1)S(1)}, u32[]{:S(2)}, u32[]{:S(2)}) async-start(bf16[8,32,512]{2,1,0:T(8,128)(2,1)} %bitcast.5), calls=%async_computation.2 | async-start | bytes 524288 | tf_op jit(solution)/shard_map/all_to_all | solution.py:178
  64.8 0.7 %copy-start.2 = (bf16[8,32,512]{2,1,0:T(8,128)(2,1)}, bf16[8,32,512]{2,1,0:T(8,128)(2,1)S(1)}, u32[]{:S(2)}) copy-start(bf16[8,32,512]{2,1,0:T(8,128)(2,1)S(1)} %all-to-all-done.2.g_ref) | copy-start | bytes 786436

commit v4 on v3

--- a/solution.py
+++ b/solution.py
@@ -43,6 +43,7 @@
         cost_estimate=pl.CostEstimate(
             flops=int(us * 1.1e9), bytes_accessed=int(us * 3.0e6), transcendentals=0
         ),
+        compiler_params=pltpu.CompilerParams(vmem_limit_bytes=16 << 20),
         name=name,
     )(*args)
 

time: 69.1 us -> 61.3 us (0.89)
  Pallas kernels: 20.3 us -> 9.23 us
  waiting for transfers between devices: 11.9 us -> 16.9 us
  local copies, waits for them, and re-layouts: 3.2 us -> 1.68 us
    pallas_call x8, Pallas kernels: 20.3 us -> 9.23 us  [call(): pl.pallas_call(kernel, out_shape=[jax.ShapeDtypeStruct(shape, dtype) for...]
    ppermute x12, waiting for transfers between devices: 8 us -> 11.6 us  [send(): lax.ppermute(v, 'chan', [(k, (k + step) % size) for k in range(size)])]
    unnamed x32 -> x10, local copies, waits for them, and re-layouts: 3.2 us -> 1.68 us
    all_to_all x3, waiting for transfers between devices: 3.92 us -> 5.22 us  [swap(): return lax.all_to_all(v, axis, 0, 0, tiled=True)]
  transfers between devices with their start and end apart: 15 -> 15, of which waited for: 8 -> 10; matrix products, arithmetic and copies ran while one was open for 1% -> 1% of each run, Pallas kernels for 19% -> 10%
where the time goes in v4:
time: 61.3 us; the launch traced here: 60.8 us
  starting transfers between devices  31.7 us (52%)
  waiting for transfers between devices  16.9 us (28%)
  Pallas kernels  9.23 us (15%)
  local copies, waits for them, and re-layouts  1.68 us (3%)
  between operations  0.68 us (1%)
  other arithmetic  0.67 us (1%)
    ppermute x12, starting transfers between devices, send(): lax.ppermute(v, 'chan', [(k, (k + step) % size) for k in range(size)])  20 us
    all_to_all x3, starting transfers between devices, swap(): return lax.all_to_all(v, axis, 0, 0, tiled=True)  11.7 us
    ppermute x12, waiting for transfers between devices, send(): lax.ppermute(v, 'chan', [(k, (k + step) % size) for k in range(size)])  11.6 us
    pallas_call x8, Pallas kernels, call(): pl.pallas_call(kernel, out_shape=[jax.ShapeDtypeStruct(shape, dtype) for...  9.23 us
    all_to_all x3, waiting for transfers between devices, swap(): return lax.all_to_all(v, axis, 0, 0, tiled=True)  5.22 us
    unnamed x10, local copies, waits for them, and re-layouts  1.68 us
  transfers between devices with their start and end apart: 15, of which 10 were waited for; matrix products, arithmetic and copies ran while one was open for 1% of the time, Pallas kernels for 10%

profile of v4, /device:TPU:0, one launch (start us, length us, event | category | flops | bytes accessed | tf_op | source)
XLA Modules:
  0.0 60.8 jit_solution(11896279758410754115)
XLA Ops:
  0.6 0.8 %copy-done.2 = bf16[1,256,128]{2,1,0:T(8,128)(2,1)S(1)} copy-done((bf16[1,256,128]{2,1,0:T(8,128)(2,1)S(1)}, bf16[1,256,128]{2,1,0:T(8,128)(2,1)}, u32[]{:S(2)}) %copy-start.2) | copy-done | bytes 65560
  1.5 0.8 %copy-done.3 = bf16[1,64,512]{2,1,0:T(8,128)(2,1)S(1)} copy-done((bf16[1,64,512]{2,1,0:T(8,128)(2,1)S(1)}, bf16[1,64,512]{2,1,0:T(8,128)(2,1)}, u32[]{:S(2)}) %copy-start.3) | copy-done | bytes 65560
  2.3 3.1 %collective-permute-start = (bf16[64,640]{1,0:T(8,128)(2,1)S(1)}, bf16[64,640]{1,0:T(8,128)(2,1)S(1)}, u32[]{:S(2)}, u32[]{:S(2)}) collective-permute-start(bf16[64,640]{1,0:T(8,128)(2,1)S(1)} %get-tuple-element.25), channel_id=1, source_target_pairs={{0,1},{1,2},{2,3},{3,0},{4,5},{5,6},{6,7},{7,4},{8,9},{9,10},{10,1... | collective-permute-start | bytes 245768 | tf_op jit(solution)/shard_map/ppermute | solution.py:183
  5.4 2.6 %collective-permute-start.1 = (bf16[64,640]{1,0:T(8,128)(2,1)S(1)}, bf16[64,640]{1,0:T(8,128)(2,1)S(1)}, u32[]{:S(2)}, u32[]{:S(2)}) collective-permute-start(bf16[64,640]{1,0:T(8,128)(2,1)S(1)} %get-tuple-element.26), channel_id=1, source_target_pairs={{0,2},{1,3},{2,0},{3,1},{4,6},{5,7},{6,4},{7,5},{8,10},{9,11},{10,... | collective-permute-start | bytes 245768 | tf_op jit(solution)/shard_map/ppermute | solution.py:183
  8.0 1.3 %collective-permute-start.2 = (bf16[64,640]{1,0:T(8,128)(2,1)S(1)}, bf16[64,640]{1,0:T(8,128)(2,1)S(1)}, u32[]{:S(2)}, u32[]{:S(2)}) collective-permute-start(bf16[64,640]{1,0:T(8,128)(2,1)S(1)} %get-tuple-element.27), channel_id=1, source_target_pairs={{0,3},{1,0},{2,1},{3,2},{4,7},{5,4},{6,5},{7,6},{8,11},{9,8},{10,9... | collective-permute-start | bytes 245768 | tf_op jit(solution)/shard_map/ppermute | solution.py:183
  9.4 1.1 %collective-permute-done.refs_0_ = bf16[64,640]{1,0:T(8,128)(2,1)S(1)} collective-permute-done((bf16[64,640]{1,0:T(8,128)(2,1)S(1)}, bf16[64,640]{1,0:T(8,128)(2,1)S(1)}, u32[]{:S(2)}, u32[]{:S(2)}) %collective-permute-start) | collective-permute-done | bytes 81952 | tf_op jit(solution)/shard_map/ppermute | solution.py:183
  10.5 3.0 %collective-permute-done.1.refs_1_ = bf16[64,640]{1,0:T(8,128)(2,1)S(1)} collective-permute-done((bf16[64,640]{1,0:T(8,128)(2,1)S(1)}, bf16[64,640]{1,0:T(8,128)(2,1)S(1)}, u32[]{:S(2)}, u32[]{:S(2)}) %collective-permute-start.1) | collective-permute-done | bytes 81952 | tf_op jit(solution)/shard_map/ppermute | solution.py:183
  13.7 1.7 %first.1 = (bf16[8,96,512]{2,1,0:T(8,128)(2,1)}, bf16[256,512]{1,0:T(8,128)(2,1)S(1)}, bf16[64,512]{1,0:T(8,128)(2,1)S(1)}, bf16[64,512]{1,0:T(8,128)(2,1)S(1)},...) custom-call(bf16[27,64,256]{2,1,0:T(8,128)(2,1)S(1)} %bitcast.9, bf16[64,128]{1,0:T(8,128)(2,1)S(1)} %get-tuple-element.24.own, ...), custom_call_target="tpu_custom_call" | custom-call | flops 3300000000 | bytes 9000000 | tf_op jit(solution)/shard_map/first/pallas_call | solution.py:37
  15.4 3.9 %all-to-all-start = ((bf16[8,96,512]{2,1,0:T(8,128)(2,1)}), bf16[8,96,512]{2,1,0:T(8,128)(2,1)S(1)}, u32[]{:S(2)}, u32[]{:S(2)}) async-start(bf16[8,96,512]{2,1,0:T(8,128)(2,1)} %get-tuple-element.39), calls=%async_computation | async-start | bytes 1572864 | tf_op jit(solution)/shard_map/all_to_all | solution.py:179
  19.3 2.0 %collective-permute-start.3 = (bf16[64,512]{1,0:T(8,128)(2,1)S(1)}, bf16[64,512]{1,0:T(8,128)(2,1)S(1)}, u32[]{:S(2)}, u32[]{:S(2)}) collective-permute-start(bf16[64,512]{1,0:T(8,128)(2,1)S(1)} %get-tuple-element.30), channel_id=1, source_target_pairs={{0,1},{1,2},{2,3},{3,0},{4,5},{5,6},{6,7},{7,4},{8,9},{9,10},{10,1... | collective-permute-start | bytes 196616 | tf_op jit(solution)/shard_map/ppermute | solution.py:183
  21.3 1.9 %collective-permute-start.4 = (bf16[64,512]{1,0:T(8,128)(2,1)S(1)}, bf16[64,512]{1,0:T(8,128)(2,1)S(1)}, u32[]{:S(2)}, u32[]{:S(2)}) collective-permute-start(bf16[64,512]{1,0:T(8,128)(2,1)S(1)} %get-tuple-element.31), channel_id=1, source_target_pairs={{0,2},{1,3},{2,0},{3,1},{4,6},{5,7},{6,4},{7,5},{8,10},{9,11},{10,... | collective-permute-start | bytes 196616 | tf_op jit(solution)/shard_map/ppermute | solution.py:183
  23.1 0.6 collective-permute-start.5
  23.7 1.5 %spread.1.hidden_grad = f32[64,512]{1,0:T(8,128)S(1)} custom-call(bf16[27,64,256]{2,1,0:T(8,128)(2,1)S(1)} %bitcast.10, bf16[256,512]{1,0:T(8,128)(2,1)S(1)} %get-tuple-element.28.g_ref), custom_call_target="tpu_custom_call" | custom-call | flops 3740000000 | bytes 10200000 | tf_op jit(solution)/shard_map/spread/pallas_call | solution.py:37
  25.3 0.8 %collective-permute-done.3.refs_1_ = bf16[64,512]{1,0:T(8,128)(2,1)S(1)} collective-permute-done((bf16[64,512]{1,0:T(8,128)(2,1)S(1)}, bf16[64,512]{1,0:T(8,128)(2,1)S(1)}, u32[]{:S(2)}, u32[]{:S(2)}) %collective-permute-start.3) | collective-permute-done | bytes 65568 | tf_op jit(solution)/shard_map/ppermute | solution.py:183
  26.1 2.4 %collective-permute-done.4.refs_2_ = bf16[64,512]{1,0:T(8,128)(2,1)S(1)} collective-permute-done((bf16[64,512]{1,0:T(8,128)(2,1)S(1)}, bf16[64,512]{1,0:T(8,128)(2,1)S(1)}, u32[]{:S(2)}, u32[]{:S(2)}) %collective-permute-start.4) | collective-permute-done | bytes 65568 | tf_op jit(solution)/shard_map/ppermute | solution.py:183
  28.7 0.9 %middle.1 = (bf16[64,512]{1,0:T(8,128)(2,1)S(1)}, bf16[8,64,512]{2,1,0:T(8,128)(2,1)}, bf16[64,512]{1,0:T(8,128)(2,1)S(1)}) custom-call(f32[64,512]{1,0:T(8,128)S(1)} %spread.1.hidden_grad, bf16[64,512]{1,0:T(8,128)(2,1)S(1)} %get-tuple-element.29.refs_0_, bf16[64,512]{1,0:T(8,128)(2,1)S(1)} %collective-permute-done.3.refs_1_, ...), custom_call_target="tpu_custom_call" | custom-call | flops 2200000000 | bytes 6000000 | tf_op jit(solution)/shard_map/middle/pallas_call | solution.py:37
  29.6 2.4 %collective-permute-start.11 = (bf16[64,512]{1,0:T(8,128)(2,1)S(1)}, bf16[64,512]{1,0:T(8,128)(2,1)S(1)}, u32[]{:S(2)}, u32[]{:S(2)}) collective-permute-start(bf16[64,512]{1,0:T(8,128)(2,1)S(1)} %get-tuple-element.41.refs_0_), channel_id=1, source_target_pairs={{0,3},{1,0},{2,1},{3,2},{4,7},{5,4},{6,5},{7,6},{8,11},{9,8},{10,9... | collective-permute-start | bytes 196616 | tf_op jit(solution)/shard_map/ppermute | solution.py:183
  32.0 0.8 %collective-permute-start.10 = (bf16[64,512]{1,0:T(8,128)(2,1)S(1)}, bf16[64,512]{1,0:T(8,128)(2,1)S(1)}, u32[]{:S(2)}, u32[]{:S(2)}) collective-permute-start(bf16[64,512]{1,0:T(8,128)(2,1)S(1)} %get-tuple-element.41.refs_0_), channel_id=1, source_target_pairs={{0,2},{1,3},{2,0},{3,1},{4,6},{5,7},{6,4},{7,5},{8,10},{9,11},{10,... | collective-permute-start | bytes 196616 | tf_op jit(solution)/shard_map/ppermute | solution.py:183
  32.8 3.8 %all-to-all-start.1 = ((bf16[8,64,512]{2,1,0:T(8,128)(2,1)}), bf16[8,64,512]{2,1,0:T(8,128)(2,1)S(1)}, u32[]{:S(2)}, u32[]{:S(2)}) async-start(bf16[8,64,512]{2,1,0:T(8,128)(2,1)} %get-tuple-element.42), calls=%async_computation.1 | async-start | bytes 1048576 | tf_op jit(solution)/shard_map/all_to_all | solution.py:179
  36.6 0.9 %second.1 = (bf16[64,512]{1,0:T(8,128)(2,1)S(1)}, bf16[64,512]{1,0:T(8,128)(2,1)S(1)}, bf16[64,512]{1,0:T(8,128)(2,1)S(1)}, bf16[64,512]{1,0:T(8,128)(2,1)S(1)}) custom-call(bf16[27,64,256]{2,1,0:T(8,128)(2,1)S(1)} %bitcast.11, bf16[64,512]{1,0:T(8,128)(2,1)S(1)} %get-tuple-element.33.v_ref), custom_call_target="tpu_custom_call" | custom-call | flops 3080000000 | bytes 8400000 | tf_op jit(solution)/shard_map/second/pallas_call | solution.py:37
  37.5 3.0 %collective-permute-start.6 = (bf16[64,512]{1,0:T(8,128)(2,1)S(1)}, bf16[64,512]{1,0:T(8,128)(2,1)S(1)}, u32[]{:S(2)}, u32[]{:S(2)}) collective-permute-start(bf16[64,512]{1,0:T(8,128)(2,1)S(1)} %get-tuple-element.35), channel_id=1, source_target_pairs={{0,1},{1,2},{2,3},{3,0},{4,5},{5,6},{6,7},{7,4},{8,9},{9,10},{10,1... | collective-permute-start | bytes 196616 | tf_op jit(solution)/shard_map/ppermute | solution.py:183
  40.5 1.4 %collective-permute-start.7 = (bf16[64,512]{1,0:T(8,128)(2,1)S(1)}, bf16[64,512]{1,0:T(8,128)(2,1)S(1)}, u32[]{:S(2)}, u32[]{:S(2)}) collective-permute-start(bf16[64,512]{1,0:T(8,128)(2,1)S(1)} %get-tuple-element.36), channel_id=1, source_target_pairs={{0,2},{1,3},{2,0},{3,1},{4,6},{5,7},{6,4},{7,5},{8,10},{9,11},{10,... | collective-permute-start | bytes 196616 | tf_op jit(solution)/shard_map/ppermute | solution.py:183
  41.9 1.0 %collective-permute-start.8 = (bf16[64,512]{1,0:T(8,128)(2,1)S(1)}, bf16[64,512]{1,0:T(8,128)(2,1)S(1)}, u32[]{:S(2)}, u32[]{:S(2)}) collective-permute-start(bf16[64,512]{1,0:T(8,128)(2,1)S(1)} %get-tuple-element.37), channel_id=1, source_target_pairs={{0,3},{1,0},{2,1},{3,2},{4,7},{5,4},{6,5},{7,6},{8,11},{9,8},{10,9... | collective-permute-start | bytes 196616 | tf_op jit(solution)/shard_map/ppermute | solution.py:183
  42.9 0.7 %join.1 = bf16[256,512]{1,0:T(8,128)(2,1)} custom-call(bf16[64,512]{1,0:T(8,128)(2,1)S(1)} %get-tuple-element.41.refs_0_, bf16[64,512]{1,0:T(8,128)(2,1)S(1)} %collective-permute-done.9.refs_1_, bf16[64,512]{1,0:T(8,128)(2,1)S(1)} %collective-permute-done.10.refs_2_, bf16[64,512]{1,0:T(8,128)(2,1)S(1)} %collective-permute-done.11.refs_3_), custom_call_target="tpu_custom_call" | custom-call | flops 1100000000 | bytes 3000000 | tf_op jit(solution)/shard_map/join/pallas_call | solution.py:37
  43.7 0.6 collective-permute-done.6
  44.2 2.8 %collective-permute-done.7 = bf16[64,512]{1,0:T(8,128)(2,1)S(1)} collective-permute-done((bf16[64,512]{1,0:T(8,128)(2,1)S(1)}, bf16[64,512]{1,0:T(8,128)(2,1)S(1)}, u32[]{:S(2)}, u32[]{:S(2)}) %collective-permute-start.7) | collective-permute-done | bytes 65568 | tf_op jit(solution)/shard_map/ppermute | solution.py:183
  47.0 0.5 collective-permute-done.8
  47.5 0.7 %fusion = bf16[1,64,512]{2,1,0:T(8,128)(2,1)} fusion(bf16[64,512]{1,0:T(8,128)(2,1)S(1)} %collective-permute-done.8, bf16[64,512]{1,0:T(8,128)(2,1)S(1)} %collective-permute-done.7, bf16[64,512]{1,0:T(8,128)(2,1)S(1)} %collective-permute-done.6, bf16[64,512]{1,0:T(8,128)(2,1)S(1)} %get-tuple-element.34), kind=kLoop, calls=%fused_computation.1 | loop fusion | flops 262144 | bytes 327680 | tf_op jit(solution)/shard_map/broadcast_in_dim | solution.py:243
  48.2 4.0 %all-to-all-start.2 = ((bf16[8,32,512]{2,1,0:T(8,128)(2,1)}), bf16[8,32,512]{2,1,0:T(8,128)(2,1)S(1)}, u32[]{:S(2)}, u32[]{:S(2)}) async-start(bf16[8,32,512]{2,1,0:T(8,128)(2,1)} %bitcast.5), calls=%async_computation.2 | async-start | bytes 524288 | tf_op jit(solution)/shard_map/all_to_all | solution.py:179
  52.2 1.7 %grad.3 = f32[27,32,64]{2,1,0:T(8,128)} custom-call(bf16[8,64,512]{2,1,0:T(8,128)(2,1)S(1)} %all-to-all-done.1.x_ref, bf16[8,96,512]{2,1,0:T(8,128)(2,1)S(1)} %all-to-all-done.x_ref.g_ref), custom_call_target="tpu_custom_call" | custom-call | flops 3300000000 | bytes 9000000 | tf_op jit(solution)/shard_map/grad/pallas_call | solution.py:37
  53.9 5.2 %all-to-all-done.2.g_ref = bf16[8,32,512]{2,1,0:T(8,128)(2,1)S(1)} async-done(((bf16[8,32,512]{2,1,0:T(8,128)(2,1)}), bf16[8,32,512]{2,1,0:T(8,128)(2,1)S(1)}, u32[]{:S(2)}, u32[]{:S(2)}) %all-to-all-start.2) | async-done | bytes 262176 | tf_op jit(solution)/shard_map/all_to_all | solution.py:179
  59.1 1.7 %grad.2 = f32[27,32,64]{2,1,0:T(8,128)} custom-call(bf16[8,96,512]{2,1,0:T(8,128)(2,1)S(1)} %all-to-all-done.x_ref.g_ref, bf16[8,32,512]{2,1,0:T(8,128)(2,1)S(1)} %all-to-all-done.2.g_ref), custom_call_target="tpu_custom_call" | custom-call | flops 3300000000 | bytes 9000000 | tf_op jit(solution)/shard_map/grad/pallas_call | solution.py:37
  (17 shorter events, 0.5 us)
Async XLA Ops:
  0.6 0.8 %copy-start.2 = (bf16[1,256,128]{2,1,0:T(8,128)(2,1)S(1)}, bf16[1,256,128]{2,1,0:T(8,128)(2,1)}, u32[]{:S(2)}) copy-start(bf16[1,256,128]{2,1,0:T(8,128)(2,1)} %param.4) | copy-start | bytes 196612
  1.5 0.8 %copy-start.3 = (bf16[1,64,512]{2,1,0:T(8,128)(2,1)S(1)}, bf16[1,64,512]{2,1,0:T(8,128)(2,1)}, u32[]{:S(2)}) copy-start(bf16[1,64,512]{2,1,0:T(8,128)(2,1)} %param.7) | copy-start | bytes 196612
  2.3 11.4 %copy-start = (bf16[64,27,256]{2,0,1:T(8,128)(2,1)S(1)}, bf16[64,27,256]{2,0,1:T(8,128)(2,1)}, u32[]{:S(2)}) copy-start(bf16[64,27,256]{2,0,1:T(8,128)(2,1)} %param.5) | copy-start | bytes 2654212
  2.3 11.4 %copy-start.4 = (bf16[1,64,512]{2,1,0:T(8,128)(2,1)S(1)}, bf16[1,64,512]{2,1,0:T(8,128)(2,1)}, u32[]{:S(2)}) copy-start(bf16[1,64,512]{2,1,0:T(8,128)(2,1)} %param.7) | copy-start | bytes 196612
  2.3 8.1 %collective-permute-start = (bf16[64,640]{1,0:T(8,128)(2,1)S(1)}, bf16[64,640]{1,0:T(8,128)(2,1)S(1)}, u32[]{:S(2)}, u32[]{:S(2)}) collective-permute-start(bf16[64,640]{1,0:T(8,128)(2,1)S(1)} %get-tuple-element.25), channel_id=1, source_target_pairs={{0,1},{1,2},{2,3},{3,0},{4,5},{5,6},{6,7},{7,4},{8,9},{9,10},{10,1... | collective-permute-start | bytes 245768 | tf_op jit(solution)/shard_map/ppermute | solution.py:183
  5.4 8.1 %collective-permute-start.1 = (bf16[64,640]{1,0:T(8,128)(2,1)S(1)}, bf16[64,640]{1,0:T(8,128)(2,1)S(1)}, u32[]{:S(2)}, u32[]{:S(2)}) collective-permute-start(bf16[64,640]{1,0:T(8,128)(2,1)S(1)} %get-tuple-element.26), channel_id=1, source_target_pairs={{0,2},{1,3},{2,0},{3,1},{4,6},{5,7},{6,4},{7,5},{8,10},{9,11},{10,... | collective-permute-start | bytes 245768 | tf_op jit(solution)/shard_map/ppermute | solution.py:183
  8.0 5.7 %collective-permute-start.2 = (bf16[64,640]{1,0:T(8,128)(2,1)S(1)}, bf16[64,640]{1,0:T(8,128)(2,1)S(1)}, u32[]{:S(2)}, u32[]{:S(2)}) collective-permute-start(bf16[64,640]{1,0:T(8,128)(2,1)S(1)} %get-tuple-element.27), channel_id=1, source_target_pairs={{0,3},{1,0},{2,1},{3,2},{4,7},{5,4},{6,5},{7,6},{8,11},{9,8},{10,9... | collective-permute-start | bytes 245768 | tf_op jit(solution)/shard_map/ppermute | solution.py:183
  15.4 8.3 %copy-start.1 = (bf16[64,27,256]{2,0,1:T(8,128)(2,1)S(1)}, bf16[64,27,256]{2,0,1:T(8,128)(2,1)}, u32[]{:S(2)}) copy-start(bf16[64,27,256]{2,0,1:T(8,128)(2,1)} %param.6) | copy-start | bytes 2654212
  15.4 17.3 %all-to-all-start = ((bf16[8,96,512]{2,1,0:T(8,128)(2,1)}), bf16[8,96,512]{2,1,0:T(8,128)(2,1)S(1)}, u32[]{:S(2)}, u32[]{:S(2)}) async-start(bf16[8,96,512]{2,1,0:T(8,128)(2,1)} %get-tuple-element.39), calls=%async_computation | async-start | bytes 1572864 | tf_op jit(solution)/shard_map/all_to_all | solution.py:179
  19.3 6.8 %collective-permute-start.3 = (bf16[64,512]{1,0:T(8,128)(2,1)S(1)}, bf16[64,512]{1,0:T(8,128)(2,1)S(1)}, u32[]{:S(2)}, u32[]{:S(2)}) collective-permute-start(bf16[64,512]{1,0:T(8,128)(2,1)S(1)} %get-tuple-element.30), channel_id=1, source_target_pairs={{0,1},{1,2},{2,3},{3,0},{4,5},{5,6},{6,7},{7,4},{8,9},{9,10},{10,1... | collective-permute-start | bytes 196616 | tf_op jit(solution)/shard_map/ppermute | solution.py:183
  21.3 7.2 %collective-permute-start.4 = (bf16[64,512]{1,0:T(8,128)(2,1)S(1)}, bf16[64,512]{1,0:T(8,128)(2,1)S(1)}, u32[]{:S(2)}, u32[]{:S(2)}) collective-permute-start(bf16[64,512]{1,0:T(8,128)(2,1)S(1)} %get-tuple-element.31), channel_id=1, source_target_pairs={{0,2},{1,3},{2,0},{3,1},{4,6},{5,7},{6,4},{7,5},{8,10},{9,11},{10,... | collective-permute-start | bytes 196616 | tf_op jit(solution)/shard_map/ppermute | solution.py:183
  23.1 5.6 %collective-permute-start.5 = (bf16[64,512]{1,0:T(8,128)(2,1)S(1)}, bf16[64,512]{1,0:T(8,128)(2,1)S(1)}, u32[]{:S(2)}, u32[]{:S(2)}) collective-permute-start(bf16[64,512]{1,0:T(8,128)(2,1)S(1)} %get-tuple-element.32), channel_id=1, source_target_pairs={{0,3},{1,0},{2,1},{3,2},{4,7},{5,4},{6,5},{7,6},{8,11},{9,8},{10,9... | collective-permute-start | bytes 196616 | tf_op jit(solution)/shard_map/ppermute | solution.py:183
  29.6 12.3 %collective-permute-start.11 = (bf16[64,512]{1,0:T(8,128)(2,1)S(1)}, bf16[64,512]{1,0:T(8,128)(2,1)S(1)}, u32[]{:S(2)}, u32[]{:S(2)}) collective-permute-start(bf16[64,512]{1,0:T(8,128)(2,1)S(1)} %get-tuple-element.41.refs_0_), channel_id=1, source_target_pairs={{0,3},{1,0},{2,1},{3,2},{4,7},{5,4},{6,5},{7,6},{8,11},{9,8},{10,9... | collective-permute-start | bytes 196616 | tf_op jit(solution)/shard_map/ppermute | solution.py:183
  32.0 10.9 %collective-permute-start.10 = (bf16[64,512]{1,0:T(8,128)(2,1)S(1)}, bf16[64,512]{1,0:T(8,128)(2,1)S(1)}, u32[]{:S(2)}, u32[]{:S(2)}) collective-permute-start(bf16[64,512]{1,0:T(8,128)(2,1)S(1)} %get-tuple-element.41.refs_0_), channel_id=1, source_target_pairs={{0,2},{1,3},{2,0},{3,1},{4,6},{5,7},{6,4},{7,5},{8,10},{9,11},{10,... | collective-permute-start | bytes 196616 | tf_op jit(solution)/shard_map/ppermute | solution.py:183
  32.8 10.2 %collective-permute-start.9 = (bf16[64,512]{1,0:T(8,128)(2,1)S(1)}, bf16[64,512]{1,0:T(8,128)(2,1)S(1)}, u32[]{:S(2)}, u32[]{:S(2)}) collective-permute-start(bf16[64,512]{1,0:T(8,128)(2,1)S(1)} %get-tuple-element.41.refs_0_), channel_id=1, source_target_pairs={{0,1},{1,2},{2,3},{3,0},{4,5},{5,6},{6,7},{7,4},{8,9},{9,10},{10,1... | collective-permute-start | bytes 196616 | tf_op jit(solution)/shard_map/ppermute | solution.py:183
  32.8 15.4 %all-to-all-start.1 = ((bf16[8,64,512]{2,1,0:T(8,128)(2,1)}), bf16[8,64,512]{2,1,0:T(8,128)(2,1)S(1)}, u32[]{:S(2)}, u32[]{:S(2)}) async-start(bf16[8,64,512]{2,1,0:T(8,128)(2,1)} %get-tuple-element.42), calls=%async_computation.1 | async-start | bytes 1048576 | tf_op jit(solution)/shard_map/all_to_all | solution.py:179
  37.5 6.7 %collective-permute-start.6 = (bf16[64,512]{1,0:T(8,128)(2,1)S(1)}, bf16[64,512]{1,0:T(8,128)(2,1)S(1)}, u32[]{:S(2)}, u32[]{:S(2)}) collective-permute-start(bf16[64,512]{1,0:T(8,128)(2,1)S(1)} %get-tuple-element.35), channel_id=1, source_target_pairs={{0,1},{1,2},{2,3},{3,0},{4,5},{5,6},{6,7},{7,4},{8,9},{9,10},{10,1... | collective-permute-start | bytes 196616 | tf_op jit(solution)/shard_map/ppermute | solution.py:183
  40.5 6.6 %collective-permute-start.7 = (bf16[64,512]{1,0:T(8,128)(2,1)S(1)}, bf16[64,512]{1,0:T(8,128)(2,1)S(1)}, u32[]{:S(2)}, u32[]{:S(2)}) collective-permute-start(bf16[64,512]{1,0:T(8,128)(2,1)S(1)} %get-tuple-element.36), channel_id=1, source_target_pairs={{0,2},{1,3},{2,0},{3,1},{4,6},{5,7},{6,4},{7,5},{8,10},{9,11},{10,... | collective-permute-start | bytes 196616 | tf_op jit(solution)/shard_map/ppermute | solution.py:183
  41.9 5.6 %collective-permute-start.8 = (bf16[64,512]{1,0:T(8,128)(2,1)S(1)}, bf16[64,512]{1,0:T(8,128)(2,1)S(1)}, u32[]{:S(2)}, u32[]{:S(2)}) collective-permute-start(bf16[64,512]{1,0:T(8,128)(2,1)S(1)} %get-tuple-element.37), channel_id=1, source_target_pairs={{0,3},{1,0},{2,1},{3,2},{4,7},{5,4},{6,5},{7,6},{8,11},{9,8},{10,9... | collective-permute-start | bytes 196616 | tf_op jit(solution)/shard_map/ppermute | solution.py:183
  48.2 10.9 %all-to-all-start.2 = ((bf16[8,32,512]{2,1,0:T(8,128)(2,1)}), bf16[8,32,512]{2,1,0:T(8,128)(2,1)S(1)}, u32[]{:S(2)}, u32[]{:S(2)}) async-start(bf16[8,32,512]{2,1,0:T(8,128)(2,1)} %bitcast.5), calls=%async_computation.2 | async-start | bytes 524288 | tf_op jit(solution)/shard_map/all_to_all | solution.py:179

commit v5 on v4

--- a/solution.py
+++ b/solution.py
@@ -136,27 +136,28 @@
     map_grad_ref[...] = (hidden_grad[...] * gate * (1.0 + first_map * (1.0 - gate))).astype(BF16)
 
 
-def grad_kernel(at, x_ref, g_ref, o_ref, left, right):
-    count, outs, _ = g_ref.shape
-    ins = o_ref.shape[2]
-    for n in range(count):
+def grad_sum(pairs, o_ref, left, right):
+    for n, (x, g) in enumerate(pairs):
         cells = pl.ds(n * CELLS, CELLS)
-        x = x_ref[n, :ins, :]
+        ins, outs = x.shape[0], g.shape[0]
         for e in range(3):
             right[e * ins : (e + 1) * ins, cells] = moved(x, (0, 0, e - 1))
-        g = g_ref[n, at:, :]
-        rows = g.shape[0]
         for a in range(3):
             for b in range(3):
-                row = (a * 3 + b) * rows
-                left[row : row + rows, cells] = moved(g, (1 - a, 1 - b, 0))
+                row = (a * 3 + b) * outs
+                left[row : row + outs, cells] = moved(g, (1 - a, 1 - b, 0))
     acc = lax.dot_general(
         left[...], right[...], (((1,), (1,)), ((), ())), preferred_element_type=F32
     )
-    rows = o_ref.shape[1]
     for ab in range(9):
         for e in range(3):
-            o_ref[ab * 3 + e] = acc[ab * rows : (ab + 1) * rows, e * ins : (e + 1) * ins]
+            o_ref[ab * 3 + e] = acc[ab * outs : (ab + 1) * outs, e * ins : (e + 1) * ins]
+
+
+def grad_kernel(at, x_ref, g_ref, o_ref, left, right):
+    ins = o_ref.shape[2]
+    pairs = [(x_ref[n, :ins, :], g_ref[n, at:, :]) for n in range(x_ref.shape[0])]
+    grad_sum(pairs, o_ref, left, right)
 
 
 def grad(x, g, ins, at):
@@ -187,7 +188,7 @@
     return [parts[0]] + [send(parts[j], j, size) for j in range(1, size)]
 
 
-def body(samples, chans, snapshots, first_weight, second_weight, cotangent):
+def plain_body(samples, chans, snapshots, first_weight, second_weight, cotangent):
     ins = first_weight.shape[0]
     full = snapshots.shape[1]
     outs = full // samples
@@ -246,6 +247,174 @@
     )
 
 
+def half(rows):
+    return pl.ds(pl.multiple_of((lax.axis_index("sample") & 1) * rows, rows), rows)
+
+
+def far(step, rows):
+    chip = (lax.axis_index("sample") >> 1) ^ step
+    return pl.ds(pl.multiple_of(chip * rows, rows), rows)
+
+
+def cells_kernel(chans, v_ref, *outs):
+    for j, out in enumerate(outs):
+        out[...] = v_ref[block(j, chans, out.shape[0]), :]
+
+
+def input_kernel(chans, w_ref, *refs):
+    parts, (x, *outs), scratch = refs[:chans], refs[chans:-2], refs[-2:]
+    for j, part in enumerate(parts):
+        x[:, block(chans - j, chans, part.shape[1])] = part[...]
+    conv_part(chans, w_ref, x[...], outs, *scratch)
+
+
+def pieces_kernel(hidden, x, full, out):
+    rows = x.shape[0]
+    for chip in range(out.shape[0]):
+        out[chip, :rows, :] = hidden[...]
+        out[chip, rows : 2 * rows, :] = x[...]
+        out[chip, 2 * rows :, :] = full[chip * rows : (chip + 1) * rows, :]
+
+
+def gate_kernel(chans, hidden_grad, *refs):
+    parts, (hidden_ref, keep, give, both) = refs[:chans], refs[chans:]
+    total = parts[0][...].astype(F32)
+    for j in range(1, chans):
+        total = total + parts[j][...].astype(F32)
+    first_map = total.astype(BF16).astype(F32)
+    gate = 1.0 / (1.0 + jnp.exp(-first_map))
+    hidden_ref[...] = (first_map * gate).astype(BF16)
+    both[...] = (hidden_grad[...] * gate * (1.0 + first_map * (1.0 - gate))).astype(BF16)
+    rows = keep.shape[0]
+    keep[...] = both[half(rows), :]
+    other = pl.multiple_of((1 - (lax.axis_index("sample") & 1)) * rows, rows)
+    give[...] = both[pl.ds(other, rows), :]
+
+
+def output_kernel(chans, w_ref, v_ref, top, bottom, *refs):
+    outs, scratch = refs[:chans], refs[chans:]
+    rows, half_rows = v_ref.shape[0], top.shape[0]
+    conv_part(chans, w_ref, v_ref[...], [out.at[:rows] for out in outs], *scratch)
+    for out in outs:
+        out[rows : rows + half_rows, :] = top[...]
+        out[rows + half_rows :, :] = bottom[...]
+
+
+def route_kernel(chans, *refs):
+    parts, outs, full = refs[:chans], refs[chans:-1], refs[-1]
+    rows = outs[0].shape[0]
+    join_kernel(chans, *[part.at[rows:] for part in parts], full)
+    for step, out in enumerate(outs):
+        out[...] = full[far(step, rows), :]
+
+
+def total_kernel(*refs):
+    *parts, out = refs
+    rows = out.shape[0]
+    total = parts[0][:rows, :].astype(F32)
+    for part in parts[1:]:
+        total = total + part[:rows, :].astype(F32)
+    out[...] = total.astype(BF16)
+
+
+def second_grad_kernel(mine, other, *rest):
+    rows, ins = rest[0].shape[1:]
+    start = pl.multiple_of(2 * ins + (lax.axis_index("sample") & 1) * rows, rows)
+    pairs = []
+    for chip in range(mine.shape[0]):
+        for v in (mine, other):
+            pairs.append((v[chip, :ins, :], v[chip, pl.ds(start, rows), :]))
+    grad_sum(pairs, *rest)
+
+
+def first_grad_kernel(mine, other, *refs):
+    maps, rest = refs[:-3], refs[-3:]
+    rows, ins = rest[0].shape[1:]
+    pairs = []
+    for step, g in enumerate(maps):
+        chip = (lax.axis_index("sample") >> 1) ^ step
+        for core, v in enumerate((mine, other)):
+            at = core * rows
+            pairs.append((v[chip, ins : 2 * ins, :], g[at : at + rows, :]))
+    grad_sum(pairs, *rest)
+
+
+def body(samples, chans, snapshots, first_weight, second_weight, cotangent):
+    ins = first_weight.shape[0]
+    full = snapshots.shape[1]
+    outs = full // samples
+    chips = samples // 2
+    run = lambda kernel: functools.partial(kernel, chans)
+    first_w = first_weight.transpose(1, 0, 2)
+    second_w = second_weight.transpose(1, 0, 2)
+    patches = [pltpu.VMEM((27 * ins, CELLS), BF16), pltpu.VMEM((full, CELLS), BF16)]
+    piece = ((ins, CELLS), BF16)
+    hop = lambda v, step: lax.ppermute(v, "sample", [(s, s ^ step) for s in range(samples)])
+
+    def chip_hops(parts):
+        return [parts[0]] + [hop(parts[d], 2 * d) for d in range(1, chips)]
+
+    cells = call(
+        run(cells_kernel), [((ins, CELLS // chans), BF16)] * chans, [snapshots[0]], (), "cells", 0.5
+    )
+    cells = exchange(cells, chans)
+    cots = exchange([cotangent[0]] * chans, chans)
+    x, *parts = call(
+        run(input_kernel), [piece] * (chans + 1), [first_w] + cells, patches, "first", 1.0
+    )
+    parts = exchange(parts, chans)
+    full_cot = call(run(join_kernel), [((full, CELLS), BF16)], cots, (), "join", 0.5)[0]
+    hidden_grad = call(
+        spread_kernel, [((ins, CELLS), F32)], [second_w, full_cot], (), "spread", 1.5
+    )[0]
+    hidden, keep, give = call(
+        run(gate_kernel),
+        [piece, ((outs, CELLS), BF16), ((outs, CELLS), BF16)],
+        [hidden_grad] + parts,
+        [pltpu.VMEM((ins, CELLS), BF16)],
+        "gate",
+        0.9,
+    )
+    parts = call(
+        run(output_kernel),
+        [((2 * ins, CELLS), BF16)] * chans,
+        [second_w, hidden, keep, hop(give, 1)],
+        patches,
+        "second",
+        1.0,
+    )
+    hidden, *parts = lax.optimization_barrier((hidden, *parts))
+    parts = exchange(parts, chans)
+    pieces = call(
+        pieces_kernel,
+        [((chips, 3 * ins, CELLS), BF16)],
+        [hidden, x, full_cot],
+        (),
+        "pieces",
+        0.8,
+    )[0]
+    cores = [list(range(core, samples, 2)) for core in (0, 1)]
+    pieces = lax.all_to_all(pieces, "sample", 0, 0, axis_index_groups=cores, tiled=True)
+    routed = call(run(route_kernel), [piece] * chips, parts, patches[1:], "route", 0.6)
+    pieces, *routed = lax.optimization_barrier((pieces, *routed))
+    map_grads = chip_hops(routed)
+    pieces = [pieces, hop(pieces, 1)]
+    scratch = [
+        pltpu.VMEM((9 * outs, samples * CELLS), BF16),
+        pltpu.VMEM((3 * ins, samples * CELLS), BF16),
+    ]
+    out = [((27, outs, ins), F32)]
+    second_grad = call(second_grad_kernel, out, pieces, scratch, "grad", 1.7)[0]
+    second_grad, *parts = lax.optimization_barrier((second_grad, *parts))
+    second_out = call(total_kernel, [piece], parts, (), "total", 0.5)[0]
+    first_grad = call(first_grad_kernel, out, pieces + map_grads, scratch, "grad", 1.7)[0]
+    return (
+        second_out[None],
+        first_grad.transpose(2, 0, 1),
+        second_grad.transpose(2, 0, 1),
+    )
+
+
 def solution(mesh):
     placed = (
         P("sample", None, "chan"),
@@ -253,8 +422,10 @@
         P("chan", None, None),
         P("sample", "chan", None),
     )
+    samples, chans = mesh.shape["sample"], mesh.shape["chan"]
+    square = samples == 2 * chans and chans in (2, 4)
     return jax.shard_map(
-        functools.partial(body, mesh.shape["sample"], mesh.shape["chan"]),
+        functools.partial(body if square else plain_body, samples, chans),
         mesh=mesh,
         in_specs=placed,
         out_specs=(P("sample", "chan", None), P("chan", None, "sample"), P("chan", None, "sample")),

time: 61.3 us -> 52.5 us (0.86)
  starting transfers between devices: 31.7 us -> 27.1 us
  waiting for transfers between devices: 16.9 us -> 14.8 us
  local copies, waits for them, and re-layouts: 1.68 us -> 0.84 us
  Pallas kernels: 9.23 us -> 8.53 us
  other arithmetic: 0.67 us -> 0 us
    all_to_all x3 -> x1, starting transfers between devices: 11.7 us -> 3.72 us  [body(): lax.all_to_all(pieces, 'sample', 0, 0, axis_index_groups=cores, tiled=True)]
    all_to_all x3 -> x1, waiting for transfers between devices: 5.22 us -> 0.01 us  [body(): lax.all_to_all(pieces, 'sample', 0, 0, axis_index_groups=cores, tiled=True)]
    ppermute x0 -> x5, starting transfers between devices: none -> 3.7 us  [body(): lax.ppermute(v, 'sample', [(s, s ^ step) for s in range(samples)])]
    ppermute x0 -> x5, waiting for transfers between devices: none -> 3.61 us  [body(): lax.ppermute(v, 'sample', [(s, s ^ step) for s in range(samples)])]
    unnamed x10 -> x8, local copies, waits for them, and re-layouts: 1.68 us -> 0.84 us
    pallas_call x8 -> x11, Pallas kernels: 9.23 us -> 8.53 us  [call(): pl.pallas_call(kernel, out_shape=[jax.ShapeDtypeStruct(shape, dtype) for...]
    broadcast_in_dim x1 -> x0, other arithmetic: 0.67 us -> none  [body(): second_out[None]]
  transfers between devices with their start and end apart: 15 -> 18, of which waited for: 10 -> 5; matrix products, arithmetic and copies ran while one was open for 1% -> 0% of each run, Pallas kernels for 10% -> 9%
where the time goes in v5:
time: 52.5 us; the launch traced here: 52 us
  starting transfers between devices  27.1 us (52%)
  waiting for transfers between devices  14.8 us (28%)
  Pallas kernels  8.53 us (16%)
  local copies, waits for them, and re-layouts  0.84 us (2%)
  between operations  0.74 us (1%)
    ppermute x12, starting transfers between devices, send(): lax.ppermute(v, 'chan', [(k, (k + step) % size) for k in range(size)])  19.7 us
    ppermute x12, waiting for transfers between devices, send(): lax.ppermute(v, 'chan', [(k, (k + step) % size) for k in range(size)])  11.2 us
    pallas_call x11, Pallas kernels, call(): pl.pallas_call(kernel, out_shape=[jax.ShapeDtypeStruct(shape, dtype) for...  8.53 us
    all_to_all x1, starting transfers between devices, body(): lax.all_to_all(pieces, 'sample', 0, 0, axis_index_groups=cores, tiled=True)  3.72 us
    ppermute x5, starting transfers between devices, body(): lax.ppermute(v, 'sample', [(s, s ^ step) for s in range(samples)])  3.7 us
    ppermute x5, waiting for transfers between devices, body(): lax.ppermute(v, 'sample', [(s, s ^ step) for s in range(samples)])  3.61 us
  transfers between devices with their start and end apart: 18, of which 5 were waited for; matrix products, arithmetic and copies ran while one was open for 0% of the time, Pallas kernels for 9%

profile of v5, /device:TPU:0, one launch (start us, length us, event | category | flops | bytes accessed | tf_op | source)
XLA Modules:
  0.0 52.0 jit_solution(914414224862903506)
XLA Ops:
  0.6 0.8 %copy-done.2 = bf16[1,256,128]{2,1,0:T(8,128)(2,1)S(1)} copy-done((bf16[1,256,128]{2,1,0:T(8,128)(2,1)S(1)}, bf16[1,256,128]{2,1,0:T(8,128)(2,1)}, u32[]{:S(2)}) %copy-start.2) | copy-done | bytes 65560
  1.5 3.1 %collective-permute-start.3 = (bf16[64,128]{1,0:T(8,128)(2,1)S(1)}, bf16[64,128]{1,0:T(8,128)(2,1)S(1)}, u32[]{:S(2)}, u32[]{:S(2)}) collective-permute-start(bf16[64,128]{1,0:T(8,128)(2,1)S(1)} %get-tuple-element.39), channel_id=1, source_target_pairs={{0,1},{1,2},{2,3},{3,0},{4,5},{5,6},{6,7},{7,4},{8,9},{9,10},{10,1... | collective-permute-start | bytes 49160 | tf_op jit(solution)/shard_map/ppermute | solution.py:184
  4.6 2.6 %collective-permute-start.4 = (bf16[64,128]{1,0:T(8,128)(2,1)S(1)}, bf16[64,128]{1,0:T(8,128)(2,1)S(1)}, u32[]{:S(2)}, u32[]{:S(2)}) collective-permute-start(bf16[64,128]{1,0:T(8,128)(2,1)S(1)} %get-tuple-element.40), channel_id=1, source_target_pairs={{0,2},{1,3},{2,0},{3,1},{4,6},{5,7},{6,4},{7,5},{8,10},{9,11},{10,... | collective-permute-start | bytes 49160 | tf_op jit(solution)/shard_map/ppermute | solution.py:184
  7.2 1.3 %collective-permute-start.5 = (bf16[64,128]{1,0:T(8,128)(2,1)S(1)}, bf16[64,128]{1,0:T(8,128)(2,1)S(1)}, u32[]{:S(2)}, u32[]{:S(2)}) collective-permute-start(bf16[64,128]{1,0:T(8,128)(2,1)S(1)} %get-tuple-element.41), channel_id=1, source_target_pairs={{0,3},{1,0},{2,1},{3,2},{4,7},{5,4},{6,5},{7,6},{8,11},{9,8},{10,9... | collective-permute-start | bytes 49160 | tf_op jit(solution)/shard_map/ppermute | solution.py:184
  8.5 0.7 %collective-permute-start = (bf16[64,512]{1,0:T(8,128)(2,1)S(1)}, bf16[64,512]{1,0:T(8,128)(2,1)S(1)}, u32[]{:S(2)}, u32[]{:S(2)}) collective-permute-start(bf16[64,512]{1,0:T(8,128)(2,1)S(1)} %bitcast.11), channel_id=1, source_target_pairs={{0,1},{1,2},{2,3},{3,0},{4,5},{5,6},{6,7},{7,4},{8,9},{9,10},{10,1... | collective-permute-start | bytes 196616 | tf_op jit(solution)/shard_map/ppermute | solution.py:184
  9.2 0.3 collective-permute-start.1
  9.5 2.8 %collective-permute-start.2 = (bf16[64,512]{1,0:T(8,128)(2,1)S(1)}, bf16[64,512]{1,0:T(8,128)(2,1)S(1)}, u32[]{:S(2)}, u32[]{:S(2)}) collective-permute-start(bf16[64,512]{1,0:T(8,128)(2,1)S(1)} %bitcast.13), channel_id=1, source_target_pairs={{0,3},{1,0},{2,1},{3,2},{4,7},{5,4},{6,5},{7,6},{8,11},{9,8},{10,9... | collective-permute-start | bytes 196616 | tf_op jit(solution)/shard_map/ppermute | solution.py:184
  12.3 0.9 %first.1 = (bf16[64,512]{1,0:T(8,128)(2,1)S(1)}, bf16[64,512]{1,0:T(8,128)(2,1)S(1)}, bf16[64,512]{1,0:T(8,128)(2,1)S(1)}, bf16[64,512]{1,0:T(8,128)(2,1)S(1)}, bf16[64,512]{1,0:T(8,128)(2,1)S(1)}) custom-call(bf16[27,64,256]{2,1,0:T(8,128)(2,1)S(1)} %bitcast.7, bf16[64,128]{1,0:T(8,128)(2,1)S(1)} %get-tuple-element.38.refs_0_, ...), custom_call_target="tpu_custom_call" | custom-call | flops 1100000000 | bytes 3000000 | tf_op jit(solution)/shard_map/first/pallas_call | solution.py:37
  13.2 0.6 %collective-permute-start.6 = (bf16[64,512]{1,0:T(8,128)(2,1)S(1)}, bf16[64,512]{1,0:T(8,128)(2,1)S(1)}, u32[]{:S(2)}, u32[]{:S(2)}) collective-permute-start(bf16[64,512]{1,0:T(8,128)(2,1)S(1)} %get-tuple-element.43), channel_id=1, source_target_pairs={{0,1},{1,2},{2,3},{3,0},{4,5},{5,6},{6,7},{7,4},{8,9},{9,10},{10,1... | collective-permute-start | bytes 196616 | tf_op jit(solution)/shard_map/ppermute | solution.py:184
  13.9 2.0 %collective-permute-start.7 = (bf16[64,512]{1,0:T(8,128)(2,1)S(1)}, bf16[64,512]{1,0:T(8,128)(2,1)S(1)}, u32[]{:S(2)}, u32[]{:S(2)}) collective-permute-start(bf16[64,512]{1,0:T(8,128)(2,1)S(1)} %get-tuple-element.44), channel_id=1, source_target_pairs={{0,2},{1,3},{2,0},{3,1},{4,6},{5,7},{6,4},{7,5},{8,10},{9,11},{10,... | collective-permute-start | bytes 196616 | tf_op jit(solution)/shard_map/ppermute | solution.py:184
  15.9 2.4 %collective-permute-start.8 = (bf16[64,512]{1,0:T(8,128)(2,1)S(1)}, bf16[64,512]{1,0:T(8,128)(2,1)S(1)}, u32[]{:S(2)}, u32[]{:S(2)}) collective-permute-start(bf16[64,512]{1,0:T(8,128)(2,1)S(1)} %get-tuple-element.45), channel_id=1, source_target_pairs={{0,3},{1,0},{2,1},{3,2},{4,7},{5,4},{6,5},{7,6},{8,11},{9,8},{10,9... | collective-permute-start | bytes 196616 | tf_op jit(solution)/shard_map/ppermute | solution.py:184
  18.3 1.5 %spread.1.hidden_grad = f32[64,512]{1,0:T(8,128)S(1)} custom-call(bf16[27,64,256]{2,1,0:T(8,128)(2,1)S(1)} %bitcast.8, bf16[256,512]{1,0:T(8,128)(2,1)S(1)} %join.1.g_ref.full), custom_call_target="tpu_custom_call" | custom-call | flops 1650000000 | bytes 4500000 | tf_op jit(solution)/shard_map/spread/pallas_call | solution.py:37
  19.9 2.1 %collective-permute-done.7.refs_2_ = bf16[64,512]{1,0:T(8,128)(2,1)S(1)} collective-permute-done((bf16[64,512]{1,0:T(8,128)(2,1)S(1)}, bf16[64,512]{1,0:T(8,128)(2,1)S(1)}, u32[]{:S(2)}, u32[]{:S(2)}) %collective-permute-start.7) | collective-permute-done | bytes 65568 | tf_op jit(solution)/shard_map/ppermute | solution.py:184
  21.9 0.1 gate.1
  22.0 0.1 collective-permute-start.9
  22.1 1.2 %collective-permute-done.9.bottom = bf16[32,512]{1,0:T(8,128)(2,1)S(1)} collective-permute-done((bf16[32,512]{1,0:T(8,128)(2,1)S(1)}, bf16[32,512]{1,0:T(8,128)(2,1)S(1)}, u32[]{:S(2)}, u32[]{:S(2)}) %collective-permute-start.9) | collective-permute-done | bytes 32800 | tf_op jit(solution)/shard_map/ppermute | solution.py:352
  23.3 0.9 %second.1 = (bf16[128,512]{1,0:T(8,128)(2,1)S(1)}, bf16[128,512]{1,0:T(8,128)(2,1)S(1)}, bf16[128,512]{1,0:T(8,128)(2,1)S(1)}, bf16[128,512]{1,0:T(8,128)(2,1)S(1)}) custom-call(bf16[27,64,256]{2,1,0:T(8,128)(2,1)S(1)} %bitcast.9, bf16[64,512]{1,0:T(8,128)(2,1)S(1)} %get-tuple-element.53.v_ref.hidden, bf16[32,512]{1,0:T(8,128)(2,1)S(1)} %get-tuple-element.47.top, ...), custom_call_target="tpu_custom_call" | custom-call | flops 1100000000 | bytes 3000000 | tf_op jit(solution)/shard_map/second/pallas_call | solution.py:37
  24.2 0.9 %pieces.1 = bf16[4,192,512]{2,1,0:T(8,128)(2,1)} custom-call(bf16[64,512]{1,0:T(8,128)(2,1)S(1)} %get-tuple-element.53.v_ref.hidden, bf16[64,512]{1,0:T(8,128)(2,1)S(1)} %get-tuple-element.54.x, bf16[256,512]{1,0:T(8,128)(2,1)S(1)} %join.1.g_ref.full), custom_call_target="tpu_custom_call" | custom-call | flops 880000000 | bytes 2400000 | tf_op jit(solution)/shard_map/pieces/pallas_call | solution.py:37
  25.1 3.7 %all-to-all-start = ((bf16[4,192,512]{2,1,0:T(8,128)(2,1)}), bf16[4,192,512]{2,1,0:T(8,128)(2,1)S(1)}, u32[]{:S(2)}, u32[]{:S(2)}) async-start(bf16[4,192,512]{2,1,0:T(8,128)(2,1)} %pieces.1), calls=%async_computation | async-start | bytes 1572864 | tf_op jit(solution)/shard_map/all_to_all | solution.py:397
  28.9 1.3 %collective-permute-start.10 = (bf16[128,512]{1,0:T(8,128)(2,1)S(1)}, bf16[128,512]{1,0:T(8,128)(2,1)S(1)}, u32[]{:S(2)}, u32[]{:S(2)}) collective-permute-start(bf16[128,512]{1,0:T(8,128)(2,1)S(1)} %get-tuple-element.56), channel_id=1, source_target_pairs={{0,1},{1,2},{2,3},{3,0},{4,5},{5,6},{6,7},{7,4},{8,9},{9,10},{10,1... | collective-permute-start | bytes 393224 | tf_op jit(solution)/shard_map/ppermute | solution.py:184
  30.1 1.7 %collective-permute-start.11 = (bf16[128,512]{1,0:T(8,128)(2,1)S(1)}, bf16[128,512]{1,0:T(8,128)(2,1)S(1)}, u32[]{:S(2)}, u32[]{:S(2)}) collective-permute-start(bf16[128,512]{1,0:T(8,128)(2,1)S(1)} %get-tuple-element.57), channel_id=1, source_target_pairs={{0,2},{1,3},{2,0},{3,1},{4,6},{5,7},{6,4},{7,5},{8,10},{9,11},{10,... | collective-permute-start | bytes 393224 | tf_op jit(solution)/shard_map/ppermute | solution.py:184
  31.8 0.9 %collective-permute-start.12 = (bf16[128,512]{1,0:T(8,128)(2,1)S(1)}, bf16[128,512]{1,0:T(8,128)(2,1)S(1)}, u32[]{:S(2)}, u32[]{:S(2)}) collective-permute-start(bf16[128,512]{1,0:T(8,128)(2,1)S(1)} %get-tuple-element.58), channel_id=1, source_target_pairs={{0,3},{1,0},{2,1},{3,2},{4,7},{5,4},{6,5},{7,6},{8,11},{9,8},{10,9... | collective-permute-start | bytes 393224 | tf_op jit(solution)/shard_map/ppermute | solution.py:184
  32.7 4.4 %collective-permute-done.10.refs_1_ = bf16[128,512]{1,0:T(8,128)(2,1)S(1)} collective-permute-done((bf16[128,512]{1,0:T(8,128)(2,1)S(1)}, bf16[128,512]{1,0:T(8,128)(2,1)S(1)}, u32[]{:S(2)}, u32[]{:S(2)}) %collective-permute-start.10) | collective-permute-done | bytes 131104 | tf_op jit(solution)/shard_map/ppermute | solution.py:184
  37.1 4.7 %collective-permute-done.11.refs_2_ = bf16[128,512]{1,0:T(8,128)(2,1)S(1)} collective-permute-done((bf16[128,512]{1,0:T(8,128)(2,1)S(1)}, bf16[128,512]{1,0:T(8,128)(2,1)S(1)}, u32[]{:S(2)}, u32[]{:S(2)}) %collective-permute-start.11) | collective-permute-done | bytes 131104 | tf_op jit(solution)/shard_map/ppermute | solution.py:184
  41.8 0.1 collective-permute-start.13
  41.9 1.7 %collective-permute-start.14 = (bf16[64,512]{1,0:T(8,128)(2,1)S(1)}, bf16[64,512]{1,0:T(8,128)(2,1)S(1)}, u32[]{:S(2)}, u32[]{:S(2)}) collective-permute-start(bf16[64,512]{1,0:T(8,128)(2,1)S(1)} %get-tuple-element.69), channel_id=1, source_target_pairs={{0,8},{4,12},{8,0},{12,4},{16,24},{20,28},{24,16},{28,20},{1,9},{5... | collective-permute-start | bytes 196616 | tf_op jit(solution)/shard_map/ppermute | solution.py:352
  43.6 1.5 %collective-permute-start.15 = (bf16[64,512]{1,0:T(8,128)(2,1)S(1)}, bf16[64,512]{1,0:T(8,128)(2,1)S(1)}, u32[]{:S(2)}, u32[]{:S(2)}) collective-permute-start(bf16[64,512]{1,0:T(8,128)(2,1)S(1)} %get-tuple-element.70), channel_id=1, source_target_pairs={{0,16},{4,20},{8,24},{12,28},{16,0},{20,4},{24,8},{28,12},{1,17},{... | collective-permute-start | bytes 196616 | tf_op jit(solution)/shard_map/ppermute | solution.py:352
  45.1 0.4 collective-permute-start.16
  45.5 1.7 %grad.2 = f32[27,32,64]{2,1,0:T(8,128)} custom-call(bf16[4,192,512]{2,1,0:T(8,128)(2,1)S(1)} %all-to-all-done.mine, bf16[4,192,512]{2,1,0:T(8,128)(2,1)S(1)} %collective-permute-done.13.other), custom_call_target="tpu_custom_call" | custom-call | flops 1870000000 | bytes 5100000 | tf_op jit(solution)/shard_map/grad/pallas_call | solution.py:37
  47.2 0.7 %total.1 = bf16[64,512]{1,0:T(8,128)(2,1)} custom-call(bf16[128,512]{1,0:T(8,128)(2,1)S(1)} %get-tuple-element.64.refs_0_, bf16[128,512]{1,0:T(8,128)(2,1)S(1)} %collective-permute-done.10.refs_1_, bf16[128,512]{1,0:T(8,128)(2,1)S(1)} %collective-permute-done.11.refs_2_, bf16[128,512]{1,0:T(8,128)(2,1)S(1)} %collective-permute-done.12.refs_3_), custom_call_target="tpu_custom_call" | custom-call | flops 550000000 | bytes 1500000 | tf_op jit(solution)/shard_map/total/pallas_call | solution.py:37
  47.9 2.4 %collective-permute-done.16.refs_3_ = bf16[64,512]{1,0:T(8,128)(2,1)S(1)} collective-permute-done((bf16[64,512]{1,0:T(8,128)(2,1)S(1)}, bf16[64,512]{1,0:T(8,128)(2,1)S(1)}, u32[]{:S(2)}, u32[]{:S(2)}) %collective-permute-start.16) | collective-permute-done | bytes 65568 | tf_op jit(solution)/shard_map/ppermute | solution.py:352
  50.3 1.7 %grad.3 = f32[27,32,64]{2,1,0:T(8,128)} custom-call(bf16[4,192,512]{2,1,0:T(8,128)(2,1)S(1)} %all-to-all-done.mine, bf16[4,192,512]{2,1,0:T(8,128)(2,1)S(1)} %collective-permute-done.13.other, bf16[64,512]{1,0:T(8,128)(2,1)S(1)} %get-tuple-element.68.refs_0_, bf16[64,512]{1,0:T(8,128)(2,1)S(1)} %collective-permute-done.14.refs_1_, ...), custom_call_target="tpu_custom_call" | custom-call | flops 1870000000 | bytes 5100000 | tf_op jit(solution)/shard_map/grad/pallas_call | solution.py:37
  (23 shorter events, 0.2 us)
Async XLA Ops:
  0.6 0.8 %copy-start.2 = (bf16[1,256,128]{2,1,0:T(8,128)(2,1)S(1)}, bf16[1,256,128]{2,1,0:T(8,128)(2,1)}, u32[]{:S(2)}) copy-start(bf16[1,256,128]{2,1,0:T(8,128)(2,1)} %param.4) | copy-start | bytes 196612
  1.5 7.0 %copy-start.3 = (bf16[1,64,512]{2,1,0:T(8,128)(2,1)S(1)}, bf16[1,64,512]{2,1,0:T(8,128)(2,1)}, u32[]{:S(2)}) copy-start(bf16[1,64,512]{2,1,0:T(8,128)(2,1)} %param.7) | copy-start | bytes 196612
  1.5 10.9 %copy-start = (bf16[64,27,256]{2,0,1:T(8,128)(2,1)S(1)}, bf16[64,27,256]{2,0,1:T(8,128)(2,1)}, u32[]{:S(2)}) copy-start(bf16[64,27,256]{2,0,1:T(8,128)(2,1)} %param.5) | copy-start | bytes 2654212
  1.5 8.0 %collective-permute-start.3 = (bf16[64,128]{1,0:T(8,128)(2,1)S(1)}, bf16[64,128]{1,0:T(8,128)(2,1)S(1)}, u32[]{:S(2)}, u32[]{:S(2)}) collective-permute-start(bf16[64,128]{1,0:T(8,128)(2,1)S(1)} %get-tuple-element.39), channel_id=1, source_target_pairs={{0,1},{1,2},{2,3},{3,0},{4,5},{5,6},{6,7},{7,4},{8,9},{9,10},{10,1... | collective-permute-start | bytes 49160 | tf_op jit(solution)/shard_map/ppermute | solution.py:184
  4.6 7.8 %collective-permute-start.4 = (bf16[64,128]{1,0:T(8,128)(2,1)S(1)}, bf16[64,128]{1,0:T(8,128)(2,1)S(1)}, u32[]{:S(2)}, u32[]{:S(2)}) collective-permute-start(bf16[64,128]{1,0:T(8,128)(2,1)S(1)} %get-tuple-element.40), channel_id=1, source_target_pairs={{0,2},{1,3},{2,0},{3,1},{4,6},{5,7},{6,4},{7,5},{8,10},{9,11},{10,... | collective-permute-start | bytes 49160 | tf_op jit(solution)/shard_map/ppermute | solution.py:184
  7.2 5.2 %collective-permute-start.5 = (bf16[64,128]{1,0:T(8,128)(2,1)S(1)}, bf16[64,128]{1,0:T(8,128)(2,1)S(1)}, u32[]{:S(2)}, u32[]{:S(2)}) collective-permute-start(bf16[64,128]{1,0:T(8,128)(2,1)S(1)} %get-tuple-element.41), channel_id=1, source_target_pairs={{0,3},{1,0},{2,1},{3,2},{4,7},{5,4},{6,5},{7,6},{8,11},{9,8},{10,9... | collective-permute-start | bytes 49160 | tf_op jit(solution)/shard_map/ppermute | solution.py:184
  8.5 7.4 %collective-permute-start = (bf16[64,512]{1,0:T(8,128)(2,1)S(1)}, bf16[64,512]{1,0:T(8,128)(2,1)S(1)}, u32[]{:S(2)}, u32[]{:S(2)}) collective-permute-start(bf16[64,512]{1,0:T(8,128)(2,1)S(1)} %bitcast.11), channel_id=1, source_target_pairs={{0,1},{1,2},{2,3},{3,0},{4,5},{5,6},{6,7},{7,4},{8,9},{9,10},{10,1... | collective-permute-start | bytes 196616 | tf_op jit(solution)/shard_map/ppermute | solution.py:184
  9.2 9.1 %collective-permute-start.1 = (bf16[64,512]{1,0:T(8,128)(2,1)S(1)}, bf16[64,512]{1,0:T(8,128)(2,1)S(1)}, u32[]{:S(2)}, u32[]{:S(2)}) collective-permute-start(bf16[64,512]{1,0:T(8,128)(2,1)S(1)} %bitcast.12), channel_id=1, source_target_pairs={{0,2},{1,3},{2,0},{3,1},{4,6},{5,7},{6,4},{7,5},{8,10},{9,11},{10,... | collective-permute-start | bytes 196616 | tf_op jit(solution)/shard_map/ppermute | solution.py:184
  9.5 8.7 %collective-permute-start.2 = (bf16[64,512]{1,0:T(8,128)(2,1)S(1)}, bf16[64,512]{1,0:T(8,128)(2,1)S(1)}, u32[]{:S(2)}, u32[]{:S(2)}) collective-permute-start(bf16[64,512]{1,0:T(8,128)(2,1)S(1)} %bitcast.13), channel_id=1, source_target_pairs={{0,3},{1,0},{2,1},{3,2},{4,7},{5,4},{6,5},{7,6},{8,11},{9,8},{10,9... | collective-permute-start | bytes 196616 | tf_op jit(solution)/shard_map/ppermute | solution.py:184
  13.2 6.6 %collective-permute-start.6 = (bf16[64,512]{1,0:T(8,128)(2,1)S(1)}, bf16[64,512]{1,0:T(8,128)(2,1)S(1)}, u32[]{:S(2)}, u32[]{:S(2)}) collective-permute-start(bf16[64,512]{1,0:T(8,128)(2,1)S(1)} %get-tuple-element.43), channel_id=1, source_target_pairs={{0,1},{1,2},{2,3},{3,0},{4,5},{5,6},{6,7},{7,4},{8,9},{9,10},{10,1... | collective-permute-start | bytes 196616 | tf_op jit(solution)/shard_map/ppermute | solution.py:184
  13.9 8.0 %collective-permute-start.7 = (bf16[64,512]{1,0:T(8,128)(2,1)S(1)}, bf16[64,512]{1,0:T(8,128)(2,1)S(1)}, u32[]{:S(2)}, u32[]{:S(2)}) collective-permute-start(bf16[64,512]{1,0:T(8,128)(2,1)S(1)} %get-tuple-element.44), channel_id=1, source_target_pairs={{0,2},{1,3},{2,0},{3,1},{4,6},{5,7},{6,4},{7,5},{8,10},{9,11},{10,... | collective-permute-start | bytes 196616 | tf_op jit(solution)/shard_map/ppermute | solution.py:184
  15.9 2.4 %copy-start.1 = (bf16[64,27,256]{2,0,1:T(8,128)(2,1)S(1)}, bf16[64,27,256]{2,0,1:T(8,128)(2,1)}, u32[]{:S(2)}) copy-start(bf16[64,27,256]{2,0,1:T(8,128)(2,1)} %param.6) | copy-start | bytes 2654212
  15.9 6.1 %collective-permute-start.8 = (bf16[64,512]{1,0:T(8,128)(2,1)S(1)}, bf16[64,512]{1,0:T(8,128)(2,1)S(1)}, u32[]{:S(2)}, u32[]{:S(2)}) collective-permute-start(bf16[64,512]{1,0:T(8,128)(2,1)S(1)} %get-tuple-element.45), channel_id=1, source_target_pairs={{0,3},{1,0},{2,1},{3,2},{4,7},{5,4},{6,5},{7,6},{8,11},{9,8},{10,9... | collective-permute-start | bytes 196616 | tf_op jit(solution)/shard_map/ppermute | solution.py:184
  22.0 1.3 %collective-permute-start.9 = (bf16[32,512]{1,0:T(8,128)(2,1)S(1)}, bf16[32,512]{1,0:T(8,128)(2,1)S(1)}, u32[]{:S(2)}, u32[]{:S(2)}) collective-permute-start(bf16[32,512]{1,0:T(8,128)(2,1)S(1)} %get-tuple-element.48), channel_id=1, source_target_pairs={{0,4},{4,0},{8,12},{12,8},{16,20},{20,16},{24,28},{28,24},{1,5},{5... | collective-permute-start | bytes 98312 | tf_op jit(solution)/shard_map/ppermute | solution.py:352
  25.1 16.7 %all-to-all-start = ((bf16[4,192,512]{2,1,0:T(8,128)(2,1)}), bf16[4,192,512]{2,1,0:T(8,128)(2,1)S(1)}, u32[]{:S(2)}, u32[]{:S(2)}) async-start(bf16[4,192,512]{2,1,0:T(8,128)(2,1)} %pieces.1), calls=%async_computation | async-start | bytes 1572864 | tf_op jit(solution)/shard_map/all_to_all | solution.py:397
  28.9 8.3 %collective-permute-start.10 = (bf16[128,512]{1,0:T(8,128)(2,1)S(1)}, bf16[128,512]{1,0:T(8,128)(2,1)S(1)}, u32[]{:S(2)}, u32[]{:S(2)}) collective-permute-start(bf16[128,512]{1,0:T(8,128)(2,1)S(1)} %get-tuple-element.56), channel_id=1, source_target_pairs={{0,1},{1,2},{2,3},{3,0},{4,5},{5,6},{6,7},{7,4},{8,9},{9,10},{10,1... | collective-permute-start | bytes 393224 | tf_op jit(solution)/shard_map/ppermute | solution.py:184
  30.1 11.6 %collective-permute-start.11 = (bf16[128,512]{1,0:T(8,128)(2,1)S(1)}, bf16[128,512]{1,0:T(8,128)(2,1)S(1)}, u32[]{:S(2)}, u32[]{:S(2)}) collective-permute-start(bf16[128,512]{1,0:T(8,128)(2,1)S(1)} %get-tuple-element.57), channel_id=1, source_target_pairs={{0,2},{1,3},{2,0},{3,1},{4,6},{5,7},{6,4},{7,5},{8,10},{9,11},{10,... | collective-permute-start | bytes 393224 | tf_op jit(solution)/shard_map/ppermute | solution.py:184
  31.8 10.0 %collective-permute-start.12 = (bf16[128,512]{1,0:T(8,128)(2,1)S(1)}, bf16[128,512]{1,0:T(8,128)(2,1)S(1)}, u32[]{:S(2)}, u32[]{:S(2)}) collective-permute-start(bf16[128,512]{1,0:T(8,128)(2,1)S(1)} %get-tuple-element.58), channel_id=1, source_target_pairs={{0,3},{1,0},{2,1},{3,2},{4,7},{5,4},{6,5},{7,6},{8,11},{9,8},{10,9... | collective-permute-start | bytes 393224 | tf_op jit(solution)/shard_map/ppermute | solution.py:184
  41.8 3.6 %collective-permute-start.13 = (bf16[4,192,512]{2,1,0:T(8,128)(2,1)S(1)}, bf16[4,192,512]{2,1,0:T(8,128)(2,1)S(1)}, u32[]{:S(2)}, u32[]{:S(2)}) collective-permute-start(bf16[4,192,512]{2,1,0:T(8,128)(2,1)S(1)} %all-to-all-done.mine), channel_id=1, source_target_pairs={{0,4},{4,0},{8,12},{12,8},{16,20},{20,16},{24,28},{28,24},{1,5},{5... | collective-permute-start | bytes 2359304 | tf_op jit(solution)/shard_map/ppermute | solution.py:352
  41.9 5.9 %collective-permute-start.14 = (bf16[64,512]{1,0:T(8,128)(2,1)S(1)}, bf16[64,512]{1,0:T(8,128)(2,1)S(1)}, u32[]{:S(2)}, u32[]{:S(2)}) collective-permute-start(bf16[64,512]{1,0:T(8,128)(2,1)S(1)} %get-tuple-element.69), channel_id=1, source_target_pairs={{0,8},{4,12},{8,0},{12,4},{16,24},{20,28},{24,16},{28,20},{1,9},{5... | collective-permute-start | bytes 196616 | tf_op jit(solution)/shard_map/ppermute | solution.py:352
  43.6 4.3 %collective-permute-start.15 = (bf16[64,512]{1,0:T(8,128)(2,1)S(1)}, bf16[64,512]{1,0:T(8,128)(2,1)S(1)}, u32[]{:S(2)}, u32[]{:S(2)}) collective-permute-start(bf16[64,512]{1,0:T(8,128)(2,1)S(1)} %get-tuple-element.70), channel_id=1, source_target_pairs={{0,16},{4,20},{8,24},{12,28},{16,0},{20,4},{24,8},{28,12},{1,17},{... | collective-permute-start | bytes 196616 | tf_op jit(solution)/shard_map/ppermute | solution.py:352
  45.1 5.2 %collective-permute-start.16 = (bf16[64,512]{1,0:T(8,128)(2,1)S(1)}, bf16[64,512]{1,0:T(8,128)(2,1)S(1)}, u32[]{:S(2)}, u32[]{:S(2)}) collective-permute-start(bf16[64,512]{1,0:T(8,128)(2,1)S(1)} %get-tuple-element.71), channel_id=1, source_target_pairs={{0,24},{4,28},{8,16},{12,20},{16,8},{20,12},{24,0},{28,4},{1,25},{... | collective-permute-start | bytes 196616 | tf_op jit(solution)/shard_map/ppermute | solution.py:352

commit v6 on v5

--- a/solution.py
+++ b/solution.py
@@ -291,29 +291,25 @@
     give[...] = both[pl.ds(other, rows), :]
 
 
-def output_kernel(chans, w_ref, v_ref, top, bottom, *refs):
-    outs, scratch = refs[:chans], refs[chans:]
-    rows, half_rows = v_ref.shape[0], top.shape[0]
-    conv_part(chans, w_ref, v_ref[...], [out.at[:rows] for out in outs], *scratch)
-    for out in outs:
-        out[rows : rows + half_rows, :] = top[...]
-        out[rows + half_rows :, :] = bottom[...]
+def stack_kernel(top, bottom, out):
+    rows = top.shape[0]
+    out[:rows, :] = top[...]
+    out[rows:, :] = bottom[...]
 
 
 def route_kernel(chans, *refs):
     parts, outs, full = refs[:chans], refs[chans:-1], refs[-1]
     rows = outs[0].shape[0]
-    join_kernel(chans, *[part.at[rows:] for part in parts], full)
+    join_kernel(chans, *parts, full)
     for step, out in enumerate(outs):
         out[...] = full[far(step, rows), :]
 
 
 def total_kernel(*refs):
     *parts, out = refs
-    rows = out.shape[0]
-    total = parts[0][:rows, :].astype(F32)
+    total = parts[0][...].astype(F32)
     for part in parts[1:]:
-        total = total + part[:rows, :].astype(F32)
+        total = total + part[...].astype(F32)
     out[...] = total.astype(BF16)
 
 
@@ -375,16 +371,12 @@
         "gate",
         0.9,
     )
-    parts = call(
-        run(output_kernel),
-        [((2 * ins, CELLS), BF16)] * chans,
-        [second_w, hidden, keep, hop(give, 1)],
-        patches,
-        "second",
-        1.0,
-    )
-    hidden, *parts = lax.optimization_barrier((hidden, *parts))
-    parts = exchange(parts, chans)
+    got = hop(give, 1)
+    map_grad = call(stack_kernel, [piece], [keep, got], (), "stack", 0.3)[0]
+    map_grads = exchange([map_grad] * chans, chans)
+    parts = exchange(
+        call(run(second_kernel), [piece] * chans, [second_w, hidden], patches, "second", 0.9), chans
+    )
     pieces = call(
         pieces_kernel,
         [((chips, 3 * ins, CELLS), BF16)],
@@ -393,10 +385,10 @@
         "pieces",
         0.8,
     )[0]
+    pieces, got = lax.optimization_barrier((pieces, got))
     cores = [list(range(core, samples, 2)) for core in (0, 1)]
     pieces = lax.all_to_all(pieces, "sample", 0, 0, axis_index_groups=cores, tiled=True)
-    routed = call(run(route_kernel), [piece] * chips, parts, patches[1:], "route", 0.6)
-    pieces, *routed = lax.optimization_barrier((pieces, *routed))
+    routed = call(run(route_kernel), [piece] * chips, map_grads, patches[1:], "route", 15.0)
     map_grads = chip_hops(routed)
     pieces = [pieces, hop(pieces, 1)]
     scratch = [

time: 52.5 us -> 47.9 us (0.912)
  waiting for transfers between devices: 14.8 us -> 5.36 us
  starting transfers between devices: 27.1 us -> 32 us
    ppermute x12 -> x15, waiting for transfers between devices: 11.2 us -> 2.1 us  [send(): lax.ppermute(v, 'chan', [(k, (k + step) % size) for k in range(size)])]
    ppermute x12 -> x15, starting transfers between devices: 19.7 us -> 24.7 us  [send(): lax.ppermute(v, 'chan', [(k, (k + step) % size) for k in range(size)])]
    ppermute x5, waiting for transfers between devices: 3.61 us -> 1.77 us  [body(): lax.ppermute(v, 'sample', [(s, s ^ step) for s in range(samples)])]
    all_to_all x1, waiting for transfers between devices: 0.01 us -> 1.49 us  [body(): lax.all_to_all(pieces, 'sample', 0, 0, axis_index_groups=cores, tiled=True)]
    pallas_call x11 -> x12, Pallas kernels: 8.53 us -> 8.55 us  [call(): pl.pallas_call(kernel, out_shape=[jax.ShapeDtypeStruct(shape, dtype) for...]
  transfers between devices with their start and end apart: 18 -> 21, of which waited for: 5 -> 5; matrix products, arithmetic and copies ran while one was open for 0% -> 0% of each run, Pallas kernels for 9% -> 14%
where the time goes in v6:
time: 47.9 us; the launch traced here: 47.5 us
  starting transfers between devices  32 us (67%)
  Pallas kernels  8.55 us (18%)
  waiting for transfers between devices  5.36 us (11%)
  local copies, waits for them, and re-layouts  0.84 us (2%)
  between operations  0.73 us (2%)
    ppermute x15, starting transfers between devices, send(): lax.ppermute(v, 'chan', [(k, (k + step) % size) for k in range(size)])  24.7 us
    pallas_call x12, Pallas kernels, call(): pl.pallas_call(kernel, out_shape=[jax.ShapeDtypeStruct(shape, dtype) for...  8.55 us
    all_to_all x1, starting transfers between devices, body(): lax.all_to_all(pieces, 'sample', 0, 0, axis_index_groups=cores, tiled=True)  3.72 us
    ppermute x5, starting transfers between devices, body(): lax.ppermute(v, 'sample', [(s, s ^ step) for s in range(samples)])  3.53 us
    ppermute x15, waiting for transfers between devices, send(): lax.ppermute(v, 'chan', [(k, (k + step) % size) for k in range(size)])  2.1 us
    ppermute x5, waiting for transfers between devices, body(): lax.ppermute(v, 'sample', [(s, s ^ step) for s in range(samples)])  1.77 us
    all_to_all x1, waiting for transfers between devices, body(): lax.all_to_all(pieces, 'sample', 0, 0, axis_index_groups=cores, tiled=True)  1.49 us
  transfers between devices with their start and end apart: 21, of which 5 were waited for; matrix products, arithmetic and copies ran while one was open for 0% of the time, Pallas kernels for 14%

profile of v6, /device:TPU:0, one launch (start us, length us, event | category | flops | bytes accessed | tf_op | source)
XLA Modules:
  0.0 47.5 jit_solution(16320901787194376967)
XLA Ops:
  0.6 0.8 %copy-done.2 = bf16[1,256,128]{2,1,0:T(8,128)(2,1)S(1)} copy-done((bf16[1,256,128]{2,1,0:T(8,128)(2,1)S(1)}, bf16[1,256,128]{2,1,0:T(8,128)(2,1)}, u32[]{:S(2)}) %copy-start.2) | copy-done | bytes 65560
  1.5 3.1 %collective-permute-start.3 = (bf16[64,128]{1,0:T(8,128)(2,1)S(1)}, bf16[64,128]{1,0:T(8,128)(2,1)S(1)}, u32[]{:S(2)}, u32[]{:S(2)}) collective-permute-start(bf16[64,128]{1,0:T(8,128)(2,1)S(1)} %get-tuple-element.30), channel_id=1, source_target_pairs={{0,1},{1,2},{2,3},{3,0},{4,5},{5,6},{6,7},{7,4},{8,9},{9,10},{10,1... | collective-permute-start | bytes 49160 | tf_op jit(solution)/shard_map/ppermute | solution.py:184
  4.6 2.6 %collective-permute-start.4 = (bf16[64,128]{1,0:T(8,128)(2,1)S(1)}, bf16[64,128]{1,0:T(8,128)(2,1)S(1)}, u32[]{:S(2)}, u32[]{:S(2)}) collective-permute-start(bf16[64,128]{1,0:T(8,128)(2,1)S(1)} %get-tuple-element.31), channel_id=1, source_target_pairs={{0,2},{1,3},{2,0},{3,1},{4,6},{5,7},{6,4},{7,5},{8,10},{9,11},{10,... | collective-permute-start | bytes 49160 | tf_op jit(solution)/shard_map/ppermute | solution.py:184
  7.2 1.3 %collective-permute-start.5 = (bf16[64,128]{1,0:T(8,128)(2,1)S(1)}, bf16[64,128]{1,0:T(8,128)(2,1)S(1)}, u32[]{:S(2)}, u32[]{:S(2)}) collective-permute-start(bf16[64,128]{1,0:T(8,128)(2,1)S(1)} %get-tuple-element.32), channel_id=1, source_target_pairs={{0,3},{1,0},{2,1},{3,2},{4,7},{5,4},{6,5},{7,6},{8,11},{9,8},{10,9... | collective-permute-start | bytes 49160 | tf_op jit(solution)/shard_map/ppermute | solution.py:184
  8.5 0.7 %collective-permute-start = (bf16[64,512]{1,0:T(8,128)(2,1)S(1)}, bf16[64,512]{1,0:T(8,128)(2,1)S(1)}, u32[]{:S(2)}, u32[]{:S(2)}) collective-permute-start(bf16[64,512]{1,0:T(8,128)(2,1)S(1)} %bitcast.11), channel_id=1, source_target_pairs={{0,1},{1,2},{2,3},{3,0},{4,5},{5,6},{6,7},{7,4},{8,9},{9,10},{10,1... | collective-permute-start | bytes 196616 | tf_op jit(solution)/shard_map/ppermute | solution.py:184
  9.2 0.3 collective-permute-start.1
  9.5 2.8 %collective-permute-start.2 = (bf16[64,512]{1,0:T(8,128)(2,1)S(1)}, bf16[64,512]{1,0:T(8,128)(2,1)S(1)}, u32[]{:S(2)}, u32[]{:S(2)}) collective-permute-start(bf16[64,512]{1,0:T(8,128)(2,1)S(1)} %bitcast.13), channel_id=1, source_target_pairs={{0,3},{1,0},{2,1},{3,2},{4,7},{5,4},{6,5},{7,6},{8,11},{9,8},{10,9... | collective-permute-start | bytes 196616 | tf_op jit(solution)/shard_map/ppermute | solution.py:184
  12.3 0.9 %first.1 = (bf16[64,512]{1,0:T(8,128)(2,1)S(1)}, bf16[64,512]{1,0:T(8,128)(2,1)S(1)}, bf16[64,512]{1,0:T(8,128)(2,1)S(1)}, bf16[64,512]{1,0:T(8,128)(2,1)S(1)}, bf16[64,512]{1,0:T(8,128)(2,1)S(1)}) custom-call(bf16[27,64,256]{2,1,0:T(8,128)(2,1)S(1)} %bitcast.7, bf16[64,128]{1,0:T(8,128)(2,1)S(1)} %get-tuple-element.29.refs_0_, ...), custom_call_target="tpu_custom_call" | custom-call | flops 1100000000 | bytes 3000000 | tf_op jit(solution)/shard_map/first/pallas_call | solution.py:37
  13.2 0.6 %collective-permute-start.6 = (bf16[64,512]{1,0:T(8,128)(2,1)S(1)}, bf16[64,512]{1,0:T(8,128)(2,1)S(1)}, u32[]{:S(2)}, u32[]{:S(2)}) collective-permute-start(bf16[64,512]{1,0:T(8,128)(2,1)S(1)} %get-tuple-element.34), channel_id=1, source_target_pairs={{0,1},{1,2},{2,3},{3,0},{4,5},{5,6},{6,7},{7,4},{8,9},{9,10},{10,1... | collective-permute-start | bytes 196616 | tf_op jit(solution)/shard_map/ppermute | solution.py:184
  13.9 2.0 %collective-permute-start.7 = (bf16[64,512]{1,0:T(8,128)(2,1)S(1)}, bf16[64,512]{1,0:T(8,128)(2,1)S(1)}, u32[]{:S(2)}, u32[]{:S(2)}) collective-permute-start(bf16[64,512]{1,0:T(8,128)(2,1)S(1)} %get-tuple-element.35), channel_id=1, source_target_pairs={{0,2},{1,3},{2,0},{3,1},{4,6},{5,7},{6,4},{7,5},{8,10},{9,11},{10,... | collective-permute-start | bytes 196616 | tf_op jit(solution)/shard_map/ppermute | solution.py:184
  15.9 2.4 %collective-permute-start.8 = (bf16[64,512]{1,0:T(8,128)(2,1)S(1)}, bf16[64,512]{1,0:T(8,128)(2,1)S(1)}, u32[]{:S(2)}, u32[]{:S(2)}) collective-permute-start(bf16[64,512]{1,0:T(8,128)(2,1)S(1)} %get-tuple-element.36), channel_id=1, source_target_pairs={{0,3},{1,0},{2,1},{3,2},{4,7},{5,4},{6,5},{7,6},{8,11},{9,8},{10,9... | collective-permute-start | bytes 196616 | tf_op jit(solution)/shard_map/ppermute | solution.py:184
  18.3 1.5 %spread.1.hidden_grad = f32[64,512]{1,0:T(8,128)S(1)} custom-call(bf16[27,64,256]{2,1,0:T(8,128)(2,1)S(1)} %bitcast.8, bf16[256,512]{1,0:T(8,128)(2,1)S(1)} %join.1.g_ref.full), custom_call_target="tpu_custom_call" | custom-call | flops 1650000000 | bytes 4500000 | tf_op jit(solution)/shard_map/spread/pallas_call | solution.py:37
  19.9 2.1 %collective-permute-done.7.refs_2_ = bf16[64,512]{1,0:T(8,128)(2,1)S(1)} collective-permute-done((bf16[64,512]{1,0:T(8,128)(2,1)S(1)}, bf16[64,512]{1,0:T(8,128)(2,1)S(1)}, u32[]{:S(2)}, u32[]{:S(2)}) %collective-permute-start.7) | collective-permute-done | bytes 65568 | tf_op jit(solution)/shard_map/ppermute | solution.py:184
  22.1 1.0 %pieces.1 = bf16[4,192,512]{2,1,0:T(8,128)(2,1)} custom-call(bf16[64,512]{1,0:T(8,128)(2,1)S(1)} %get-tuple-element.37.hidden.v_ref, bf16[64,512]{1,0:T(8,128)(2,1)S(1)} %get-tuple-element.38.x, bf16[256,512]{1,0:T(8,128)(2,1)S(1)} %join.1.g_ref.full), custom_call_target="tpu_custom_call" | custom-call | flops 880000000 | bytes 2400000 | tf_op jit(solution)/shard_map/pieces/pallas_call | solution.py:37
  23.1 0.2 collective-permute-done.9.bottom
  23.3 3.7 %all-to-all-start = ((bf16[4,192,512]{2,1,0:T(8,128)(2,1)}), bf16[4,192,512]{2,1,0:T(8,128)(2,1)S(1)}, u32[]{:S(2)}, u32[]{:S(2)}) async-start(bf16[4,192,512]{2,1,0:T(8,128)(2,1)} %pieces.1), calls=%async_computation | async-start | bytes 1572864 | tf_op jit(solution)/shard_map/all_to_all | solution.py:390
  27.0 1.3 %collective-permute-start.14 = (bf16[64,512]{1,0:T(8,128)(2,1)S(1)}, bf16[64,512]{1,0:T(8,128)(2,1)S(1)}, u32[]{:S(2)}, u32[]{:S(2)}) collective-permute-start(bf16[64,512]{1,0:T(8,128)(2,1)S(1)} %stack.1.refs_0_), channel_id=1, source_target_pairs={{0,1},{1,2},{2,3},{3,0},{4,5},{5,6},{6,7},{7,4},{8,9},{9,10},{10,1... | collective-permute-start | bytes 196616 | tf_op jit(solution)/shard_map/ppermute | solution.py:184
  28.4 1.7 %collective-permute-start.15 = (bf16[64,512]{1,0:T(8,128)(2,1)S(1)}, bf16[64,512]{1,0:T(8,128)(2,1)S(1)}, u32[]{:S(2)}, u32[]{:S(2)}) collective-permute-start(bf16[64,512]{1,0:T(8,128)(2,1)S(1)} %stack.1.refs_0_), channel_id=1, source_target_pairs={{0,2},{1,3},{2,0},{3,1},{4,6},{5,7},{6,4},{7,5},{8,10},{9,11},{10,... | collective-permute-start | bytes 196616 | tf_op jit(solution)/shard_map/ppermute | solution.py:184
  30.0 0.9 %collective-permute-start.16 = (bf16[64,512]{1,0:T(8,128)(2,1)S(1)}, bf16[64,512]{1,0:T(8,128)(2,1)S(1)}, u32[]{:S(2)}, u32[]{:S(2)}) collective-permute-start(bf16[64,512]{1,0:T(8,128)(2,1)S(1)} %stack.1.refs_0_), channel_id=1, source_target_pairs={{0,3},{1,0},{2,1},{3,2},{4,7},{5,4},{6,5},{7,6},{8,11},{9,8},{10,9... | collective-permute-start | bytes 196616 | tf_op jit(solution)/shard_map/ppermute | solution.py:184
  30.9 0.9 %second.1 = (bf16[64,512]{1,0:T(8,128)(2,1)S(1)}, bf16[64,512]{1,0:T(8,128)(2,1)S(1)}, bf16[64,512]{1,0:T(8,128)(2,1)S(1)}, bf16[64,512]{1,0:T(8,128)(2,1)S(1)}) custom-call(bf16[27,64,256]{2,1,0:T(8,128)(2,1)S(1)} %bitcast.9, bf16[64,512]{1,0:T(8,128)(2,1)S(1)} %get-tuple-element.37.hidden.v_ref), custom_call_target="tpu_custom_call" | custom-call | flops 990000000 | bytes 2700000 | tf_op jit(solution)/shard_map/second/pallas_call | solution.py:37
  31.8 1.2 %collective-permute-start.11 = (bf16[64,512]{1,0:T(8,128)(2,1)S(1)}, bf16[64,512]{1,0:T(8,128)(2,1)S(1)}, u32[]{:S(2)}, u32[]{:S(2)}) collective-permute-start(bf16[64,512]{1,0:T(8,128)(2,1)S(1)} %get-tuple-element.42), channel_id=1, source_target_pairs={{0,1},{1,2},{2,3},{3,0},{4,5},{5,6},{6,7},{7,4},{8,9},{9,10},{10,1... | collective-permute-start | bytes 196616 | tf_op jit(solution)/shard_map/ppermute | solution.py:184
  33.0 1.2 %collective-permute-start.12 = (bf16[64,512]{1,0:T(8,128)(2,1)S(1)}, bf16[64,512]{1,0:T(8,128)(2,1)S(1)}, u32[]{:S(2)}, u32[]{:S(2)}) collective-permute-start(bf16[64,512]{1,0:T(8,128)(2,1)S(1)} %get-tuple-element.43), channel_id=1, source_target_pairs={{0,2},{1,3},{2,0},{3,1},{4,6},{5,7},{6,4},{7,5},{8,10},{9,11},{10,... | collective-permute-start | bytes 196616 | tf_op jit(solution)/shard_map/ppermute | solution.py:184
  34.3 2.6 %collective-permute-start.13 = (bf16[64,512]{1,0:T(8,128)(2,1)S(1)}, bf16[64,512]{1,0:T(8,128)(2,1)S(1)}, u32[]{:S(2)}, u32[]{:S(2)}) collective-permute-start(bf16[64,512]{1,0:T(8,128)(2,1)S(1)} %get-tuple-element.44), channel_id=1, source_target_pairs={{0,3},{1,0},{2,1},{3,2},{4,7},{5,4},{6,5},{7,6},{8,11},{9,8},{10,9... | collective-permute-start | bytes 196616 | tf_op jit(solution)/shard_map/ppermute | solution.py:184
  36.8 1.5 %all-to-all-done.mine = bf16[4,192,512]{2,1,0:T(8,128)(2,1)S(1)} async-done(((bf16[4,192,512]{2,1,0:T(8,128)(2,1)}), bf16[4,192,512]{2,1,0:T(8,128)(2,1)S(1)}, u32[]{:S(2)}, u32[]{:S(2)}) %all-to-all-start) | async-done | bytes 786464 | tf_op jit(solution)/shard_map/all_to_all | solution.py:390
  38.4 1.5 %collective-permute-start.17 = (bf16[64,512]{1,0:T(8,128)(2,1)S(1)}, bf16[64,512]{1,0:T(8,128)(2,1)S(1)}, u32[]{:S(2)}, u32[]{:S(2)}) collective-permute-start(bf16[64,512]{1,0:T(8,128)(2,1)S(1)} %get-tuple-element.51), channel_id=1, source_target_pairs={{0,8},{4,12},{8,0},{12,4},{16,24},{20,28},{24,16},{28,20},{1,9},{5... | collective-permute-start | bytes 196616 | tf_op jit(solution)/shard_map/ppermute | solution.py:348
  39.9 0.6 %collective-permute-start.18 = (bf16[64,512]{1,0:T(8,128)(2,1)S(1)}, bf16[64,512]{1,0:T(8,128)(2,1)S(1)}, u32[]{:S(2)}, u32[]{:S(2)}) collective-permute-start(bf16[64,512]{1,0:T(8,128)(2,1)S(1)} %get-tuple-element.52), channel_id=1, source_target_pairs={{0,16},{4,20},{8,24},{12,28},{16,0},{20,4},{24,8},{28,12},{1,17},{... | collective-permute-start | bytes 196616 | tf_op jit(solution)/shard_map/ppermute | solution.py:348
  40.4 0.2 collective-permute-done.10.other
  40.6 1.4 %collective-permute-start.19 = (bf16[64,512]{1,0:T(8,128)(2,1)S(1)}, bf16[64,512]{1,0:T(8,128)(2,1)S(1)}, u32[]{:S(2)}, u32[]{:S(2)}) collective-permute-start(bf16[64,512]{1,0:T(8,128)(2,1)S(1)} %get-tuple-element.53), channel_id=1, source_target_pairs={{0,24},{4,28},{8,16},{12,20},{16,8},{20,12},{24,0},{28,4},{1,25},{... | collective-permute-start | bytes 196616 | tf_op jit(solution)/shard_map/ppermute | solution.py:348
  42.0 1.7 %grad.2 = f32[27,32,64]{2,1,0:T(8,128)} custom-call(bf16[4,192,512]{2,1,0:T(8,128)(2,1)S(1)} %all-to-all-done.mine, bf16[4,192,512]{2,1,0:T(8,128)(2,1)S(1)} %collective-permute-done.10.other), custom_call_target="tpu_custom_call" | custom-call | flops 1870000000 | bytes 5100000 | tf_op jit(solution)/shard_map/grad/pallas_call | solution.py:37
  43.7 0.7 %total.1 = bf16[64,512]{1,0:T(8,128)(2,1)} custom-call(bf16[64,512]{1,0:T(8,128)(2,1)S(1)} %get-tuple-element.45.refs_0_, bf16[64,512]{1,0:T(8,128)(2,1)S(1)} %collective-permute-done.11.refs_1_, bf16[64,512]{1,0:T(8,128)(2,1)S(1)} %collective-permute-done.12.refs_2_, bf16[64,512]{1,0:T(8,128)(2,1)S(1)} %collective-permute-done.13.refs_3_), custom_call_target="tpu_custom_call" | custom-call | flops 550000000 | bytes 1500000 | tf_op jit(solution)/shard_map/total/pallas_call | solution.py:37
  44.4 1.4 %collective-permute-done.19.refs_3_ = bf16[64,512]{1,0:T(8,128)(2,1)S(1)} collective-permute-done((bf16[64,512]{1,0:T(8,128)(2,1)S(1)}, bf16[64,512]{1,0:T(8,128)(2,1)S(1)}, u32[]{:S(2)}, u32[]{:S(2)}) %collective-permute-start.19) | collective-permute-done | bytes 65568 | tf_op jit(solution)/shard_map/ppermute | solution.py:348
  45.8 1.7 %grad.3 = f32[27,32,64]{2,1,0:T(8,128)} custom-call(bf16[4,192,512]{2,1,0:T(8,128)(2,1)S(1)} %all-to-all-done.mine, bf16[4,192,512]{2,1,0:T(8,128)(2,1)S(1)} %collective-permute-done.10.other, bf16[64,512]{1,0:T(8,128)(2,1)S(1)} %get-tuple-element.50.refs_0_, bf16[64,512]{1,0:T(8,128)(2,1)S(1)} %collective-permute-done.17.refs_1_, ...), custom_call_target="tpu_custom_call" | custom-call | flops 1870000000 | bytes 5100000 | tf_op jit(solution)/shard_map/grad/pallas_call | solution.py:37
  (30 shorter events, 0.3 us)
Async XLA Ops:
  0.6 0.8 %copy-start.2 = (bf16[1,256,128]{2,1,0:T(8,128)(2,1)S(1)}, bf16[1,256,128]{2,1,0:T(8,128)(2,1)}, u32[]{:S(2)}) copy-start(bf16[1,256,128]{2,1,0:T(8,128)(2,1)} %param.4) | copy-start | bytes 196612
  1.5 7.0 %copy-start.3 = (bf16[1,64,512]{2,1,0:T(8,128)(2,1)S(1)}, bf16[1,64,512]{2,1,0:T(8,128)(2,1)}, u32[]{:S(2)}) copy-start(bf16[1,64,512]{2,1,0:T(8,128)(2,1)} %param.7) | copy-start | bytes 196612
  1.5 10.9 %copy-start = (bf16[64,27,256]{2,0,1:T(8,128)(2,1)S(1)}, bf16[64,27,256]{2,0,1:T(8,128)(2,1)}, u32[]{:S(2)}) copy-start(bf16[64,27,256]{2,0,1:T(8,128)(2,1)} %param.5) | copy-start | bytes 2654212
  1.5 8.0 %collective-permute-start.3 = (bf16[64,128]{1,0:T(8,128)(2,1)S(1)}, bf16[64,128]{1,0:T(8,128)(2,1)S(1)}, u32[]{:S(2)}, u32[]{:S(2)}) collective-permute-start(bf16[64,128]{1,0:T(8,128)(2,1)S(1)} %get-tuple-element.30), channel_id=1, source_target_pairs={{0,1},{1,2},{2,3},{3,0},{4,5},{5,6},{6,7},{7,4},{8,9},{9,10},{10,1... | collective-permute-start | bytes 49160 | tf_op jit(solution)/shard_map/ppermute | solution.py:184
  4.6 7.8 %collective-permute-start.4 = (bf16[64,128]{1,0:T(8,128)(2,1)S(1)}, bf16[64,128]{1,0:T(8,128)(2,1)S(1)}, u32[]{:S(2)}, u32[]{:S(2)}) collective-permute-start(bf16[64,128]{1,0:T(8,128)(2,1)S(1)} %get-tuple-element.31), channel_id=1, source_target_pairs={{0,2},{1,3},{2,0},{3,1},{4,6},{5,7},{6,4},{7,5},{8,10},{9,11},{10,... | collective-permute-start | bytes 49160 | tf_op jit(solution)/shard_map/ppermute | solution.py:184
  7.2 5.2 %collective-permute-start.5 = (bf16[64,128]{1,0:T(8,128)(2,1)S(1)}, bf16[64,128]{1,0:T(8,128)(2,1)S(1)}, u32[]{:S(2)}, u32[]{:S(2)}) collective-permute-start(bf16[64,128]{1,0:T(8,128)(2,1)S(1)} %get-tuple-element.32), channel_id=1, source_target_pairs={{0,3},{1,0},{2,1},{3,2},{4,7},{5,4},{6,5},{7,6},{8,11},{9,8},{10,9... | collective-permute-start | bytes 49160 | tf_op jit(solution)/shard_map/ppermute | solution.py:184
  8.5 7.4 %collective-permute-start = (bf16[64,512]{1,0:T(8,128)(2,1)S(1)}, bf16[64,512]{1,0:T(8,128)(2,1)S(1)}, u32[]{:S(2)}, u32[]{:S(2)}) collective-permute-start(bf16[64,512]{1,0:T(8,128)(2,1)S(1)} %bitcast.11), channel_id=1, source_target_pairs={{0,1},{1,2},{2,3},{3,0},{4,5},{5,6},{6,7},{7,4},{8,9},{9,10},{10,1... | collective-permute-start | bytes 196616 | tf_op jit(solution)/shard_map/ppermute | solution.py:184
  9.2 9.1 %collective-permute-start.1 = (bf16[64,512]{1,0:T(8,128)(2,1)S(1)}, bf16[64,512]{1,0:T(8,128)(2,1)S(1)}, u32[]{:S(2)}, u32[]{:S(2)}) collective-permute-start(bf16[64,512]{1,0:T(8,128)(2,1)S(1)} %bitcast.12), channel_id=1, source_target_pairs={{0,2},{1,3},{2,0},{3,1},{4,6},{5,7},{6,4},{7,5},{8,10},{9,11},{10,... | collective-permute-start | bytes 196616 | tf_op jit(solution)/shard_map/ppermute | solution.py:184
  9.5 8.7 %collective-permute-start.2 = (bf16[64,512]{1,0:T(8,128)(2,1)S(1)}, bf16[64,512]{1,0:T(8,128)(2,1)S(1)}, u32[]{:S(2)}, u32[]{:S(2)}) collective-permute-start(bf16[64,512]{1,0:T(8,128)(2,1)S(1)} %bitcast.13), channel_id=1, source_target_pairs={{0,3},{1,0},{2,1},{3,2},{4,7},{5,4},{6,5},{7,6},{8,11},{9,8},{10,9... | collective-permute-start | bytes 196616 | tf_op jit(solution)/shard_map/ppermute | solution.py:184
  13.2 6.6 %collective-permute-start.6 = (bf16[64,512]{1,0:T(8,128)(2,1)S(1)}, bf16[64,512]{1,0:T(8,128)(2,1)S(1)}, u32[]{:S(2)}, u32[]{:S(2)}) collective-permute-start(bf16[64,512]{1,0:T(8,128)(2,1)S(1)} %get-tuple-element.34), channel_id=1, source_target_pairs={{0,1},{1,2},{2,3},{3,0},{4,5},{5,6},{6,7},{7,4},{8,9},{9,10},{10,1... | collective-permute-start | bytes 196616 | tf_op jit(solution)/shard_map/ppermute | solution.py:184
  13.9 8.0 %collective-permute-start.7 = (bf16[64,512]{1,0:T(8,128)(2,1)S(1)}, bf16[64,512]{1,0:T(8,128)(2,1)S(1)}, u32[]{:S(2)}, u32[]{:S(2)}) collective-permute-start(bf16[64,512]{1,0:T(8,128)(2,1)S(1)} %get-tuple-element.35), channel_id=1, source_target_pairs={{0,2},{1,3},{2,0},{3,1},{4,6},{5,7},{6,4},{7,5},{8,10},{9,11},{10,... | collective-permute-start | bytes 196616 | tf_op jit(solution)/shard_map/ppermute | solution.py:184
  15.9 2.4 %copy-start.1 = (bf16[64,27,256]{2,0,1:T(8,128)(2,1)S(1)}, bf16[64,27,256]{2,0,1:T(8,128)(2,1)}, u32[]{:S(2)}) copy-start(bf16[64,27,256]{2,0,1:T(8,128)(2,1)} %param.6) | copy-start | bytes 2654212
  15.9 6.1 %collective-permute-start.8 = (bf16[64,512]{1,0:T(8,128)(2,1)S(1)}, bf16[64,512]{1,0:T(8,128)(2,1)S(1)}, u32[]{:S(2)}, u32[]{:S(2)}) collective-permute-start(bf16[64,512]{1,0:T(8,128)(2,1)S(1)} %get-tuple-element.36), channel_id=1, source_target_pairs={{0,3},{1,0},{2,1},{3,2},{4,7},{5,4},{6,5},{7,6},{8,11},{9,8},{10,9... | collective-permute-start | bytes 196616 | tf_op jit(solution)/shard_map/ppermute | solution.py:184
  22.0 1.3 %collective-permute-start.9 = (bf16[32,512]{1,0:T(8,128)(2,1)S(1)}, bf16[32,512]{1,0:T(8,128)(2,1)S(1)}, u32[]{:S(2)}, u32[]{:S(2)}) collective-permute-start(bf16[32,512]{1,0:T(8,128)(2,1)S(1)} %get-tuple-element.39), channel_id=1, source_target_pairs={{0,4},{4,0},{8,12},{12,8},{16,20},{20,16},{24,28},{28,24},{1,5},{5... | collective-permute-start | bytes 98312 | tf_op jit(solution)/shard_map/ppermute | solution.py:348
  23.3 15.0 %all-to-all-start = ((bf16[4,192,512]{2,1,0:T(8,128)(2,1)}), bf16[4,192,512]{2,1,0:T(8,128)(2,1)S(1)}, u32[]{:S(2)}, u32[]{:S(2)}) async-start(bf16[4,192,512]{2,1,0:T(8,128)(2,1)} %pieces.1), calls=%async_computation | async-start | bytes 1572864 | tf_op jit(solution)/shard_map/all_to_all | solution.py:390
  27.0 7.2 %collective-permute-start.14 = (bf16[64,512]{1,0:T(8,128)(2,1)S(1)}, bf16[64,512]{1,0:T(8,128)(2,1)S(1)}, u32[]{:S(2)}, u32[]{:S(2)}) collective-permute-start(bf16[64,512]{1,0:T(8,128)(2,1)S(1)} %stack.1.refs_0_), channel_id=1, source_target_pairs={{0,1},{1,2},{2,3},{3,0},{4,5},{5,6},{6,7},{7,4},{8,9},{9,10},{10,1... | collective-permute-start | bytes 196616 | tf_op jit(solution)/shard_map/ppermute | solution.py:184
  28.4 8.5 %collective-permute-start.15 = (bf16[64,512]{1,0:T(8,128)(2,1)S(1)}, bf16[64,512]{1,0:T(8,128)(2,1)S(1)}, u32[]{:S(2)}, u32[]{:S(2)}) collective-permute-start(bf16[64,512]{1,0:T(8,128)(2,1)S(1)} %stack.1.refs_0_), channel_id=1, source_target_pairs={{0,2},{1,3},{2,0},{3,1},{4,6},{5,7},{6,4},{7,5},{8,10},{9,11},{10,... | collective-permute-start | bytes 196616 | tf_op jit(solution)/shard_map/ppermute | solution.py:184
  30.0 8.3 %collective-permute-start.16 = (bf16[64,512]{1,0:T(8,128)(2,1)S(1)}, bf16[64,512]{1,0:T(8,128)(2,1)S(1)}, u32[]{:S(2)}, u32[]{:S(2)}) collective-permute-start(bf16[64,512]{1,0:T(8,128)(2,1)S(1)} %stack.1.refs_0_), channel_id=1, source_target_pairs={{0,3},{1,0},{2,1},{3,2},{4,7},{5,4},{6,5},{7,6},{8,11},{9,8},{10,9... | collective-permute-start | bytes 196616 | tf_op jit(solution)/shard_map/ppermute | solution.py:184
  31.8 8.0 %collective-permute-start.11 = (bf16[64,512]{1,0:T(8,128)(2,1)S(1)}, bf16[64,512]{1,0:T(8,128)(2,1)S(1)}, u32[]{:S(2)}, u32[]{:S(2)}) collective-permute-start(bf16[64,512]{1,0:T(8,128)(2,1)S(1)} %get-tuple-element.42), channel_id=1, source_target_pairs={{0,1},{1,2},{2,3},{3,0},{4,5},{5,6},{6,7},{7,4},{8,9},{9,10},{10,1... | collective-permute-start | bytes 196616 | tf_op jit(solution)/shard_map/ppermute | solution.py:184
  33.0 10.7 %collective-permute-start.12 = (bf16[64,512]{1,0:T(8,128)(2,1)S(1)}, bf16[64,512]{1,0:T(8,128)(2,1)S(1)}, u32[]{:S(2)}, u32[]{:S(2)}) collective-permute-start(bf16[64,512]{1,0:T(8,128)(2,1)S(1)} %get-tuple-element.43), channel_id=1, source_target_pairs={{0,2},{1,3},{2,0},{3,1},{4,6},{5,7},{6,4},{7,5},{8,10},{9,11},{10,... | collective-permute-start | bytes 196616 | tf_op jit(solution)/shard_map/ppermute | solution.py:184
  34.3 9.5 %collective-permute-start.13 = (bf16[64,512]{1,0:T(8,128)(2,1)S(1)}, bf16[64,512]{1,0:T(8,128)(2,1)S(1)}, u32[]{:S(2)}, u32[]{:S(2)}) collective-permute-start(bf16[64,512]{1,0:T(8,128)(2,1)S(1)} %get-tuple-element.44), channel_id=1, source_target_pairs={{0,3},{1,0},{2,1},{3,2},{4,7},{5,4},{6,5},{7,6},{8,11},{9,8},{10,9... | collective-permute-start | bytes 196616 | tf_op jit(solution)/shard_map/ppermute | solution.py:184
  38.3 2.3 %collective-permute-start.10 = (bf16[4,192,512]{2,1,0:T(8,128)(2,1)S(1)}, bf16[4,192,512]{2,1,0:T(8,128)(2,1)S(1)}, u32[]{:S(2)}, u32[]{:S(2)}) collective-permute-start(bf16[4,192,512]{2,1,0:T(8,128)(2,1)S(1)} %all-to-all-done.mine), channel_id=1, source_target_pairs={{0,4},{4,0},{8,12},{12,8},{16,20},{20,16},{24,28},{28,24},{1,5},{5... | collective-permute-start | bytes 2359304 | tf_op jit(solution)/shard_map/ppermute | solution.py:348
  38.4 6.0 %collective-permute-start.17 = (bf16[64,512]{1,0:T(8,128)(2,1)S(1)}, bf16[64,512]{1,0:T(8,128)(2,1)S(1)}, u32[]{:S(2)}, u32[]{:S(2)}) collective-permute-start(bf16[64,512]{1,0:T(8,128)(2,1)S(1)} %get-tuple-element.51), channel_id=1, source_target_pairs={{0,8},{4,12},{8,0},{12,4},{16,24},{20,28},{24,16},{28,20},{1,9},{5... | collective-permute-start | bytes 196616 | tf_op jit(solution)/shard_map/ppermute | solution.py:348
  39.9 4.5 %collective-permute-start.18 = (bf16[64,512]{1,0:T(8,128)(2,1)S(1)}, bf16[64,512]{1,0:T(8,128)(2,1)S(1)}, u32[]{:S(2)}, u32[]{:S(2)}) collective-permute-start(bf16[64,512]{1,0:T(8,128)(2,1)S(1)} %get-tuple-element.52), channel_id=1, source_target_pairs={{0,16},{4,20},{8,24},{12,28},{16,0},{20,4},{24,8},{28,12},{1,17},{... | collective-permute-start | bytes 196616 | tf_op jit(solution)/shard_map/ppermute | solution.py:348
  40.6 5.2 %collective-permute-start.19 = (bf16[64,512]{1,0:T(8,128)(2,1)S(1)}, bf16[64,512]{1,0:T(8,128)(2,1)S(1)}, u32[]{:S(2)}, u32[]{:S(2)}) collective-permute-start(bf16[64,512]{1,0:T(8,128)(2,1)S(1)} %get-tuple-element.53), channel_id=1, source_target_pairs={{0,24},{4,28},{8,16},{12,20},{16,8},{20,12},{24,0},{28,4},{1,25},{... | collective-permute-start | bytes 196616 | tf_op jit(solution)/shard_map/ppermute | solution.py:348

commit v7 on v6

--- a/solution.py
+++ b/solution.py
@@ -136,7 +136,7 @@
     map_grad_ref[...] = (hidden_grad[...] * gate * (1.0 + first_map * (1.0 - gate))).astype(BF16)
 
 
-def grad_sum(pairs, o_ref, left, right):
+def grad_sum(pairs, o_ref, left, right, begin=None):
     for n, (x, g) in enumerate(pairs):
         cells = pl.ds(n * CELLS, CELLS)
         ins, outs = x.shape[0], g.shape[0]
@@ -151,7 +151,8 @@
     )
     for ab in range(9):
         for e in range(3):
-            o_ref[ab * 3 + e] = acc[ab * outs : (ab + 1) * outs, e * ins : (e + 1) * ins]
+            out = acc[ab * outs : (ab + 1) * outs, e * ins : (e + 1) * ins]
+            o_ref[ab * 3 + e] = out if begin is None else out + begin[ab * 3 + e]
 
 
 def grad_kernel(at, x_ref, g_ref, o_ref, left, right):
@@ -323,16 +324,17 @@
     grad_sum(pairs, *rest)
 
 
-def first_grad_kernel(mine, other, *refs):
-    maps, rest = refs[:-3], refs[-3:]
+def first_grad_kernel(steps, mine, other, *refs):
+    count = len(steps)
+    maps, begin, rest = refs[:count], refs[count:-3], refs[-3:]
     rows, ins = rest[0].shape[1:]
     pairs = []
-    for step, g in enumerate(maps):
+    for step, g in zip(steps, maps):
         chip = (lax.axis_index("sample") >> 1) ^ step
         for core, v in enumerate((mine, other)):
             at = core * rows
             pairs.append((v[chip, ins : 2 * ins, :], g[at : at + rows, :]))
-    grad_sum(pairs, *rest)
+    grad_sum(pairs, *rest, *begin)
 
 
 def body(samples, chans, snapshots, first_weight, second_weight, cotangent):
@@ -355,6 +357,7 @@
     )
     cells = exchange(cells, chans)
     cots = exchange([cotangent[0]] * chans, chans)
+    cots[1], *cells = lax.optimization_barrier((cots[1], *cells))
     x, *parts = call(
         run(input_kernel), [piece] * (chans + 1), [first_w] + cells, patches, "first", 1.0
     )
@@ -391,15 +394,23 @@
     routed = call(run(route_kernel), [piece] * chips, map_grads, patches[1:], "route", 15.0)
     map_grads = chip_hops(routed)
     pieces = [pieces, hop(pieces, 1)]
-    scratch = [
-        pltpu.VMEM((9 * outs, samples * CELLS), BF16),
-        pltpu.VMEM((3 * ins, samples * CELLS), BF16),
-    ]
-    out = [((27, outs, ins), F32)]
-    second_grad = call(second_grad_kernel, out, pieces, scratch, "grad", 1.7)[0]
+    def grad_call(kernel, args, count):
+        scratch = [
+            pltpu.VMEM((9 * outs, count * CELLS), BF16),
+            pltpu.VMEM((3 * ins, count * CELLS), BF16),
+        ]
+        us = 0.3
+        return call(kernel, [((27, outs, ins), F32)], args, scratch, "grad", us)[0]
+
+    second_grad = grad_call(second_grad_kernel, pieces, samples)
     second_grad, *parts = lax.optimization_barrier((second_grad, *parts))
-    second_out = call(total_kernel, [piece], parts, (), "total", 0.5)[0]
-    first_grad = call(first_grad_kernel, out, pieces + map_grads, scratch, "grad", 1.7)[0]
+    second_out = call(total_kernel, [piece], parts, (), "total", 0.1)[0]
+    first_grad = []
+    for steps in (range(chips - 1), [chips - 1]):
+        args = pieces + [map_grads[d] for d in steps] + first_grad
+        kernel = functools.partial(first_grad_kernel, tuple(steps))
+        first_grad = [grad_call(kernel, args, 2 * len(steps))]
+    first_grad = first_grad[0]
     return (
         second_out[None],
         first_grad.transpose(2, 0, 1),

time: 47.9 us -> 47.2 us (0.985)
  waiting for transfers between devices: 5.36 us -> 4.21 us
  local copies, waits for them, and re-layouts: 0.84 us -> 1.95 us
  starting transfers between devices: 32 us -> 30.9 us
    unnamed x8, local copies, waits for them, and re-layouts: 0.84 us -> 1.95 us
    ppermute x15, starting transfers between devices: 24.7 us -> 23.7 us  [send(): lax.ppermute(v, 'chan', [(k, (k + step) % size) for k in range(size)])]
    ppermute x5, waiting for transfers between devices: 1.77 us -> 0.98 us  [body(): lax.ppermute(v, 'sample', [(s, s ^ step) for s in range(samples)])]
    pallas_call x12 -> x13, Pallas kernels: 8.55 us -> 8.91 us  [call(): pl.pallas_call(kernel, out_shape=[jax.ShapeDtypeStruct(shape, dtype) for...]
  transfers between devices with their start and end apart: 21 -> 21, of which waited for: 5 -> 6; matrix products, arithmetic and copies ran while one was open for 0% -> 0% of each run, Pallas kernels for 14% -> 16%
where the time goes in v7:
time: 47.2 us; the launch traced here: 46.7 us
  starting transfers between devices  30.9 us (65%)
  Pallas kernels  8.91 us (19%)
  waiting for transfers between devices  4.21 us (9%)
  local copies, waits for them, and re-layouts  1.95 us (4%)
  between operations  0.74 us (2%)
    ppermute x15, starting transfers between devices, send(): lax.ppermute(v, 'chan', [(k, (k + step) % size) for k in range(size)])  23.7 us
    pallas_call x13, Pallas kernels, call(): pl.pallas_call(kernel, out_shape=[jax.ShapeDtypeStruct(shape, dtype) for...  8.91 us
    all_to_all x1, starting transfers between devices, body(): lax.all_to_all(pieces, 'sample', 0, 0, axis_index_groups=cores, tiled=True)  3.72 us
    ppermute x5, starting transfers between devices, body(): lax.ppermute(v, 'sample', [(s, s ^ step) for s in range(samples)])  3.53 us
    unnamed x8, local copies, waits for them, and re-layouts  1.95 us
    ppermute x15, waiting for transfers between devices, send(): lax.ppermute(v, 'chan', [(k, (k + step) % size) for k in range(size)])  1.74 us
    all_to_all x1, waiting for transfers between devices, body(): lax.all_to_all(pieces, 'sample', 0, 0, axis_index_groups=cores, tiled=True)  1.49 us
    ppermute x5, waiting for transfers between devices, body(): lax.ppermute(v, 'sample', [(s, s ^ step) for s in range(samples)])  0.98 us
  transfers between devices with their start and end apart: 21, of which 6 were waited for; matrix products, arithmetic and copies ran while one was open for 0% of the time, Pallas kernels for 16%

profile of v7, /device:TPU:0, one launch (start us, length us, event | category | flops | bytes accessed | tf_op | source)
XLA Modules:
  0.0 46.7 jit_solution(17981065191106128956)
XLA Ops:
  0.6 3.1 %collective-permute-start = (bf16[64,512]{1,0:T(8,128)(2,1)}, bf16[64,512]{1,0:T(8,128)(2,1)S(1)}, u32[]{:S(2)}, u32[]{:S(2)}) collective-permute-start(bf16[64,512]{1,0:T(8,128)(2,1)} %bitcast.11), channel_id=1, source_target_pairs={{0,1},{1,2},{2,3},{3,0},{4,5},{5,6},{6,7},{7,4},{8,9},{9,10},{10,1... | collective-permute-start | bytes 196616 | tf_op jit(solution)/shard_map/ppermute | solution.py:185
  3.7 0.8 %copy-done.2 = bf16[1,256,128]{2,1,0:T(8,128)(2,1)S(1)} copy-done((bf16[1,256,128]{2,1,0:T(8,128)(2,1)S(1)}, bf16[1,256,128]{2,1,0:T(8,128)(2,1)}, u32[]{:S(2)}) %copy-start.2) | copy-done | bytes 65560
  4.6 1.6 %collective-permute-start.1 = (bf16[64,128]{1,0:T(8,128)(2,1)S(1)}, bf16[64,128]{1,0:T(8,128)(2,1)S(1)}, u32[]{:S(2)}, u32[]{:S(2)}) collective-permute-start(bf16[64,128]{1,0:T(8,128)(2,1)S(1)} %get-tuple-element.35), channel_id=1, source_target_pairs={{0,1},{1,2},{2,3},{3,0},{4,5},{5,6},{6,7},{7,4},{8,9},{9,10},{10,1... | collective-permute-start | bytes 49160 | tf_op jit(solution)/shard_map/ppermute | solution.py:185
  6.2 1.1 %collective-permute-start.2 = (bf16[64,128]{1,0:T(8,128)(2,1)S(1)}, bf16[64,128]{1,0:T(8,128)(2,1)S(1)}, u32[]{:S(2)}, u32[]{:S(2)}) collective-permute-start(bf16[64,128]{1,0:T(8,128)(2,1)S(1)} %get-tuple-element.36), channel_id=1, source_target_pairs={{0,2},{1,3},{2,0},{3,1},{4,6},{5,7},{6,4},{7,5},{8,10},{9,11},{10,... | collective-permute-start | bytes 49160 | tf_op jit(solution)/shard_map/ppermute | solution.py:185
  7.3 2.8 %collective-permute-start.3 = (bf16[64,128]{1,0:T(8,128)(2,1)S(1)}, bf16[64,128]{1,0:T(8,128)(2,1)S(1)}, u32[]{:S(2)}, u32[]{:S(2)}) collective-permute-start(bf16[64,128]{1,0:T(8,128)(2,1)S(1)} %get-tuple-element.37), channel_id=1, source_target_pairs={{0,3},{1,0},{2,1},{3,2},{4,7},{5,4},{6,5},{7,6},{8,11},{9,8},{10,9... | collective-permute-start | bytes 49160 | tf_op jit(solution)/shard_map/ppermute | solution.py:185
  10.1 0.3 collective-permute-start.4
  10.5 1.2 %collective-permute-start.5 = (bf16[64,512]{1,0:T(8,128)(2,1)S(1)}, bf16[64,512]{1,0:T(8,128)(2,1)S(1)}, u32[]{:S(2)}, u32[]{:S(2)}) collective-permute-start(bf16[64,512]{1,0:T(8,128)(2,1)S(1)} %bitcast.13), channel_id=1, source_target_pairs={{0,3},{1,0},{2,1},{3,2},{4,7},{5,4},{6,5},{7,6},{8,11},{9,8},{10,9... | collective-permute-start | bytes 196616 | tf_op jit(solution)/shard_map/ppermute | solution.py:185
  11.7 0.9 %first.1 = (bf16[64,512]{1,0:T(8,128)(2,1)S(1)}, bf16[64,512]{1,0:T(8,128)(2,1)S(1)}, bf16[64,512]{1,0:T(8,128)(2,1)S(1)}, bf16[64,512]{1,0:T(8,128)(2,1)S(1)}, bf16[64,512]{1,0:T(8,128)(2,1)S(1)}) custom-call(bf16[27,64,256]{2,1,0:T(8,128)(2,1)S(1)} %bitcast.7, bf16[64,128]{1,0:T(8,128)(2,1)S(1)} %get-tuple-element.39.refs_0_, ...), custom_call_target="tpu_custom_call" | custom-call | flops 1100000000 | bytes 3000000 | tf_op jit(solution)/shard_map/first/pallas_call | solution.py:37
  12.6 1.2 %collective-permute-start.6 = (bf16[64,512]{1,0:T(8,128)(2,1)S(1)}, bf16[64,512]{1,0:T(8,128)(2,1)S(1)}, u32[]{:S(2)}, u32[]{:S(2)}) collective-permute-start(bf16[64,512]{1,0:T(8,128)(2,1)S(1)} %get-tuple-element.44), channel_id=1, source_target_pairs={{0,1},{1,2},{2,3},{3,0},{4,5},{5,6},{6,7},{7,4},{8,9},{9,10},{10,1... | collective-permute-start | bytes 196616 | tf_op jit(solution)/shard_map/ppermute | solution.py:185
  13.8 3.4 %collective-permute-start.7 = (bf16[64,512]{1,0:T(8,128)(2,1)S(1)}, bf16[64,512]{1,0:T(8,128)(2,1)S(1)}, u32[]{:S(2)}, u32[]{:S(2)}) collective-permute-start(bf16[64,512]{1,0:T(8,128)(2,1)S(1)} %get-tuple-element.45), channel_id=1, source_target_pairs={{0,2},{1,3},{2,0},{3,1},{4,6},{5,7},{6,4},{7,5},{8,10},{9,11},{10,... | collective-permute-start | bytes 196616 | tf_op jit(solution)/shard_map/ppermute | solution.py:185
  17.2 1.1 %copy-done.1 = bf16[64,27,256]{2,0,1:T(8,128)(2,1)S(1)} copy-done((bf16[64,27,256]{2,0,1:T(8,128)(2,1)S(1)}, bf16[64,27,256]{2,0,1:T(8,128)(2,1)}, u32[]{:S(2)}) %copy-start.1) | copy-done | bytes 884760
  18.4 1.5 %spread.1.hidden_grad = f32[64,512]{1,0:T(8,128)S(1)} custom-call(bf16[27,64,256]{2,1,0:T(8,128)(2,1)S(1)} %bitcast.8, bf16[256,512]{1,0:T(8,128)(2,1)S(1)} %join.1.g_ref.full), custom_call_target="tpu_custom_call" | custom-call | flops 1650000000 | bytes 4500000 | tf_op jit(solution)/shard_map/spread/pallas_call | solution.py:37
  19.9 1.0 %collective-permute-done.7.refs_2_ = bf16[64,512]{1,0:T(8,128)(2,1)S(1)} collective-permute-done((bf16[64,512]{1,0:T(8,128)(2,1)S(1)}, bf16[64,512]{1,0:T(8,128)(2,1)S(1)}, u32[]{:S(2)}, u32[]{:S(2)}) %collective-permute-start.7) | collective-permute-done | bytes 65568 | tf_op jit(solution)/shard_map/ppermute | solution.py:185
  20.9 0.7 %collective-permute-done.8.refs_3_ = bf16[64,512]{1,0:T(8,128)(2,1)S(1)} collective-permute-done((bf16[64,512]{1,0:T(8,128)(2,1)S(1)}, bf16[64,512]{1,0:T(8,128)(2,1)S(1)}, u32[]{:S(2)}, u32[]{:S(2)}) %collective-permute-start.8) | collective-permute-done | bytes 65568 | tf_op jit(solution)/shard_map/ppermute | solution.py:185
  21.8 1.0 %pieces.1 = bf16[4,192,512]{2,1,0:T(8,128)(2,1)} custom-call(bf16[64,512]{1,0:T(8,128)(2,1)S(1)} %get-tuple-element.47.hidden.v_ref, bf16[64,512]{1,0:T(8,128)(2,1)S(1)} %get-tuple-element.48.x, bf16[256,512]{1,0:T(8,128)(2,1)S(1)} %join.1.g_ref.full), custom_call_target="tpu_custom_call" | custom-call | flops 880000000 | bytes 2400000 | tf_op jit(solution)/shard_map/pieces/pallas_call | solution.py:37
  23.0 3.7 %all-to-all-start = ((bf16[4,192,512]{2,1,0:T(8,128)(2,1)}), bf16[4,192,512]{2,1,0:T(8,128)(2,1)S(1)}, u32[]{:S(2)}, u32[]{:S(2)}) async-start(bf16[4,192,512]{2,1,0:T(8,128)(2,1)} %pieces.1), calls=%async_computation | async-start | bytes 1572864 | tf_op jit(solution)/shard_map/all_to_all | solution.py:393
  26.7 0.6 %collective-permute-start.14 = (bf16[64,512]{1,0:T(8,128)(2,1)S(1)}, bf16[64,512]{1,0:T(8,128)(2,1)S(1)}, u32[]{:S(2)}, u32[]{:S(2)}) collective-permute-start(bf16[64,512]{1,0:T(8,128)(2,1)S(1)} %stack.1.refs_0_), channel_id=1, source_target_pairs={{0,1},{1,2},{2,3},{3,0},{4,5},{5,6},{6,7},{7,4},{8,9},{9,10},{10,1... | collective-permute-start | bytes 196616 | tf_op jit(solution)/shard_map/ppermute | solution.py:185
  27.3 2.3 %collective-permute-start.15 = (bf16[64,512]{1,0:T(8,128)(2,1)S(1)}, bf16[64,512]{1,0:T(8,128)(2,1)S(1)}, u32[]{:S(2)}, u32[]{:S(2)}) collective-permute-start(bf16[64,512]{1,0:T(8,128)(2,1)S(1)} %stack.1.refs_0_), channel_id=1, source_target_pairs={{0,2},{1,3},{2,0},{3,1},{4,6},{5,7},{6,4},{7,5},{8,10},{9,11},{10,... | collective-permute-start | bytes 196616 | tf_op jit(solution)/shard_map/ppermute | solution.py:185
  29.7 0.9 %collective-permute-start.16 = (bf16[64,512]{1,0:T(8,128)(2,1)S(1)}, bf16[64,512]{1,0:T(8,128)(2,1)S(1)}, u32[]{:S(2)}, u32[]{:S(2)}) collective-permute-start(bf16[64,512]{1,0:T(8,128)(2,1)S(1)} %stack.1.refs_0_), channel_id=1, source_target_pairs={{0,3},{1,0},{2,1},{3,2},{4,7},{5,4},{6,5},{7,6},{8,11},{9,8},{10,9... | collective-permute-start | bytes 196616 | tf_op jit(solution)/shard_map/ppermute | solution.py:185
  30.6 0.9 %second.1 = (bf16[64,512]{1,0:T(8,128)(2,1)S(1)}, bf16[64,512]{1,0:T(8,128)(2,1)S(1)}, bf16[64,512]{1,0:T(8,128)(2,1)S(1)}, bf16[64,512]{1,0:T(8,128)(2,1)S(1)}) custom-call(bf16[27,64,256]{2,1,0:T(8,128)(2,1)S(1)} %bitcast.9, bf16[64,512]{1,0:T(8,128)(2,1)S(1)} %get-tuple-element.47.hidden.v_ref), custom_call_target="tpu_custom_call" | custom-call | flops 990000000 | bytes 2700000 | tf_op jit(solution)/shard_map/second/pallas_call | solution.py:37
  31.5 1.2 %collective-permute-start.11 = (bf16[64,512]{1,0:T(8,128)(2,1)S(1)}, bf16[64,512]{1,0:T(8,128)(2,1)S(1)}, u32[]{:S(2)}, u32[]{:S(2)}) collective-permute-start(bf16[64,512]{1,0:T(8,128)(2,1)S(1)} %get-tuple-element.52), channel_id=1, source_target_pairs={{0,1},{1,2},{2,3},{3,0},{4,5},{5,6},{6,7},{7,4},{8,9},{9,10},{10,1... | collective-permute-start | bytes 196616 | tf_op jit(solution)/shard_map/ppermute | solution.py:185
  32.7 1.0 %collective-permute-start.12 = (bf16[64,512]{1,0:T(8,128)(2,1)S(1)}, bf16[64,512]{1,0:T(8,128)(2,1)S(1)}, u32[]{:S(2)}, u32[]{:S(2)}) collective-permute-start(bf16[64,512]{1,0:T(8,128)(2,1)S(1)} %get-tuple-element.53), channel_id=1, source_target_pairs={{0,2},{1,3},{2,0},{3,1},{4,6},{5,7},{6,4},{7,5},{8,10},{9,11},{10,... | collective-permute-start | bytes 196616 | tf_op jit(solution)/shard_map/ppermute | solution.py:185
  33.7 2.8 %collective-permute-start.13 = (bf16[64,512]{1,0:T(8,128)(2,1)S(1)}, bf16[64,512]{1,0:T(8,128)(2,1)S(1)}, u32[]{:S(2)}, u32[]{:S(2)}) collective-permute-start(bf16[64,512]{1,0:T(8,128)(2,1)S(1)} %get-tuple-element.54), channel_id=1, source_target_pairs={{0,3},{1,0},{2,1},{3,2},{4,7},{5,4},{6,5},{7,6},{8,11},{9,8},{10,9... | collective-permute-start | bytes 196616 | tf_op jit(solution)/shard_map/ppermute | solution.py:185
  36.5 1.5 %all-to-all-done.mine = bf16[4,192,512]{2,1,0:T(8,128)(2,1)S(1)} async-done(((bf16[4,192,512]{2,1,0:T(8,128)(2,1)}), bf16[4,192,512]{2,1,0:T(8,128)(2,1)S(1)}, u32[]{:S(2)}, u32[]{:S(2)}) %all-to-all-start) | async-done | bytes 786464 | tf_op jit(solution)/shard_map/all_to_all | solution.py:393
  38.1 1.5 %collective-permute-start.18 = (bf16[64,512]{1,0:T(8,128)(2,1)S(1)}, bf16[64,512]{1,0:T(8,128)(2,1)S(1)}, u32[]{:S(2)}, u32[]{:S(2)}) collective-permute-start(bf16[64,512]{1,0:T(8,128)(2,1)S(1)} %get-tuple-element.62), channel_id=1, source_target_pairs={{0,8},{4,12},{8,0},{12,4},{16,24},{20,28},{24,16},{28,20},{1,9},{5... | collective-permute-start | bytes 196616 | tf_op jit(solution)/shard_map/ppermute | solution.py:350
  39.6 0.6 %collective-permute-start.19 = (bf16[64,512]{1,0:T(8,128)(2,1)S(1)}, bf16[64,512]{1,0:T(8,128)(2,1)S(1)}, u32[]{:S(2)}, u32[]{:S(2)}) collective-permute-start(bf16[64,512]{1,0:T(8,128)(2,1)S(1)} %get-tuple-element.63), channel_id=1, source_target_pairs={{0,16},{4,20},{8,24},{12,28},{16,0},{20,4},{24,8},{28,12},{1,17},{... | collective-permute-start | bytes 196616 | tf_op jit(solution)/shard_map/ppermute | solution.py:350
  40.3 1.4 %collective-permute-start.17 = (bf16[64,512]{1,0:T(8,128)(2,1)S(1)}, bf16[64,512]{1,0:T(8,128)(2,1)S(1)}, u32[]{:S(2)}, u32[]{:S(2)}) collective-permute-start(bf16[64,512]{1,0:T(8,128)(2,1)S(1)} %get-tuple-element.60), channel_id=1, source_target_pairs={{0,24},{4,28},{8,16},{12,20},{16,8},{20,12},{24,0},{28,4},{1,25},{... | collective-permute-start | bytes 196616 | tf_op jit(solution)/shard_map/ppermute | solution.py:350
  41.7 1.7 %grad.3 = f32[27,32,64]{2,1,0:T(8,128)} custom-call(bf16[4,192,512]{2,1,0:T(8,128)(2,1)S(1)} %all-to-all-done.mine, bf16[4,192,512]{2,1,0:T(8,128)(2,1)S(1)} %collective-permute-done.10.other), custom_call_target="tpu_custom_call" | custom-call | flops 330000000 | bytes 900000 | tf_op jit(solution)/shard_map/grad/pallas_call | solution.py:37
  43.4 0.7 %total.1 = bf16[64,512]{1,0:T(8,128)(2,1)} custom-call(bf16[64,512]{1,0:T(8,128)(2,1)S(1)} %get-tuple-element.55.refs_0_, bf16[64,512]{1,0:T(8,128)(2,1)S(1)} %collective-permute-done.11.refs_1_, bf16[64,512]{1,0:T(8,128)(2,1)S(1)} %collective-permute-done.12.refs_2_, bf16[64,512]{1,0:T(8,128)(2,1)S(1)} %collective-permute-done.13.refs_3_), custom_call_target="tpu_custom_call" | custom-call | flops 110000000 | bytes 300000 | tf_op jit(solution)/shard_map/total/pallas_call | solution.py:37
  44.1 0.8 %grad.4.refs_1_ = f32[27,32,64]{2,1,0:T(8,128)S(1)} custom-call(bf16[4,192,512]{2,1,0:T(8,128)(2,1)S(1)} %all-to-all-done.mine, bf16[4,192,512]{2,1,0:T(8,128)(2,1)S(1)} %collective-permute-done.10.other, bf16[64,512]{1,0:T(8,128)(2,1)S(1)} %get-tuple-element.61.refs_0_, bf16[64,512]{1,0:T(8,128)(2,1)S(1)} %collective-permute-done.18.refs_1_, ...), custom_call_target="tpu_custom_call" | custom-call | flops 330000000 | bytes 900000 | tf_op jit(solution)/shard_map/grad/pallas_call | solution.py:37
  44.9 0.6 %collective-permute-done.17.refs_0_ = bf16[64,512]{1,0:T(8,128)(2,1)S(1)} collective-permute-done((bf16[64,512]{1,0:T(8,128)(2,1)S(1)}, bf16[64,512]{1,0:T(8,128)(2,1)S(1)}, u32[]{:S(2)}, u32[]{:S(2)}) %collective-permute-start.17) | collective-permute-done | bytes 65568 | tf_op jit(solution)/shard_map/ppermute | solution.py:350
  45.5 1.3 %grad.5 = f32[27,32,64]{2,1,0:T(8,128)} custom-call(bf16[4,192,512]{2,1,0:T(8,128)(2,1)S(1)} %all-to-all-done.mine, bf16[4,192,512]{2,1,0:T(8,128)(2,1)S(1)} %collective-permute-done.10.other, bf16[64,512]{1,0:T(8,128)(2,1)S(1)} %collective-permute-done.17.refs_0_, f32[27,32,64]{2,1,0:T(8,128)S(1)} %grad.4.refs_1_), custom_call_target="tpu_custom_call" | custom-call | flops 330000000 | bytes 900000 | tf_op jit(solution)/shard_map/grad/pallas_call | solution.py:37
  (31 shorter events, 0.7 us)
Async XLA Ops:
  0.6 11.1 %collective-permute-start = (bf16[64,512]{1,0:T(8,128)(2,1)}, bf16[64,512]{1,0:T(8,128)(2,1)S(1)}, u32[]{:S(2)}, u32[]{:S(2)}) collective-permute-start(bf16[64,512]{1,0:T(8,128)(2,1)} %bitcast.11), channel_id=1, source_target_pairs={{0,1},{1,2},{2,3},{3,0},{4,5},{5,6},{6,7},{7,4},{8,9},{9,10},{10,1... | collective-permute-start | bytes 196616 | tf_op jit(solution)/shard_map/ppermute | solution.py:185
  3.7 0.8 %copy-start.2 = (bf16[1,256,128]{2,1,0:T(8,128)(2,1)S(1)}, bf16[1,256,128]{2,1,0:T(8,128)(2,1)}, u32[]{:S(2)}) copy-start(bf16[1,256,128]{2,1,0:T(8,128)(2,1)} %param.4) | copy-start | bytes 196612
  4.5 5.6 %copy-start.3 = (bf16[1,64,512]{2,1,0:T(8,128)(2,1)S(1)}, bf16[1,64,512]{2,1,0:T(8,128)(2,1)}, u32[]{:S(2)}) copy-start(bf16[1,64,512]{2,1,0:T(8,128)(2,1)} %param.7) | copy-start | bytes 196612
  4.5 7.1 %copy-start = (bf16[64,27,256]{2,0,1:T(8,128)(2,1)S(1)}, bf16[64,27,256]{2,0,1:T(8,128)(2,1)}, u32[]{:S(2)}) copy-start(bf16[64,27,256]{2,0,1:T(8,128)(2,1)} %param.5) | copy-start | bytes 2654212
  4.6 5.9 %collective-permute-start.1 = (bf16[64,128]{1,0:T(8,128)(2,1)S(1)}, bf16[64,128]{1,0:T(8,128)(2,1)S(1)}, u32[]{:S(2)}, u32[]{:S(2)}) collective-permute-start(bf16[64,128]{1,0:T(8,128)(2,1)S(1)} %get-tuple-element.35), channel_id=1, source_target_pairs={{0,1},{1,2},{2,3},{3,0},{4,5},{5,6},{6,7},{7,4},{8,9},{9,10},{10,1... | collective-permute-start | bytes 49160 | tf_op jit(solution)/shard_map/ppermute | solution.py:185
  6.2 5.5 %collective-permute-start.2 = (bf16[64,128]{1,0:T(8,128)(2,1)S(1)}, bf16[64,128]{1,0:T(8,128)(2,1)S(1)}, u32[]{:S(2)}, u32[]{:S(2)}) collective-permute-start(bf16[64,128]{1,0:T(8,128)(2,1)S(1)} %get-tuple-element.36), channel_id=1, source_target_pairs={{0,2},{1,3},{2,0},{3,1},{4,6},{5,7},{6,4},{7,5},{8,10},{9,11},{10,... | collective-permute-start | bytes 49160 | tf_op jit(solution)/shard_map/ppermute | solution.py:185
  7.3 4.4 %collective-permute-start.3 = (bf16[64,128]{1,0:T(8,128)(2,1)S(1)}, bf16[64,128]{1,0:T(8,128)(2,1)S(1)}, u32[]{:S(2)}, u32[]{:S(2)}) collective-permute-start(bf16[64,128]{1,0:T(8,128)(2,1)S(1)} %get-tuple-element.37), channel_id=1, source_target_pairs={{0,3},{1,0},{2,1},{3,2},{4,7},{5,4},{6,5},{7,6},{8,11},{9,8},{10,9... | collective-permute-start | bytes 49160 | tf_op jit(solution)/shard_map/ppermute | solution.py:185
  10.1 7.1 %collective-permute-start.4 = (bf16[64,512]{1,0:T(8,128)(2,1)S(1)}, bf16[64,512]{1,0:T(8,128)(2,1)S(1)}, u32[]{:S(2)}, u32[]{:S(2)}) collective-permute-start(bf16[64,512]{1,0:T(8,128)(2,1)S(1)} %bitcast.12), channel_id=1, source_target_pairs={{0,2},{1,3},{2,0},{3,1},{4,6},{5,7},{6,4},{7,5},{8,10},{9,11},{10,... | collective-permute-start | bytes 196616 | tf_op jit(solution)/shard_map/ppermute | solution.py:185
  10.5 6.7 %collective-permute-start.5 = (bf16[64,512]{1,0:T(8,128)(2,1)S(1)}, bf16[64,512]{1,0:T(8,128)(2,1)S(1)}, u32[]{:S(2)}, u32[]{:S(2)}) collective-permute-start(bf16[64,512]{1,0:T(8,128)(2,1)S(1)} %bitcast.13), channel_id=1, source_target_pairs={{0,3},{1,0},{2,1},{3,2},{4,7},{5,4},{6,5},{7,6},{8,11},{9,8},{10,9... | collective-permute-start | bytes 196616 | tf_op jit(solution)/shard_map/ppermute | solution.py:185
  12.6 7.3 %collective-permute-start.6 = (bf16[64,512]{1,0:T(8,128)(2,1)S(1)}, bf16[64,512]{1,0:T(8,128)(2,1)S(1)}, u32[]{:S(2)}, u32[]{:S(2)}) collective-permute-start(bf16[64,512]{1,0:T(8,128)(2,1)S(1)} %get-tuple-element.44), channel_id=1, source_target_pairs={{0,1},{1,2},{2,3},{3,0},{4,5},{5,6},{6,7},{7,4},{8,9},{9,10},{10,1... | collective-permute-start | bytes 196616 | tf_op jit(solution)/shard_map/ppermute | solution.py:185
  13.8 7.1 %collective-permute-start.7 = (bf16[64,512]{1,0:T(8,128)(2,1)S(1)}, bf16[64,512]{1,0:T(8,128)(2,1)S(1)}, u32[]{:S(2)}, u32[]{:S(2)}) collective-permute-start(bf16[64,512]{1,0:T(8,128)(2,1)S(1)} %get-tuple-element.45), channel_id=1, source_target_pairs={{0,2},{1,3},{2,0},{3,1},{4,6},{5,7},{6,4},{7,5},{8,10},{9,11},{10,... | collective-permute-start | bytes 196616 | tf_op jit(solution)/shard_map/ppermute | solution.py:185
  17.2 1.2 %copy-start.1 = (bf16[64,27,256]{2,0,1:T(8,128)(2,1)S(1)}, bf16[64,27,256]{2,0,1:T(8,128)(2,1)}, u32[]{:S(2)}) copy-start(bf16[64,27,256]{2,0,1:T(8,128)(2,1)} %param.6) | copy-start | bytes 2654212
  17.2 4.4 %collective-permute-start.8 = (bf16[64,512]{1,0:T(8,128)(2,1)S(1)}, bf16[64,512]{1,0:T(8,128)(2,1)S(1)}, u32[]{:S(2)}, u32[]{:S(2)}) collective-permute-start(bf16[64,512]{1,0:T(8,128)(2,1)S(1)} %get-tuple-element.46), channel_id=1, source_target_pairs={{0,3},{1,0},{2,1},{3,2},{4,7},{5,4},{6,5},{7,6},{8,11},{9,8},{10,9... | collective-permute-start | bytes 196616 | tf_op jit(solution)/shard_map/ppermute | solution.py:185
  21.7 1.3 %collective-permute-start.9 = (bf16[32,512]{1,0:T(8,128)(2,1)S(1)}, bf16[32,512]{1,0:T(8,128)(2,1)S(1)}, u32[]{:S(2)}, u32[]{:S(2)}) collective-permute-start(bf16[32,512]{1,0:T(8,128)(2,1)S(1)} %get-tuple-element.49), channel_id=1, source_target_pairs={{0,4},{4,0},{8,12},{12,8},{16,20},{20,16},{24,28},{28,24},{1,5},{5... | collective-permute-start | bytes 98312 | tf_op jit(solution)/shard_map/ppermute | solution.py:350
  23.0 15.0 %all-to-all-start = ((bf16[4,192,512]{2,1,0:T(8,128)(2,1)}), bf16[4,192,512]{2,1,0:T(8,128)(2,1)S(1)}, u32[]{:S(2)}, u32[]{:S(2)}) async-start(bf16[4,192,512]{2,1,0:T(8,128)(2,1)} %pieces.1), calls=%async_computation | async-start | bytes 1572864 | tf_op jit(solution)/shard_map/all_to_all | solution.py:393
  26.7 6.9 %collective-permute-start.14 = (bf16[64,512]{1,0:T(8,128)(2,1)S(1)}, bf16[64,512]{1,0:T(8,128)(2,1)S(1)}, u32[]{:S(2)}, u32[]{:S(2)}) collective-permute-start(bf16[64,512]{1,0:T(8,128)(2,1)S(1)} %stack.1.refs_0_), channel_id=1, source_target_pairs={{0,1},{1,2},{2,3},{3,0},{4,5},{5,6},{6,7},{7,4},{8,9},{9,10},{10,1... | collective-permute-start | bytes 196616 | tf_op jit(solution)/shard_map/ppermute | solution.py:185
  27.3 9.2 %collective-permute-start.15 = (bf16[64,512]{1,0:T(8,128)(2,1)S(1)}, bf16[64,512]{1,0:T(8,128)(2,1)S(1)}, u32[]{:S(2)}, u32[]{:S(2)}) collective-permute-start(bf16[64,512]{1,0:T(8,128)(2,1)S(1)} %stack.1.refs_0_), channel_id=1, source_target_pairs={{0,2},{1,3},{2,0},{3,1},{4,6},{5,7},{6,4},{7,5},{8,10},{9,11},{10,... | collective-permute-start | bytes 196616 | tf_op jit(solution)/shard_map/ppermute | solution.py:185
  29.7 8.3 %collective-permute-start.16 = (bf16[64,512]{1,0:T(8,128)(2,1)S(1)}, bf16[64,512]{1,0:T(8,128)(2,1)S(1)}, u32[]{:S(2)}, u32[]{:S(2)}) collective-permute-start(bf16[64,512]{1,0:T(8,128)(2,1)S(1)} %stack.1.refs_0_), channel_id=1, source_target_pairs={{0,3},{1,0},{2,1},{3,2},{4,7},{5,4},{6,5},{7,6},{8,11},{9,8},{10,9... | collective-permute-start | bytes 196616 | tf_op jit(solution)/shard_map/ppermute | solution.py:185
  31.5 8.0 %collective-permute-start.11 = (bf16[64,512]{1,0:T(8,128)(2,1)S(1)}, bf16[64,512]{1,0:T(8,128)(2,1)S(1)}, u32[]{:S(2)}, u32[]{:S(2)}) collective-permute-start(bf16[64,512]{1,0:T(8,128)(2,1)S(1)} %get-tuple-element.52), channel_id=1, source_target_pairs={{0,1},{1,2},{2,3},{3,0},{4,5},{5,6},{6,7},{7,4},{8,9},{9,10},{10,1... | collective-permute-start | bytes 196616 | tf_op jit(solution)/shard_map/ppermute | solution.py:185
  32.7 10.8 %collective-permute-start.12 = (bf16[64,512]{1,0:T(8,128)(2,1)S(1)}, bf16[64,512]{1,0:T(8,128)(2,1)S(1)}, u32[]{:S(2)}, u32[]{:S(2)}) collective-permute-start(bf16[64,512]{1,0:T(8,128)(2,1)S(1)} %get-tuple-element.53), channel_id=1, source_target_pairs={{0,2},{1,3},{2,0},{3,1},{4,6},{5,7},{6,4},{7,5},{8,10},{9,11},{10,... | collective-permute-start | bytes 196616 | tf_op jit(solution)/shard_map/ppermute | solution.py:185
  33.7 9.8 %collective-permute-start.13 = (bf16[64,512]{1,0:T(8,128)(2,1)S(1)}, bf16[64,512]{1,0:T(8,128)(2,1)S(1)}, u32[]{:S(2)}, u32[]{:S(2)}) collective-permute-start(bf16[64,512]{1,0:T(8,128)(2,1)S(1)} %get-tuple-element.54), channel_id=1, source_target_pairs={{0,3},{1,0},{2,1},{3,2},{4,7},{5,4},{6,5},{7,6},{8,11},{9,8},{10,9... | collective-permute-start | bytes 196616 | tf_op jit(solution)/shard_map/ppermute | solution.py:185
  38.0 2.3 %collective-permute-start.10 = (bf16[4,192,512]{2,1,0:T(8,128)(2,1)S(1)}, bf16[4,192,512]{2,1,0:T(8,128)(2,1)S(1)}, u32[]{:S(2)}, u32[]{:S(2)}) collective-permute-start(bf16[4,192,512]{2,1,0:T(8,128)(2,1)S(1)} %all-to-all-done.mine), channel_id=1, source_target_pairs={{0,4},{4,0},{8,12},{12,8},{16,20},{20,16},{24,28},{28,24},{1,5},{5... | collective-permute-start | bytes 2359304 | tf_op jit(solution)/shard_map/ppermute | solution.py:350
  38.1 6.0 %collective-permute-start.18 = (bf16[64,512]{1,0:T(8,128)(2,1)S(1)}, bf16[64,512]{1,0:T(8,128)(2,1)S(1)}, u32[]{:S(2)}, u32[]{:S(2)}) collective-permute-start(bf16[64,512]{1,0:T(8,128)(2,1)S(1)} %get-tuple-element.62), channel_id=1, source_target_pairs={{0,8},{4,12},{8,0},{12,4},{16,24},{20,28},{24,16},{28,20},{1,9},{5... | collective-permute-start | bytes 196616 | tf_op jit(solution)/shard_map/ppermute | solution.py:350
  39.6 4.5 %collective-permute-start.19 = (bf16[64,512]{1,0:T(8,128)(2,1)S(1)}, bf16[64,512]{1,0:T(8,128)(2,1)S(1)}, u32[]{:S(2)}, u32[]{:S(2)}) collective-permute-start(bf16[64,512]{1,0:T(8,128)(2,1)S(1)} %get-tuple-element.63), channel_id=1, source_target_pairs={{0,16},{4,20},{8,24},{12,28},{16,0},{20,4},{24,8},{28,12},{1,17},{... | collective-permute-start | bytes 196616 | tf_op jit(solution)/shard_map/ppermute | solution.py:350
  40.3 5.2 %collective-permute-start.17 = (bf16[64,512]{1,0:T(8,128)(2,1)S(1)}, bf16[64,512]{1,0:T(8,128)(2,1)S(1)}, u32[]{:S(2)}, u32[]{:S(2)}) collective-permute-start(bf16[64,512]{1,0:T(8,128)(2,1)S(1)} %get-tuple-element.60), channel_id=1, source_target_pairs={{0,24},{4,28},{8,16},{12,20},{16,8},{20,12},{24,0},{28,4},{1,25},{... | collective-permute-start | bytes 196616 | tf_op jit(solution)/shard_map/ppermute | solution.py:350

commit v8 on v7

--- a/solution.py
+++ b/solution.py
@@ -232,8 +232,9 @@
     copies, packed = lax.optimization_barrier((copies, packed))
     all_hidden = swap(copies, "sample")
     map_grads = exchange([map_grad] * chans, chans)
+    late, _ = lax.optimization_barrier((hidden, map_grads[1]))
     parts = exchange(
-        call(run(second_kernel), [piece] * chans, [second_w, hidden], patches, "second", 2.8), chans
+        call(run(second_kernel), [piece] * chans, [second_w, late], patches, "second", 2.8), chans
     )
     full_map_grad = call(run(join_kernel), [((full, CELLS), BF16)], map_grads, name="join")[0]
     full_map_grad, all_hidden = lax.optimization_barrier((full_map_grad, all_hidden))

time: 47.2 us -> 47.2 us (level)
  no operation moved by 1% of the time
where the time goes in v8:
time: 47.2 us; the launch traced here: 46.7 us
  starting transfers between devices  30.9 us (65%)
  Pallas kernels  8.91 us (19%)
  waiting for transfers between devices  4.21 us (9%)
  local copies, waits for them, and re-layouts  1.95 us (4%)
  between operations  0.74 us (2%)
    ppermute x15, starting transfers between devices, send(): lax.ppermute(v, 'chan', [(k, (k + step) % size) for k in range(size)])  23.7 us
    pallas_call x13, Pallas kernels, call(): pl.pallas_call(kernel, out_shape=[jax.ShapeDtypeStruct(shape, dtype) for...  8.91 us
    all_to_all x1, starting transfers between devices, body(): lax.all_to_all(pieces, 'sample', 0, 0, axis_index_groups=cores, tiled=True)  3.72 us
    ppermute x5, starting transfers between devices, body(): lax.ppermute(v, 'sample', [(s, s ^ step) for s in range(samples)])  3.53 us
    unnamed x8, local copies, waits for them, and re-layouts  1.95 us
    ppermute x15, waiting for transfers between devices, send(): lax.ppermute(v, 'chan', [(k, (k + step) % size) for k in range(size)])  1.74 us
    all_to_all x1, waiting for transfers between devices, body(): lax.all_to_all(pieces, 'sample', 0, 0, axis_index_groups=cores, tiled=True)  1.49 us
    ppermute x5, waiting for transfers between devices, body(): lax.ppermute(v, 'sample', [(s, s ^ step) for s in range(samples)])  0.98 us
  transfers between devices with their start and end apart: 21, of which 6 were waited for; matrix products, arithmetic and copies ran while one was open for 0% of the time, Pallas kernels for 16%

profile of v8, /device:TPU:0, one launch (start us, length us, event | category | flops | bytes accessed | tf_op | source)
XLA Modules:
  0.0 46.7 jit_solution(17981065191106128956)
XLA Ops:
  0.6 3.1 %collective-permute-start = (bf16[64,512]{1,0:T(8,128)(2,1)}, bf16[64,512]{1,0:T(8,128)(2,1)S(1)}, u32[]{:S(2)}, u32[]{:S(2)}) collective-permute-start(bf16[64,512]{1,0:T(8,128)(2,1)} %bitcast.11), channel_id=1, source_target_pairs={{0,1},{1,2},{2,3},{3,0},{4,5},{5,6},{6,7},{7,4},{8,9},{9,10},{10,1... | collective-permute-start | bytes 196616 | tf_op jit(solution)/shard_map/ppermute | solution.py:185
  3.7 0.8 %copy-done.2 = bf16[1,256,128]{2,1,0:T(8,128)(2,1)S(1)} copy-done((bf16[1,256,128]{2,1,0:T(8,128)(2,1)S(1)}, bf16[1,256,128]{2,1,0:T(8,128)(2,1)}, u32[]{:S(2)}) %copy-start.2) | copy-done | bytes 65560
  4.6 1.6 %collective-permute-start.1 = (bf16[64,128]{1,0:T(8,128)(2,1)S(1)}, bf16[64,128]{1,0:T(8,128)(2,1)S(1)}, u32[]{:S(2)}, u32[]{:S(2)}) collective-permute-start(bf16[64,128]{1,0:T(8,128)(2,1)S(1)} %get-tuple-element.35), channel_id=1, source_target_pairs={{0,1},{1,2},{2,3},{3,0},{4,5},{5,6},{6,7},{7,4},{8,9},{9,10},{10,1... | collective-permute-start | bytes 49160 | tf_op jit(solution)/shard_map/ppermute | solution.py:185
  6.2 1.1 %collective-permute-start.2 = (bf16[64,128]{1,0:T(8,128)(2,1)S(1)}, bf16[64,128]{1,0:T(8,128)(2,1)S(1)}, u32[]{:S(2)}, u32[]{:S(2)}) collective-permute-start(bf16[64,128]{1,0:T(8,128)(2,1)S(1)} %get-tuple-element.36), channel_id=1, source_target_pairs={{0,2},{1,3},{2,0},{3,1},{4,6},{5,7},{6,4},{7,5},{8,10},{9,11},{10,... | collective-permute-start | bytes 49160 | tf_op jit(solution)/shard_map/ppermute | solution.py:185
  7.3 2.8 %collective-permute-start.3 = (bf16[64,128]{1,0:T(8,128)(2,1)S(1)}, bf16[64,128]{1,0:T(8,128)(2,1)S(1)}, u32[]{:S(2)}, u32[]{:S(2)}) collective-permute-start(bf16[64,128]{1,0:T(8,128)(2,1)S(1)} %get-tuple-element.37), channel_id=1, source_target_pairs={{0,3},{1,0},{2,1},{3,2},{4,7},{5,4},{6,5},{7,6},{8,11},{9,8},{10,9... | collective-permute-start | bytes 49160 | tf_op jit(solution)/shard_map/ppermute | solution.py:185
  10.1 0.3 collective-permute-start.4
  10.5 1.2 %collective-permute-start.5 = (bf16[64,512]{1,0:T(8,128)(2,1)S(1)}, bf16[64,512]{1,0:T(8,128)(2,1)S(1)}, u32[]{:S(2)}, u32[]{:S(2)}) collective-permute-start(bf16[64,512]{1,0:T(8,128)(2,1)S(1)} %bitcast.13), channel_id=1, source_target_pairs={{0,3},{1,0},{2,1},{3,2},{4,7},{5,4},{6,5},{7,6},{8,11},{9,8},{10,9... | collective-permute-start | bytes 196616 | tf_op jit(solution)/shard_map/ppermute | solution.py:185
  11.7 0.9 %first.1 = (bf16[64,512]{1,0:T(8,128)(2,1)S(1)}, bf16[64,512]{1,0:T(8,128)(2,1)S(1)}, bf16[64,512]{1,0:T(8,128)(2,1)S(1)}, bf16[64,512]{1,0:T(8,128)(2,1)S(1)}, bf16[64,512]{1,0:T(8,128)(2,1)S(1)}) custom-call(bf16[27,64,256]{2,1,0:T(8,128)(2,1)S(1)} %bitcast.7, bf16[64,128]{1,0:T(8,128)(2,1)S(1)} %get-tuple-element.39.refs_0_, ...), custom_call_target="tpu_custom_call" | custom-call | flops 1100000000 | bytes 3000000 | tf_op jit(solution)/shard_map/first/pallas_call | solution.py:37
  12.6 1.2 %collective-permute-start.6 = (bf16[64,512]{1,0:T(8,128)(2,1)S(1)}, bf16[64,512]{1,0:T(8,128)(2,1)S(1)}, u32[]{:S(2)}, u32[]{:S(2)}) collective-permute-start(bf16[64,512]{1,0:T(8,128)(2,1)S(1)} %get-tuple-element.44), channel_id=1, source_target_pairs={{0,1},{1,2},{2,3},{3,0},{4,5},{5,6},{6,7},{7,4},{8,9},{9,10},{10,1... | collective-permute-start | bytes 196616 | tf_op jit(solution)/shard_map/ppermute | solution.py:185
  13.8 3.4 %collective-permute-start.7 = (bf16[64,512]{1,0:T(8,128)(2,1)S(1)}, bf16[64,512]{1,0:T(8,128)(2,1)S(1)}, u32[]{:S(2)}, u32[]{:S(2)}) collective-permute-start(bf16[64,512]{1,0:T(8,128)(2,1)S(1)} %get-tuple-element.45), channel_id=1, source_target_pairs={{0,2},{1,3},{2,0},{3,1},{4,6},{5,7},{6,4},{7,5},{8,10},{9,11},{10,... | collective-permute-start | bytes 196616 | tf_op jit(solution)/shard_map/ppermute | solution.py:185
  17.2 1.1 %copy-done.1 = bf16[64,27,256]{2,0,1:T(8,128)(2,1)S(1)} copy-done((bf16[64,27,256]{2,0,1:T(8,128)(2,1)S(1)}, bf16[64,27,256]{2,0,1:T(8,128)(2,1)}, u32[]{:S(2)}) %copy-start.1) | copy-done | bytes 884760
  18.4 1.5 %spread.1.hidden_grad = f32[64,512]{1,0:T(8,128)S(1)} custom-call(bf16[27,64,256]{2,1,0:T(8,128)(2,1)S(1)} %bitcast.8, bf16[256,512]{1,0:T(8,128)(2,1)S(1)} %join.1.g_ref.full), custom_call_target="tpu_custom_call" | custom-call | flops 1650000000 | bytes 4500000 | tf_op jit(solution)/shard_map/spread/pallas_call | solution.py:37
  19.9 1.0 %collective-permute-done.7.refs_2_ = bf16[64,512]{1,0:T(8,128)(2,1)S(1)} collective-permute-done((bf16[64,512]{1,0:T(8,128)(2,1)S(1)}, bf16[64,512]{1,0:T(8,128)(2,1)S(1)}, u32[]{:S(2)}, u32[]{:S(2)}) %collective-permute-start.7) | collective-permute-done | bytes 65568 | tf_op jit(solution)/shard_map/ppermute | solution.py:185
  20.9 0.7 %collective-permute-done.8.refs_3_ = bf16[64,512]{1,0:T(8,128)(2,1)S(1)} collective-permute-done((bf16[64,512]{1,0:T(8,128)(2,1)S(1)}, bf16[64,512]{1,0:T(8,128)(2,1)S(1)}, u32[]{:S(2)}, u32[]{:S(2)}) %collective-permute-start.8) | collective-permute-done | bytes 65568 | tf_op jit(solution)/shard_map/ppermute | solution.py:185
  21.8 1.0 %pieces.1 = bf16[4,192,512]{2,1,0:T(8,128)(2,1)} custom-call(bf16[64,512]{1,0:T(8,128)(2,1)S(1)} %get-tuple-element.47.hidden.v_ref, bf16[64,512]{1,0:T(8,128)(2,1)S(1)} %get-tuple-element.48.x, bf16[256,512]{1,0:T(8,128)(2,1)S(1)} %join.1.g_ref.full), custom_call_target="tpu_custom_call" | custom-call | flops 880000000 | bytes 2400000 | tf_op jit(solution)/shard_map/pieces/pallas_call | solution.py:37
  23.0 3.7 %all-to-all-start = ((bf16[4,192,512]{2,1,0:T(8,128)(2,1)}), bf16[4,192,512]{2,1,0:T(8,128)(2,1)S(1)}, u32[]{:S(2)}, u32[]{:S(2)}) async-start(bf16[4,192,512]{2,1,0:T(8,128)(2,1)} %pieces.1), calls=%async_computation | async-start | bytes 1572864 | tf_op jit(solution)/shard_map/all_to_all | solution.py:394
  26.7 0.6 %collective-permute-start.14 = (bf16[64,512]{1,0:T(8,128)(2,1)S(1)}, bf16[64,512]{1,0:T(8,128)(2,1)S(1)}, u32[]{:S(2)}, u32[]{:S(2)}) collective-permute-start(bf16[64,512]{1,0:T(8,128)(2,1)S(1)} %stack.1.refs_0_), channel_id=1, source_target_pairs={{0,1},{1,2},{2,3},{3,0},{4,5},{5,6},{6,7},{7,4},{8,9},{9,10},{10,1... | collective-permute-start | bytes 196616 | tf_op jit(solution)/shard_map/ppermute | solution.py:185
  27.3 2.3 %collective-permute-start.15 = (bf16[64,512]{1,0:T(8,128)(2,1)S(1)}, bf16[64,512]{1,0:T(8,128)(2,1)S(1)}, u32[]{:S(2)}, u32[]{:S(2)}) collective-permute-start(bf16[64,512]{1,0:T(8,128)(2,1)S(1)} %stack.1.refs_0_), channel_id=1, source_target_pairs={{0,2},{1,3},{2,0},{3,1},{4,6},{5,7},{6,4},{7,5},{8,10},{9,11},{10,... | collective-permute-start | bytes 196616 | tf_op jit(solution)/shard_map/ppermute | solution.py:185
  29.7 0.9 %collective-permute-start.16 = (bf16[64,512]{1,0:T(8,128)(2,1)S(1)}, bf16[64,512]{1,0:T(8,128)(2,1)S(1)}, u32[]{:S(2)}, u32[]{:S(2)}) collective-permute-start(bf16[64,512]{1,0:T(8,128)(2,1)S(1)} %stack.1.refs_0_), channel_id=1, source_target_pairs={{0,3},{1,0},{2,1},{3,2},{4,7},{5,4},{6,5},{7,6},{8,11},{9,8},{10,9... | collective-permute-start | bytes 196616 | tf_op jit(solution)/shard_map/ppermute | solution.py:185
  30.6 0.9 %second.1 = (bf16[64,512]{1,0:T(8,128)(2,1)S(1)}, bf16[64,512]{1,0:T(8,128)(2,1)S(1)}, bf16[64,512]{1,0:T(8,128)(2,1)S(1)}, bf16[64,512]{1,0:T(8,128)(2,1)S(1)}) custom-call(bf16[27,64,256]{2,1,0:T(8,128)(2,1)S(1)} %bitcast.9, bf16[64,512]{1,0:T(8,128)(2,1)S(1)} %get-tuple-element.47.hidden.v_ref), custom_call_target="tpu_custom_call" | custom-call | flops 990000000 | bytes 2700000 | tf_op jit(solution)/shard_map/second/pallas_call | solution.py:37
  31.5 1.2 %collective-permute-start.11 = (bf16[64,512]{1,0:T(8,128)(2,1)S(1)}, bf16[64,512]{1,0:T(8,128)(2,1)S(1)}, u32[]{:S(2)}, u32[]{:S(2)}) collective-permute-start(bf16[64,512]{1,0:T(8,128)(2,1)S(1)} %get-tuple-element.52), channel_id=1, source_target_pairs={{0,1},{1,2},{2,3},{3,0},{4,5},{5,6},{6,7},{7,4},{8,9},{9,10},{10,1... | collective-permute-start | bytes 196616 | tf_op jit(solution)/shard_map/ppermute | solution.py:185
  32.7 1.0 %collective-permute-start.12 = (bf16[64,512]{1,0:T(8,128)(2,1)S(1)}, bf16[64,512]{1,0:T(8,128)(2,1)S(1)}, u32[]{:S(2)}, u32[]{:S(2)}) collective-permute-start(bf16[64,512]{1,0:T(8,128)(2,1)S(1)} %get-tuple-element.53), channel_id=1, source_target_pairs={{0,2},{1,3},{2,0},{3,1},{4,6},{5,7},{6,4},{7,5},{8,10},{9,11},{10,... | collective-permute-start | bytes 196616 | tf_op jit(solution)/shard_map/ppermute | solution.py:185
  33.7 2.8 %collective-permute-start.13 = (bf16[64,512]{1,0:T(8,128)(2,1)S(1)}, bf16[64,512]{1,0:T(8,128)(2,1)S(1)}, u32[]{:S(2)}, u32[]{:S(2)}) collective-permute-start(bf16[64,512]{1,0:T(8,128)(2,1)S(1)} %get-tuple-element.54), channel_id=1, source_target_pairs={{0,3},{1,0},{2,1},{3,2},{4,7},{5,4},{6,5},{7,6},{8,11},{9,8},{10,9... | collective-permute-start | bytes 196616 | tf_op jit(solution)/shard_map/ppermute | solution.py:185
  36.5 1.5 %all-to-all-done.mine = bf16[4,192,512]{2,1,0:T(8,128)(2,1)S(1)} async-done(((bf16[4,192,512]{2,1,0:T(8,128)(2,1)}), bf16[4,192,512]{2,1,0:T(8,128)(2,1)S(1)}, u32[]{:S(2)}, u32[]{:S(2)}) %all-to-all-start) | async-done | bytes 786464 | tf_op jit(solution)/shard_map/all_to_all | solution.py:394
  38.1 1.5 %collective-permute-start.18 = (bf16[64,512]{1,0:T(8,128)(2,1)S(1)}, bf16[64,512]{1,0:T(8,128)(2,1)S(1)}, u32[]{:S(2)}, u32[]{:S(2)}) collective-permute-start(bf16[64,512]{1,0:T(8,128)(2,1)S(1)} %get-tuple-element.62), channel_id=1, source_target_pairs={{0,8},{4,12},{8,0},{12,4},{16,24},{20,28},{24,16},{28,20},{1,9},{5... | collective-permute-start | bytes 196616 | tf_op jit(solution)/shard_map/ppermute | solution.py:351
  39.6 0.6 %collective-permute-start.19 = (bf16[64,512]{1,0:T(8,128)(2,1)S(1)}, bf16[64,512]{1,0:T(8,128)(2,1)S(1)}, u32[]{:S(2)}, u32[]{:S(2)}) collective-permute-start(bf16[64,512]{1,0:T(8,128)(2,1)S(1)} %get-tuple-element.63), channel_id=1, source_target_pairs={{0,16},{4,20},{8,24},{12,28},{16,0},{20,4},{24,8},{28,12},{1,17},{... | collective-permute-start | bytes 196616 | tf_op jit(solution)/shard_map/ppermute | solution.py:351
  40.3 1.4 %collective-permute-start.17 = (bf16[64,512]{1,0:T(8,128)(2,1)S(1)}, bf16[64,512]{1,0:T(8,128)(2,1)S(1)}, u32[]{:S(2)}, u32[]{:S(2)}) collective-permute-start(bf16[64,512]{1,0:T(8,128)(2,1)S(1)} %get-tuple-element.60), channel_id=1, source_target_pairs={{0,24},{4,28},{8,16},{12,20},{16,8},{20,12},{24,0},{28,4},{1,25},{... | collective-permute-start | bytes 196616 | tf_op jit(solution)/shard_map/ppermute | solution.py:351
  41.7 1.7 %grad.3 = f32[27,32,64]{2,1,0:T(8,128)} custom-call(bf16[4,192,512]{2,1,0:T(8,128)(2,1)S(1)} %all-to-all-done.mine, bf16[4,192,512]{2,1,0:T(8,128)(2,1)S(1)} %collective-permute-done.10.other), custom_call_target="tpu_custom_call" | custom-call | flops 330000000 | bytes 900000 | tf_op jit(solution)/shard_map/grad/pallas_call | solution.py:37
  43.4 0.7 %total.1 = bf16[64,512]{1,0:T(8,128)(2,1)} custom-call(bf16[64,512]{1,0:T(8,128)(2,1)S(1)} %get-tuple-element.55.refs_0_, bf16[64,512]{1,0:T(8,128)(2,1)S(1)} %collective-permute-done.11.refs_1_, bf16[64,512]{1,0:T(8,128)(2,1)S(1)} %collective-permute-done.12.refs_2_, bf16[64,512]{1,0:T(8,128)(2,1)S(1)} %collective-permute-done.13.refs_3_), custom_call_target="tpu_custom_call" | custom-call | flops 110000000 | bytes 300000 | tf_op jit(solution)/shard_map/total/pallas_call | solution.py:37
  44.1 0.8 %grad.4.refs_1_ = f32[27,32,64]{2,1,0:T(8,128)S(1)} custom-call(bf16[4,192,512]{2,1,0:T(8,128)(2,1)S(1)} %all-to-all-done.mine, bf16[4,192,512]{2,1,0:T(8,128)(2,1)S(1)} %collective-permute-done.10.other, bf16[64,512]{1,0:T(8,128)(2,1)S(1)} %get-tuple-element.61.refs_0_, bf16[64,512]{1,0:T(8,128)(2,1)S(1)} %collective-permute-done.18.refs_1_, ...), custom_call_target="tpu_custom_call" | custom-call | flops 330000000 | bytes 900000 | tf_op jit(solution)/shard_map/grad/pallas_call | solution.py:37
  44.9 0.6 %collective-permute-done.17.refs_0_ = bf16[64,512]{1,0:T(8,128)(2,1)S(1)} collective-permute-done((bf16[64,512]{1,0:T(8,128)(2,1)S(1)}, bf16[64,512]{1,0:T(8,128)(2,1)S(1)}, u32[]{:S(2)}, u32[]{:S(2)}) %collective-permute-start.17) | collective-permute-done | bytes 65568 | tf_op jit(solution)/shard_map/ppermute | solution.py:351
  45.5 1.3 %grad.5 = f32[27,32,64]{2,1,0:T(8,128)} custom-call(bf16[4,192,512]{2,1,0:T(8,128)(2,1)S(1)} %all-to-all-done.mine, bf16[4,192,512]{2,1,0:T(8,128)(2,1)S(1)} %collective-permute-done.10.other, bf16[64,512]{1,0:T(8,128)(2,1)S(1)} %collective-permute-done.17.refs_0_, f32[27,32,64]{2,1,0:T(8,128)S(1)} %grad.4.refs_1_), custom_call_target="tpu_custom_call" | custom-call | flops 330000000 | bytes 900000 | tf_op jit(solution)/shard_map/grad/pallas_call | solution.py:37
  (31 shorter events, 0.7 us)
Async XLA Ops:
  0.6 11.1 %collective-permute-start = (bf16[64,512]{1,0:T(8,128)(2,1)}, bf16[64,512]{1,0:T(8,128)(2,1)S(1)}, u32[]{:S(2)}, u32[]{:S(2)}) collective-permute-start(bf16[64,512]{1,0:T(8,128)(2,1)} %bitcast.11), channel_id=1, source_target_pairs={{0,1},{1,2},{2,3},{3,0},{4,5},{5,6},{6,7},{7,4},{8,9},{9,10},{10,1... | collective-permute-start | bytes 196616 | tf_op jit(solution)/shard_map/ppermute | solution.py:185
  3.7 0.8 %copy-start.2 = (bf16[1,256,128]{2,1,0:T(8,128)(2,1)S(1)}, bf16[1,256,128]{2,1,0:T(8,128)(2,1)}, u32[]{:S(2)}) copy-start(bf16[1,256,128]{2,1,0:T(8,128)(2,1)} %param.4) | copy-start | bytes 196612
  4.5 5.6 %copy-start.3 = (bf16[1,64,512]{2,1,0:T(8,128)(2,1)S(1)}, bf16[1,64,512]{2,1,0:T(8,128)(2,1)}, u32[]{:S(2)}) copy-start(bf16[1,64,512]{2,1,0:T(8,128)(2,1)} %param.7) | copy-start | bytes 196612
  4.5 7.1 %copy-start = (bf16[64,27,256]{2,0,1:T(8,128)(2,1)S(1)}, bf16[64,27,256]{2,0,1:T(8,128)(2,1)}, u32[]{:S(2)}) copy-start(bf16[64,27,256]{2,0,1:T(8,128)(2,1)} %param.5) | copy-start | bytes 2654212
  4.6 5.9 %collective-permute-start.1 = (bf16[64,128]{1,0:T(8,128)(2,1)S(1)}, bf16[64,128]{1,0:T(8,128)(2,1)S(1)}, u32[]{:S(2)}, u32[]{:S(2)}) collective-permute-start(bf16[64,128]{1,0:T(8,128)(2,1)S(1)} %get-tuple-element.35), channel_id=1, source_target_pairs={{0,1},{1,2},{2,3},{3,0},{4,5},{5,6},{6,7},{7,4},{8,9},{9,10},{10,1... | collective-permute-start | bytes 49160 | tf_op jit(solution)/shard_map/ppermute | solution.py:185
  6.2 5.5 %collective-permute-start.2 = (bf16[64,128]{1,0:T(8,128)(2,1)S(1)}, bf16[64,128]{1,0:T(8,128)(2,1)S(1)}, u32[]{:S(2)}, u32[]{:S(2)}) collective-permute-start(bf16[64,128]{1,0:T(8,128)(2,1)S(1)} %get-tuple-element.36), channel_id=1, source_target_pairs={{0,2},{1,3},{2,0},{3,1},{4,6},{5,7},{6,4},{7,5},{8,10},{9,11},{10,... | collective-permute-start | bytes 49160 | tf_op jit(solution)/shard_map/ppermute | solution.py:185
  7.3 4.4 %collective-permute-start.3 = (bf16[64,128]{1,0:T(8,128)(2,1)S(1)}, bf16[64,128]{1,0:T(8,128)(2,1)S(1)}, u32[]{:S(2)}, u32[]{:S(2)}) collective-permute-start(bf16[64,128]{1,0:T(8,128)(2,1)S(1)} %get-tuple-element.37), channel_id=1, source_target_pairs={{0,3},{1,0},{2,1},{3,2},{4,7},{5,4},{6,5},{7,6},{8,11},{9,8},{10,9... | collective-permute-start | bytes 49160 | tf_op jit(solution)/shard_map/ppermute | solution.py:185
  10.1 7.1 %collective-permute-start.4 = (bf16[64,512]{1,0:T(8,128)(2,1)S(1)}, bf16[64,512]{1,0:T(8,128)(2,1)S(1)}, u32[]{:S(2)}, u32[]{:S(2)}) collective-permute-start(bf16[64,512]{1,0:T(8,128)(2,1)S(1)} %bitcast.12), channel_id=1, source_target_pairs={{0,2},{1,3},{2,0},{3,1},{4,6},{5,7},{6,4},{7,5},{8,10},{9,11},{10,... | collective-permute-start | bytes 196616 | tf_op jit(solution)/shard_map/ppermute | solution.py:185
  10.5 6.7 %collective-permute-start.5 = (bf16[64,512]{1,0:T(8,128)(2,1)S(1)}, bf16[64,512]{1,0:T(8,128)(2,1)S(1)}, u32[]{:S(2)}, u32[]{:S(2)}) collective-permute-start(bf16[64,512]{1,0:T(8,128)(2,1)S(1)} %bitcast.13), channel_id=1, source_target_pairs={{0,3},{1,0},{2,1},{3,2},{4,7},{5,4},{6,5},{7,6},{8,11},{9,8},{10,9... | collective-permute-start | bytes 196616 | tf_op jit(solution)/shard_map/ppermute | solution.py:185
  12.6 7.3 %collective-permute-start.6 = (bf16[64,512]{1,0:T(8,128)(2,1)S(1)}, bf16[64,512]{1,0:T(8,128)(2,1)S(1)}, u32[]{:S(2)}, u32[]{:S(2)}) collective-permute-start(bf16[64,512]{1,0:T(8,128)(2,1)S(1)} %get-tuple-element.44), channel_id=1, source_target_pairs={{0,1},{1,2},{2,3},{3,0},{4,5},{5,6},{6,7},{7,4},{8,9},{9,10},{10,1... | collective-permute-start | bytes 196616 | tf_op jit(solution)/shard_map/ppermute | solution.py:185
  13.8 7.1 %collective-permute-start.7 = (bf16[64,512]{1,0:T(8,128)(2,1)S(1)}, bf16[64,512]{1,0:T(8,128)(2,1)S(1)}, u32[]{:S(2)}, u32[]{:S(2)}) collective-permute-start(bf16[64,512]{1,0:T(8,128)(2,1)S(1)} %get-tuple-element.45), channel_id=1, source_target_pairs={{0,2},{1,3},{2,0},{3,1},{4,6},{5,7},{6,4},{7,5},{8,10},{9,11},{10,... | collective-permute-start | bytes 196616 | tf_op jit(solution)/shard_map/ppermute | solution.py:185
  17.2 1.2 %copy-start.1 = (bf16[64,27,256]{2,0,1:T(8,128)(2,1)S(1)}, bf16[64,27,256]{2,0,1:T(8,128)(2,1)}, u32[]{:S(2)}) copy-start(bf16[64,27,256]{2,0,1:T(8,128)(2,1)} %param.6) | copy-start | bytes 2654212
  17.2 4.4 %collective-permute-start.8 = (bf16[64,512]{1,0:T(8,128)(2,1)S(1)}, bf16[64,512]{1,0:T(8,128)(2,1)S(1)}, u32[]{:S(2)}, u32[]{:S(2)}) collective-permute-start(bf16[64,512]{1,0:T(8,128)(2,1)S(1)} %get-tuple-element.46), channel_id=1, source_target_pairs={{0,3},{1,0},{2,1},{3,2},{4,7},{5,4},{6,5},{7,6},{8,11},{9,8},{10,9... | collective-permute-start | bytes 196616 | tf_op jit(solution)/shard_map/ppermute | solution.py:185
  21.7 1.3 %collective-permute-start.9 = (bf16[32,512]{1,0:T(8,128)(2,1)S(1)}, bf16[32,512]{1,0:T(8,128)(2,1)S(1)}, u32[]{:S(2)}, u32[]{:S(2)}) collective-permute-start(bf16[32,512]{1,0:T(8,128)(2,1)S(1)} %get-tuple-element.49), channel_id=1, source_target_pairs={{0,4},{4,0},{8,12},{12,8},{16,20},{20,16},{24,28},{28,24},{1,5},{5... | collective-permute-start | bytes 98312 | tf_op jit(solution)/shard_map/ppermute | solution.py:351
  23.0 15.0 %all-to-all-start = ((bf16[4,192,512]{2,1,0:T(8,128)(2,1)}), bf16[4,192,512]{2,1,0:T(8,128)(2,1)S(1)}, u32[]{:S(2)}, u32[]{:S(2)}) async-start(bf16[4,192,512]{2,1,0:T(8,128)(2,1)} %pieces.1), calls=%async_computation | async-start | bytes 1572864 | tf_op jit(solution)/shard_map/all_to_all | solution.py:394
  26.7 6.9 %collective-permute-start.14 = (bf16[64,512]{1,0:T(8,128)(2,1)S(1)}, bf16[64,512]{1,0:T(8,128)(2,1)S(1)}, u32[]{:S(2)}, u32[]{:S(2)}) collective-permute-start(bf16[64,512]{1,0:T(8,128)(2,1)S(1)} %stack.1.refs_0_), channel_id=1, source_target_pairs={{0,1},{1,2},{2,3},{3,0},{4,5},{5,6},{6,7},{7,4},{8,9},{9,10},{10,1... | collective-permute-start | bytes 196616 | tf_op jit(solution)/shard_map/ppermute | solution.py:185
  27.3 9.2 %collective-permute-start.15 = (bf16[64,512]{1,0:T(8,128)(2,1)S(1)}, bf16[64,512]{1,0:T(8,128)(2,1)S(1)}, u32[]{:S(2)}, u32[]{:S(2)}) collective-permute-start(bf16[64,512]{1,0:T(8,128)(2,1)S(1)} %stack.1.refs_0_), channel_id=1, source_target_pairs={{0,2},{1,3},{2,0},{3,1},{4,6},{5,7},{6,4},{7,5},{8,10},{9,11},{10,... | collective-permute-start | bytes 196616 | tf_op jit(solution)/shard_map/ppermute | solution.py:185
  29.7 8.3 %collective-permute-start.16 = (bf16[64,512]{1,0:T(8,128)(2,1)S(1)}, bf16[64,512]{1,0:T(8,128)(2,1)S(1)}, u32[]{:S(2)}, u32[]{:S(2)}) collective-permute-start(bf16[64,512]{1,0:T(8,128)(2,1)S(1)} %stack.1.refs_0_), channel_id=1, source_target_pairs={{0,3},{1,0},{2,1},{3,2},{4,7},{5,4},{6,5},{7,6},{8,11},{9,8},{10,9... | collective-permute-start | bytes 196616 | tf_op jit(solution)/shard_map/ppermute | solution.py:185
  31.5 8.0 %collective-permute-start.11 = (bf16[64,512]{1,0:T(8,128)(2,1)S(1)}, bf16[64,512]{1,0:T(8,128)(2,1)S(1)}, u32[]{:S(2)}, u32[]{:S(2)}) collective-permute-start(bf16[64,512]{1,0:T(8,128)(2,1)S(1)} %get-tuple-element.52), channel_id=1, source_target_pairs={{0,1},{1,2},{2,3},{3,0},{4,5},{5,6},{6,7},{7,4},{8,9},{9,10},{10,1... | collective-permute-start | bytes 196616 | tf_op jit(solution)/shard_map/ppermute | solution.py:185
  32.7 10.8 %collective-permute-start.12 = (bf16[64,512]{1,0:T(8,128)(2,1)S(1)}, bf16[64,512]{1,0:T(8,128)(2,1)S(1)}, u32[]{:S(2)}, u32[]{:S(2)}) collective-permute-start(bf16[64,512]{1,0:T(8,128)(2,1)S(1)} %get-tuple-element.53), channel_id=1, source_target_pairs={{0,2},{1,3},{2,0},{3,1},{4,6},{5,7},{6,4},{7,5},{8,10},{9,11},{10,... | collective-permute-start | bytes 196616 | tf_op jit(solution)/shard_map/ppermute | solution.py:185
  33.7 9.8 %collective-permute-start.13 = (bf16[64,512]{1,0:T(8,128)(2,1)S(1)}, bf16[64,512]{1,0:T(8,128)(2,1)S(1)}, u32[]{:S(2)}, u32[]{:S(2)}) collective-permute-start(bf16[64,512]{1,0:T(8,128)(2,1)S(1)} %get-tuple-element.54), channel_id=1, source_target_pairs={{0,3},{1,0},{2,1},{3,2},{4,7},{5,4},{6,5},{7,6},{8,11},{9,8},{10,9... | collective-permute-start | bytes 196616 | tf_op jit(solution)/shard_map/ppermute | solution.py:185
  38.0 2.3 %collective-permute-start.10 = (bf16[4,192,512]{2,1,0:T(8,128)(2,1)S(1)}, bf16[4,192,512]{2,1,0:T(8,128)(2,1)S(1)}, u32[]{:S(2)}, u32[]{:S(2)}) collective-permute-start(bf16[4,192,512]{2,1,0:T(8,128)(2,1)S(1)} %all-to-all-done.mine), channel_id=1, source_target_pairs={{0,4},{4,0},{8,12},{12,8},{16,20},{20,16},{24,28},{28,24},{1,5},{5... | collective-permute-start | bytes 2359304 | tf_op jit(solution)/shard_map/ppermute | solution.py:351
  38.1 6.0 %collective-permute-start.18 = (bf16[64,512]{1,0:T(8,128)(2,1)S(1)}, bf16[64,512]{1,0:T(8,128)(2,1)S(1)}, u32[]{:S(2)}, u32[]{:S(2)}) collective-permute-start(bf16[64,512]{1,0:T(8,128)(2,1)S(1)} %get-tuple-element.62), channel_id=1, source_target_pairs={{0,8},{4,12},{8,0},{12,4},{16,24},{20,28},{24,16},{28,20},{1,9},{5... | collective-permute-start | bytes 196616 | tf_op jit(solution)/shard_map/ppermute | solution.py:351
  39.6 4.5 %collective-permute-start.19 = (bf16[64,512]{1,0:T(8,128)(2,1)S(1)}, bf16[64,512]{1,0:T(8,128)(2,1)S(1)}, u32[]{:S(2)}, u32[]{:S(2)}) collective-permute-start(bf16[64,512]{1,0:T(8,128)(2,1)S(1)} %get-tuple-element.63), channel_id=1, source_target_pairs={{0,16},{4,20},{8,24},{12,28},{16,0},{20,4},{24,8},{28,12},{1,17},{... | collective-permute-start | bytes 196616 | tf_op jit(solution)/shard_map/ppermute | solution.py:351
  40.3 5.2 %collective-permute-start.17 = (bf16[64,512]{1,0:T(8,128)(2,1)S(1)}, bf16[64,512]{1,0:T(8,128)(2,1)S(1)}, u32[]{:S(2)}, u32[]{:S(2)}) collective-permute-start(bf16[64,512]{1,0:T(8,128)(2,1)S(1)} %get-tuple-element.60), channel_id=1, source_target_pairs={{0,24},{4,28},{8,16},{12,20},{16,8},{20,12},{24,0},{28,4},{1,25},{... | collective-permute-start | bytes 196616 | tf_op jit(solution)/shard_map/ppermute | solution.py:351
